TPU v7x, 32 devices: a whole 2x2x4 slice. The times are simulated.
32 devices in a mesh: sec: 4 (over y, x), ctx: 8 (over z, core).
Axes of the slice: x: 2, y: 2, z: 4, core: 2. Of those that a mesh axis runs over, the one named last changes fastest.
Arguments:
- hidden_state: bfloat16 [4, 1024, 4096], P('sec', 'ctx'), may hold values from -8 to 8
- queries: bfloat16 [4, 1024, 4096], P('sec', 'ctx'), may hold values from -6 to 6
- key_vectors: bfloat16 [4, 1024, 4096], P('sec', 'ctx'), may hold values from -4.5 to 4.5
- value_vectors: bfloat16 [4, 1024, 4096], P('sec', 'ctx'), may hold values from -6 to 6
- modulation: float32 [32, 3, 4096], replicated, may hold values from -3 to 3
- down_weight: bfloat16 [4096, 256], replicated, may hold values from -0.09375 to 0.09375
- conv_weight: bfloat16 [3, 3, 3, 256, 256], replicated, may hold values from -0.078125 to 0.078125
- clip_frames: int32 [4], replicated, may hold values from 4 to 16, as said below
- destination: int32 [4], replicated, may hold values from 0 to 3, as said below
- timestep: int32 [4], replicated, may hold values from 0 to 31
Outputs:
- upsampled: bfloat16 [4, 1024, 256], P('sec', 'ctx')
Inputs may be any that keep to these rules, and one draw needn't show every extreme that they name: `clip_frames`: one section's clip fills all 16 frames. `destination`: every upsampler group receives exactly one clip; some group d receives the clip of section (d + 2) mod 4.
All inputs are finite; a program needn't handle non-finite values.
Results may differ from a plain program's by a relative error of at most 0.0063.
Values may be sent and summed in bfloat16 or wider, within the bound.
No kernel may reach another device: no remote copies, remote signals or barrier semaphores. Data moves between devices by JAX's collectives and lax.ppermute only.
A program may use at most 64 MiB of HBM per device.

v0:
```python
import functools
import itertools
import math

import jax
import jax.numpy as jnp
from jax import lax
from jax.experimental import pallas as pl
from jax.experimental.pallas import tpu as pltpu
from jax.sharding import PartitionSpec as P


HEADS = 32
VMEM_BYTES = 67043328
HH = 8
WW = 8


def head_chunks(group):
    late = max(1, group // 4)
    return group - late, late


def partner(me, step, count):
    if count & (count - 1) == 0:
        return me ^ step, me ^ step
    return lax.rem(me + step, count), lax.rem(me - step + count, count)


def ring(step, count):
    if count & (count - 1) == 0:
        return [(i, i ^ step) for i in range(count)]
    return [(i, (i + step) % count) for i in range(count)]


def send(value, step, chips):
    pairs = [
        (2 * one + core, 2 * two + core) for one, two in ring(step, chips) for core in range(2)
    ]
    return lax.ppermute(value, "ctx", pairs)


def across(value, chips):
    return lax.ppermute(value, "ctx", [(i, i ^ 1) for i in range(2 * chips)])


def my_chip(step, chips):
    return partner(lax.axis_index("ctx") // 2, step, chips)


def pack_kernel(chips, kinds, head_cols, first_col, width, *rest):
    sources, outs, (buf, in_sem, out_sem) = rest[:kinds], rest[kinds : kinds + chips], rest[kinds + chips :]
    order = list(range(chips - 1, -1, -1))

    def load(step, kind):
        col = pl.multiple_of(my_chip(step, chips)[0] * head_cols + first_col, 128)
        return pltpu.make_async_copy(
            sources[kind].at[0, :, pl.ds(col, width)], buf.at[step, kind], in_sem.at[step, kind]
        )

    def save(step):
        return pltpu.make_async_copy(buf.at[step], outs[step], out_sem.at[step])

    for step in order:
        for kind in range(kinds):
            load(step, kind).start()
    for step in order:
        for kind in range(kinds):
            load(step, kind).wait()
        save(step).start()
    for step in order:
        save(step).wait()


def pack(sources, chips, head_cols, first_col, width):
    rows = sources[0].shape[1]
    kinds = len(sources)
    piece = jax.ShapeDtypeStruct((kinds, rows, width), sources[0].dtype)
    return pl.pallas_call(
        functools.partial(pack_kernel, chips, kinds, head_cols, first_col, width),
        out_shape=[piece] * chips,
        in_specs=[pl.BlockSpec(memory_space=pltpu.HBM)] * kinds,
        out_specs=[pl.BlockSpec(memory_space=pltpu.HBM)] * chips,
        scratch_shapes=[
            pltpu.VMEM((chips, kinds, rows, width), sources[0].dtype),
            pltpu.SemaphoreType.DMA((chips, kinds)),
            pltpu.SemaphoreType.DMA((chips,)),
        ],
        cost_estimate=pl.CostEstimate(
            flops=0, bytes_accessed=4 * kinds * chips * rows * width, transcendentals=0
        ),
        compiler_params=pltpu.CompilerParams(vmem_limit_bytes=VMEM_BYTES),
        name="pack",
    )(*sources)


def attend_kernel(chips, heads, block_rows, frames_ref, *rest):
    own, beside, outs = rest[:chips], rest[chips : 2 * chips], rest[2 * chips : 3 * chips]
    queries, keys, values, result, in_sem, value_sem, out_sem = rest[3 * chips :]
    core = lax.rem(lax.axis_index("ctx"), 2)
    rows = own[0].shape[1]
    asked = chips * rows
    seq = 2 * asked
    size = own[0].shape[2] // heads
    scale = math.log2(math.e) / math.sqrt(size)
    blocks = asked // block_rows

    def place(step, side):
        device = my_chip(step, chips)[1] * 2 + (core if side == 0 else 1 - core)
        return pl.ds(pl.multiple_of(device * rows, rows), rows)

    def load(step, which):
        if which == 2:
            source, target = own[step].at[0], queries.at[pl.ds(step * rows, rows), :]
        else:
            source, target = (own, beside)[which][step].at[1], keys.at[place(step, which), :]
        return pltpu.make_async_copy(source, target, in_sem.at[which, step])

    def load_values(step, side, head):
        return pltpu.make_async_copy(
            (own, beside)[side][step].at[2, :, pl.ds(head * size, size)],
            values.at[place(step, side), pl.ds(head * 2 * size, size)],
            value_sem.at[side, head, step],
        )

    def save(step):
        return pltpu.make_async_copy(
            result.at[pl.ds(step * rows, rows), :], outs[step], out_sem.at[step]
        )

    for step in range(chips):
        for which in range(3):
            load(step, which).start()
    for head in range(heads):
        for step in range(chips):
            for side in range(2):
                load_values(step, side, head).start()
    for head in range(heads):
        values[:, pl.ds((head * 2 + 1) * size, size)] = jnp.ones((seq, size), jnp.bfloat16)
    valid = frames_ref[0] * (HH * WW)
    places = lax.broadcasted_iota(jnp.int32, (1, seq), 1)
    bias = jnp.where(places < valid, 0.0, -jnp.inf)
    for step in range(chips):
        for which in range(3):
            load(step, which).wait()
    for head in range(heads):
        for step in range(chips):
            for side in range(2):
                load_values(step, side, head).wait()

    def task(index, carry):
        head = index // blocks
        start = pl.multiple_of(lax.rem(index, blocks) * block_rows, block_rows)
        here = pl.ds(start, block_rows)
        lanes = pl.ds(pl.multiple_of(head * size, size), size)
        scores = lax.dot_general(
            queries[here, lanes],
            keys[:, lanes],
            (((1,), (1,)), ((), ())),
            preferred_element_type=jnp.float32,
        )
        scores = scores * scale + bias
        weights = jnp.exp2(scores - jnp.max(scores, axis=1, keepdims=True))
        both = jnp.dot(
            weights.astype(jnp.bfloat16),
            values[:, pl.ds(pl.multiple_of(head * (2 * size), 2 * size), 2 * size)],
            preferred_element_type=jnp.float32,
        )
        result[here, lanes] = (both[:, :size] / both[:, size:]).astype(result.dtype)
        return carry

    lax.fori_loop(0, heads * blocks, task, 0, unroll=4)
    for step in range(chips):
        save(step).start()
    for step in range(chips):
        save(step).wait()


def attend(frames, own, beside, heads):
    chips = len(own)
    _, rows, width = own[0].shape
    asked = chips * rows
    seq = 2 * asked
    block_rows = min(256, asked)
    return pl.pallas_call(
        functools.partial(attend_kernel, chips, heads, block_rows),
        out_shape=[jax.ShapeDtypeStruct((rows, width), jnp.bfloat16)] * chips,
        in_specs=[pl.BlockSpec(memory_space=pltpu.SMEM)]
        + [pl.BlockSpec(memory_space=pltpu.HBM)] * (2 * chips),
        out_specs=[pl.BlockSpec(memory_space=pltpu.HBM)] * chips,
        scratch_shapes=[
            pltpu.VMEM((asked, width), jnp.bfloat16),
            pltpu.VMEM((seq, width), jnp.bfloat16),
            pltpu.VMEM((seq, 2 * width), jnp.bfloat16),
            pltpu.VMEM((asked, width), jnp.bfloat16),
            pltpu.SemaphoreType.DMA((3, chips)),
            pltpu.SemaphoreType.DMA((2, heads, chips)),
            pltpu.SemaphoreType.DMA((chips,)),
        ],
        cost_estimate=pl.CostEstimate(
            flops=6 * asked * seq * width,
            bytes_accessed=8 * seq * width,
            transcendentals=asked * seq * heads,
        ),
        compiler_params=pltpu.CompilerParams(vmem_limit_bytes=VMEM_BYTES),
        name="attend",
    )(frames, *own, *beside)


def prepare_kernel(chips, head_cols, width, h_ref, mod_ref, weight_ref, *rest):
    h_out, mod_out, weight_out, const_ref, _, mod, weight, late_h, late_mod, late_weight, in_sem, out_sem = rest
    late = head_cols - width

    def pull(step, which):
        col = pl.multiple_of(my_chip(step, chips)[1] * head_cols + width, 128)
        here = pl.ds(step * late, late)
        source, target = (
            (h_ref.at[0, :, pl.ds(col, late)], late_h.at[:, here]),
            (mod_ref.at[:, pl.ds(col, late)], late_mod.at[:, here]),
            (weight_ref.at[pl.ds(col, late), :], late_weight.at[here, :]),
        )[which]
        return pltpu.make_async_copy(source, target, in_sem.at[which, step])

    def whole(which):
        source, target = ((mod_ref, mod), (weight_ref, weight))[which]
        return pltpu.make_async_copy(source, target, in_sem.at[3, which])

    def push(which):
        source, target = ((late_h, h_out), (late_mod, mod_out), (late_weight, weight_out))[which]
        return pltpu.make_async_copy(source, target, out_sem.at[which])

    for which in range(3):
        for step in range(chips):
            pull(step, which).start()
    whole(0).start()
    whole(1).start()
    for which in range(3):
        for step in range(chips):
            pull(step, which).wait()
        push(which).start()

    def product(row):
        high = row.astype(jnp.bfloat16)
        low = (row - high.astype(jnp.float32)).astype(jnp.bfloat16)
        split = jnp.concatenate(
            [jnp.broadcast_to(high, (8,) + high.shape[1:]), jnp.broadcast_to(low, (8,) + low.shape[1:])],
            axis=0,
        )
        both = jnp.dot(split, weight[...], preferred_element_type=jnp.float32)
        return both[:8] + both[8:]

    whole(0).wait()
    whole(1).wait()
    const_ref[0] = product(1.0 + mod[1:2, :])
    const_ref[1] = product(mod[0:1, :])
    for which in range(3):
        push(which).wait()


def prepare(hidden_state, mod_rows, down_weight, chips, width):
    _, rows, model = hidden_state.shape
    channels = down_weight.shape[1]
    head_cols = model // chips
    late = chips * (head_cols - width)
    hbm = pl.BlockSpec(memory_space=pltpu.HBM)
    shapes = [
        ((rows, late), jnp.bfloat16),
        ((3, late), jnp.float32),
        ((late, channels), jnp.bfloat16),
    ]
    return pl.pallas_call(
        functools.partial(prepare_kernel, chips, head_cols, width),
        out_shape=[jax.ShapeDtypeStruct(*shape) for shape in shapes]
        + [jax.ShapeDtypeStruct((2, 8, channels), jnp.float32)],
        in_specs=[hbm] * 3,
        out_specs=[hbm] * 3 + [pl.BlockSpec(memory_space=pltpu.VMEM)],
        scratch_shapes=[
            pltpu.VMEM((8, 128), jnp.float32),
            pltpu.VMEM((3, model), jnp.float32),
            pltpu.VMEM((model, channels), jnp.bfloat16),
        ]
        + [pltpu.VMEM(*shape) for shape in shapes]
        + [pltpu.SemaphoreType.DMA((4, max(chips, 2))), pltpu.SemaphoreType.DMA((3,))],
        cost_estimate=pl.CostEstimate(
            flops=64 * model * channels, bytes_accessed=4 * model * channels, transcendentals=0
        ),
        compiler_params=pltpu.CompilerParams(vmem_limit_bytes=VMEM_BYTES),
        name="prepare",
    )(hidden_state, mod_rows, down_weight)


def early_kernel(chips, head_cols, h_ref, mod_ref, weight_ref, *rest):
    pieces, rest = rest[:chips], rest[chips:]
    acc_ref, centre_ref, square_ref = rest[:3]
    attended, hidden, weight, mod, sem = rest[3:]
    rows, width = pieces[0].shape
    block_rows = 16

    def pull(step, which):
        col = pl.multiple_of(my_chip(step, chips)[1] * head_cols, 128)
        here = pl.ds(step * width, width)
        source, target = (
            (pieces[step], attended.at[:, here]),
            (h_ref.at[0, :, pl.ds(col, width)], hidden.at[:, here]),
            (mod_ref.at[:, pl.ds(col, width)], mod.at[:, here]),
            (weight_ref.at[pl.ds(col, width), :], weight.at[here, :]),
        )[which]
        return pltpu.make_async_copy(source, target, sem.at[which, step])

    for which in range(4):
        for step in range(chips):
            pull(step, which).start()
    for which in range(3):
        for step in range(chips):
            pull(step, which).wait()

    def rows_of(index, carry):
        here = pl.ds(pl.multiple_of(index * block_rows, block_rows), block_rows)
        wide = (
            (
                hidden[here, :].astype(jnp.float32)
                + mod[2:3, :] * attended[here, :].astype(jnp.float32)
            )
            .astype(jnp.bfloat16)
            .astype(jnp.float32)
        )
        centre = jnp.mean(wide, axis=-1, keepdims=True)
        away = wide - centre
        square = jnp.sum(jnp.square(away), axis=-1, keepdims=True)
        attended[here, :] = (away * (1.0 + mod[1:2, :])).astype(jnp.bfloat16)
        centre_ref[here, :] = jnp.broadcast_to(centre, (block_rows, 128))
        square_ref[here, :] = jnp.broadcast_to(square, (block_rows, 128))
        return carry

    lax.fori_loop(0, rows // block_rows, rows_of, 0, unroll=2)
    for step in range(chips):
        pull(step, 3).wait()
    acc_ref[...] = jnp.dot(attended[...], weight[...], preferred_element_type=jnp.float32)


def project_early(hidden_state, mod_rows, down_weight, pieces):
    chips = len(pieces)
    _, rows, model = hidden_state.shape
    channels = down_weight.shape[1]
    width = pieces[0].shape[1]
    return pl.pallas_call(
        functools.partial(early_kernel, chips, model // chips),
        out_shape=[
            jax.ShapeDtypeStruct((rows, channels), jnp.float32),
            jax.ShapeDtypeStruct((rows, 128), jnp.float32),
            jax.ShapeDtypeStruct((rows, 128), jnp.float32),
        ],
        in_specs=[pl.BlockSpec(memory_space=pltpu.HBM)] * (chips + 3),
        out_specs=[pl.BlockSpec(memory_space=pltpu.VMEM)] * 3,
        scratch_shapes=[
            pltpu.VMEM((rows, chips * width), jnp.bfloat16),
            pltpu.VMEM((rows, chips * width), jnp.bfloat16),
            pltpu.VMEM((chips * width, channels), jnp.bfloat16),
            pltpu.VMEM((3, chips * width), jnp.float32),
            pltpu.SemaphoreType.DMA((4, chips)),
        ],
        cost_estimate=pl.CostEstimate(
            flops=2 * rows * chips * width * channels,
            bytes_accessed=4 * rows * model + 2 * model * channels,
            transcendentals=0,
        ),
        compiler_params=pltpu.CompilerParams(vmem_limit_bytes=VMEM_BYTES),
        name="project_early",
    )(hidden_state, mod_rows, down_weight, *pieces)


def late_kernel(count, early, frames_ref, *rest):
    sources, pieces, rest = rest[:7], rest[7 : 7 + count], rest[7 + count :]
    out_ref, attended, held, in_sem, held_sem = rest[0], rest[1], rest[2:9], rest[9], rest[10]
    acc_ref, centre_ref, square_ref, h_ref, mod_ref, weight_ref, const_ref = held
    rows, width = pieces[0].shape
    late = count * width
    model = early + late

    def load(step):
        return pltpu.make_async_copy(
            pieces[step], attended.at[:, pl.ds(step * width, width)], in_sem.at[step]
        )

    def hold(which):
        return pltpu.make_async_copy(sources[which], held[which], held_sem.at[which])

    for step in range(count):
        load(step).start()
    for which in (3, 4, 1, 2, 5, 0, 6):
        hold(which).start()
    for which in (3, 4, 1, 2):
        hold(which).wait()
    for step in range(count):
        load(step).wait()
    wide = (
        (h_ref[...].astype(jnp.float32) + mod_ref[2:3, :] * attended[...].astype(jnp.float32))
        .astype(jnp.bfloat16)
        .astype(jnp.float32)
    )
    first = centre_ref[:, :1]
    scaled = ((wide - first) * (1.0 + mod_ref[1:2, :])).astype(jnp.bfloat16)
    for which in (5, 0, 6):
        hold(which).wait()
    total = acc_ref[...] + jnp.dot(scaled, weight_ref[...], preferred_element_type=jnp.float32)
    own = jnp.mean(wide, axis=-1, keepdims=True)
    square = jnp.sum(jnp.square(wide - own), axis=-1, keepdims=True)
    gap = own - first
    centre = first + gap * (late / model)
    spread = (square_ref[:, :1] + square + gap * gap * (early * late / model)) / model
    total = total + (first - centre) * const_ref[0, :1, :]
    total = total * lax.rsqrt(spread + 1e-06) + const_ref[1, :1, :]
    token = lax.axis_index("ctx") * rows + lax.broadcasted_iota(jnp.int32, (rows, 1), 0)
    out_ref[...] = jnp.where(token < frames_ref[0] * (HH * WW), total, 0.0).astype(out_ref.dtype)


def project_late(frames, early, consts, pieces, count, model):
    rows, width = pieces[0].shape
    channels = consts.shape[-1]
    hbm = pl.BlockSpec(memory_space=pltpu.HBM)
    sources = (*early, consts)
    return pl.pallas_call(
        functools.partial(late_kernel, count, model - count * width),
        out_shape=jax.ShapeDtypeStruct((rows, channels), jnp.bfloat16),
        in_specs=[pl.BlockSpec(memory_space=pltpu.SMEM)] + [hbm] * (7 + count),
        out_specs=pl.BlockSpec(memory_space=pltpu.VMEM),
        scratch_shapes=[pltpu.VMEM((rows, count * width), jnp.bfloat16)]
        + [pltpu.VMEM(source.shape, source.dtype) for source in sources]
        + [pltpu.SemaphoreType.DMA((count,)), pltpu.SemaphoreType.DMA((7,))],
        cost_estimate=pl.CostEstimate(
            flops=2 * rows * count * width * channels,
            bytes_accessed=4 * rows * count * width,
            transcendentals=0,
        ),
        compiler_params=pltpu.CompilerParams(vmem_limit_bytes=VMEM_BYTES),
        name="project_late",
    )(frames, *sources, *pieces)


def gather_taps(frames, taps):
    cells = HH * WW
    channels = frames[0].shape[1]
    column = lax.broadcasted_iota(jnp.int32, (cells, 1), 0) % WW
    blank = jnp.zeros((WW, channels), jnp.float32)
    for number, frame in enumerate(frames):
        wide = frame.astype(jnp.float32)
        for across, offset in enumerate((-1, 0, 1)):
            cell = wide
            if offset:
                inside = (column + offset >= 0) & (column + offset < WW)
                cell = jnp.where(inside, pltpu.roll(wide, (-offset) % cells, 0), 0.0)
            cell = jnp.concatenate([blank, cell, blank], axis=0)
            for down in range(3):
                taps[
                    pl.ds(number * cells, cells), pl.ds((down * 3 + across) * channels, channels)
                ] = cell[down * WW : down * WW + cells].astype(jnp.bfloat16)


def refine_kernel(frames_ref, mid_ref, even_ref, odd_ref, weight_ref, out_ref, held, taps, weight, sem, weight_sem):
    cells = HH * WW
    rows, _ = mid_ref.shape
    me = lax.axis_index("ctx")
    odd = lax.rem(me, 2)
    before, after = rows - cells, rows + cells

    def at(start):
        return pl.ds(pl.multiple_of(start, cells), cells)

    copies = (
        pltpu.make_async_copy(mid_ref, held.at[pl.ds(cells, rows), :], sem.at[0]),
        pltpu.make_async_copy(
            even_ref.at[at(odd * before), :], held.at[at((1 - odd) * after), :], sem.at[1]
        ),
        pltpu.make_async_copy(
            odd_ref.at[at((1 - odd) * before), :], held.at[at(odd * after), :], sem.at[2]
        ),
    )

    def fetch(ahead):
        return pltpu.make_async_copy(weight_ref.at[ahead], weight.at[ahead], weight_sem.at[ahead])

    for copy in copies:
        copy.start()
    for ahead in range(3):
        fetch(ahead).start()
    for copy in copies:
        copy.wait()
    gather_taps(
        [held[pl.ds(start, cells), :] for start in range(0, rows + 2 * cells, cells)], taps
    )
    total = held[pl.ds(cells, rows), :].astype(jnp.float32)
    for ahead in range(3):
        fetch(ahead).wait()
        total = total + jnp.dot(
            taps[pl.ds(ahead * cells, rows), :], weight[ahead], preferred_element_type=jnp.float32
        )
    token = me * rows + lax.broadcasted_iota(jnp.int32, (rows, 1), 0)
    out_ref[0] = jnp.where(token < frames_ref[0] * cells, total, 0.0).astype(out_ref.dtype)


def refine(frames, mid, even, odd, conv_weight):
    rows, channels = mid.shape
    taps = conv_weight.reshape(3, 9 * channels, channels)
    return pl.pallas_call(
        refine_kernel,
        out_shape=jax.ShapeDtypeStruct((1, rows, channels), jnp.bfloat16),
        in_specs=[pl.BlockSpec(memory_space=pltpu.SMEM)]
        + [pl.BlockSpec(memory_space=pltpu.HBM)] * 4,
        out_specs=pl.BlockSpec(memory_space=pltpu.VMEM),
        scratch_shapes=[
            pltpu.VMEM((rows + 2 * HH * WW, channels), jnp.bfloat16),
            pltpu.VMEM((rows + 2 * HH * WW, 9 * channels), jnp.bfloat16),
            pltpu.VMEM(taps.shape, taps.dtype),
            pltpu.SemaphoreType.DMA((3,)),
            pltpu.SemaphoreType.DMA((3,)),
        ],
        cost_estimate=pl.CostEstimate(
            flops=54 * rows * channels * channels,
            bytes_accessed=2 * taps.size + 6 * rows * channels,
            transcendentals=0,
        ),
        compiler_params=pltpu.CompilerParams(vmem_limit_bytes=VMEM_BYTES),
        name="refine",
    )(frames, mid, even, odd, taps)


def clip_orders(sec_count):
    return [
        order
        for order in itertools.permutations(range(sec_count))
        if any(order[(d + sec_count // 2) % sec_count] == d for d in range(sec_count))
    ]


def order_index(destination, sec_count):
    if sec_count > 4:
        return jnp.int32(0)
    orders = clip_orders(sec_count)
    codes = jnp.asarray(
        [sum(d * sec_count**i for i, d in enumerate(order)) for order in orders], jnp.int32
    )
    powers = jnp.asarray([sec_count**i for i in range(sec_count)], jnp.int32)
    code = jnp.sum(destination * powers)
    return jnp.sum(jnp.where(codes == code, jnp.arange(len(orders), dtype=jnp.int32), 0))


def handoff(projected, which, source, sec_count):
    if sec_count <= 4:
        def take(order):
            return lambda value: lax.ppermute(value, "sec", list(enumerate(order)))

        return lax.switch(which, [take(order) for order in clip_orders(sec_count)], projected)
    my_section = lax.axis_index("sec")
    chosen = projected
    for step in range(1, sec_count):
        arrived = lax.ppermute(projected, "sec", ring(step, sec_count))
        chosen = jnp.where(source == partner(my_section, step, sec_count)[1], arrived, chosen)
    return chosen


def body(
    hidden_state,
    queries,
    key_vectors,
    value_vectors,
    modulation,
    down_weight,
    conv_weight,
    clip_frames,
    destination,
    timestep,
):
    my_section = lax.axis_index("sec")
    sec_count = lax.axis_size("sec")
    count = lax.axis_size("ctx")
    chips = count // 2
    model_width = hidden_state.shape[2]
    group = HEADS // chips
    head_size = model_width // HEADS
    head_cols = group * head_size
    chunks = head_chunks(group)
    widths = [heads * head_size for heads in chunks]
    tensors = (queries, key_vectors, value_vectors)
    steps = range(1, chips)

    own, beside = [], []
    for chunk, width in enumerate(widths):
        packed = pack(tensors, chips, head_cols, sum(widths[:chunk]), width)
        beside.append([across(packed[0], chips)])
        own.append([packed[0]] + [send(packed[step], step, chips) for step in steps])
        beside[chunk] += [across(own[chunk][step], chips) for step in steps]

    section_ids = jnp.arange(destination.shape[0], dtype=jnp.int32)
    source = jnp.sum(jnp.where(destination == my_section, section_ids, 0))
    own_frames = lax.dynamic_slice(clip_frames, (my_section,), (1,))
    clip_length = lax.dynamic_slice(clip_frames, (source,), (1,))
    which = order_index(destination, sec_count)
    mod_rows = lax.dynamic_index_in_dim(modulation, timestep[my_section], 0, keepdims=False)
    ready = prepare(hidden_state, mod_rows, down_weight, chips, widths[0])
    own_frames, clip_length, which, mod_rows, ready = lax.optimization_barrier(
        (own_frames, clip_length, which, mod_rows, ready)
    )

    returned = []
    for chunk, heads in enumerate(chunks):
        outs = attend(own_frames, own[chunk], beside[chunk], heads)
        returned.append([outs[0]] + [send(outs[step], step, chips) for step in steps])
    early = project_early(hidden_state, mod_rows, down_weight, returned[0])
    projected = project_late(
        own_frames, (*early, *tuple(ready[:3])), ready[3], returned[1], chips, model_width
    )
    mid = handoff(projected, which, source, sec_count)
    even = lax.ppermute(mid, "ctx", [(i, i ^ 1) for i in range(count)])
    joints = [(i, i + 1) for i in range(1, count - 1, 2)]
    odd = lax.ppermute(mid, "ctx", joints + [(two, one) for one, two in joints])
    return refine(clip_length, mid, even, odd, conv_weight)


def solution(mesh):
    split = P("sec", "ctx", None)
    return jax.shard_map(
        body,
        mesh=mesh,
        in_specs=(split,) * 4 + (P(),) * 6,
        out_specs=split,
        check_vma=False,
    )
```

profile of v0, /device:TPU:13, one launch (start us, length us, event | category | flops | bytes accessed | tf_op | source)
XLA Modules:
  0.0 139.2 jit_solution(4833709547495947186)
XLA Ops:
  0.0 2.7 %pack.2 = (bf16[3,128,768]{2,1,0:T(8,128)(2,1)}, bf16[3,128,768]{2,1,0:T(8,128)(2,1)}, bf16[3,128,768]{2,1,0:T(8,128)(2,1)}, bf16[3,128,768]{2,1,0:T(8,128)(2,1)}) custom-call(bf16[1,128,4096]{2,1,0:T(8,128)(2,1)} %rest_0_.3, bf16[1,128,4096]{2,1,0:T(8,128)(2,1)} %rest_1_.3, bf16[1,128,4096]{2,1,0:T(8,128)(2,1)} %rest_2_.3), custom_call_target="tpu_custom_call" | custom-call | bytes 4718592 | tf_op jit(solution)/shard_map/pack/pallas_call | solution.py:79
  2.9 2.3 %collective-permute-start.16 = (bf16[3,128,768]{2,1,0:T(8,128)(2,1)}, bf16[3,128,768]{2,1,0:T(8,128)(2,1)}, u32[]{:S(2)}, u32[]{:S(2)}) collective-permute-start(bf16[3,128,768]{2,1,0:T(8,128)(2,1)} %get-tuple-element.77), channel_id=1, source_target_pairs={{0,4},{1,5},{2,6},{3,7},{4,0},{5,1},{6,2},{7,3},{8,12},{9,13},{10,... | collective-permute-start | bytes 1769480 | tf_op jit(solution)/shard_map/ppermute | solution.py:40
  5.4 2.0 %pack.3 = (bf16[3,128,256]{2,1,0:T(8,128)(2,1)}, bf16[3,128,256]{2,1,0:T(8,128)(2,1)}, bf16[3,128,256]{2,1,0:T(8,128)(2,1)}, bf16[3,128,256]{2,1,0:T(8,128)(2,1)}) custom-call(bf16[1,128,4096]{2,1,0:T(8,128)(2,1)} %rest_0_.3, bf16[1,128,4096]{2,1,0:T(8,128)(2,1)} %rest_1_.3, bf16[1,128,4096]{2,1,0:T(8,128)(2,1)} %rest_2_.3), custom_call_target="tpu_custom_call" | custom-call | bytes 1572864 | tf_op jit(solution)/shard_map/pack/pallas_call | solution.py:79
  7.4 1.2 collective-permute-start.25
  8.6 1.7 %collective-permute-start.18 = (bf16[3,128,768]{2,1,0:T(8,128)(2,1)}, bf16[3,128,768]{2,1,0:T(8,128)(2,1)}, u32[]{:S(2)}, u32[]{:S(2)}) collective-permute-start(bf16[3,128,768]{2,1,0:T(8,128)(2,1)} %get-tuple-element.75.rest_0_), channel_id=1, source_target_pairs={{0,1},{1,0},{2,3},{3,2},{4,5},{5,4},{6,7},{7,6},{8,9},{9,8},{10,11... | collective-permute-start | bytes 1769480 | tf_op jit(solution)/shard_map/ppermute | solution.py:44
  10.4 1.2 dynamic_slice.15
  13.5 33.3 %collective-permute-done.25.rest_1_ = bf16[3,128,256]{2,1,0:T(8,128)(2,1)S(1)} collective-permute-done((bf16[3,128,256]{2,1,0:T(8,128)(2,1)}, bf16[3,128,256]{2,1,0:T(8,128)(2,1)S(1)}, u32[]{:S(2)}, u32[]{:S(2)}) %collective-permute-start.25) | collective-permute-done | bytes 196640 | tf_op jit(solution)/shard_map/ppermute | solution.py:40
  46.9 2.1 %collective-permute-start.26 = (bf16[3,128,256]{2,1,0:T(8,128)(2,1)}, bf16[3,128,256]{2,1,0:T(8,128)(2,1)}, u32[]{:S(2)}, u32[]{:S(2)}) collective-permute-start(bf16[3,128,256]{2,1,0:T(8,128)(2,1)} %get-tuple-element.92), channel_id=1, source_target_pairs={{0,4},{1,5},{2,6},{3,7},{4,0},{5,1},{6,2},{7,3},{8,12},{9,13},{10,... | collective-permute-start | bytes 589832 | tf_op jit(solution)/shard_map/ppermute | solution.py:40
  49.0 1.8 %collective-permute-start.19 = (bf16[3,128,768]{2,1,0:T(8,128)(2,1)}, bf16[3,128,768]{2,1,0:T(8,128)(2,1)}, u32[]{:S(2)}, u32[]{:S(2)}) collective-permute-start(bf16[3,128,768]{2,1,0:T(8,128)(2,1)} %collective-permute-done.15.rest_1_), channel_id=1, source_target_pairs={{0,1},{1,0},{2,3},{3,2},{4,5},{5,4},{6,7},{7,6},{8,9},{9,8},{10,11... | collective-permute-start | bytes 1769480 | tf_op jit(solution)/shard_map/ppermute | solution.py:44
  50.9 9.6 %collective-permute-done.17.rest_3_ = bf16[3,128,768]{2,1,0:T(8,128)(2,1)} collective-permute-done((bf16[3,128,768]{2,1,0:T(8,128)(2,1)}, bf16[3,128,768]{2,1,0:T(8,128)(2,1)}, u32[]{:S(2)}, u32[]{:S(2)}) %collective-permute-start.17) | collective-permute-done | bytes 589856 | tf_op jit(solution)/shard_map/ppermute | solution.py:40
  60.5 3.1 %collective-permute-start.21 = (bf16[3,128,768]{2,1,0:T(8,128)(2,1)}, bf16[3,128,768]{2,1,0:T(8,128)(2,1)}, u32[]{:S(2)}, u32[]{:S(2)}) collective-permute-start(bf16[3,128,768]{2,1,0:T(8,128)(2,1)} %collective-permute-done.17.rest_3_), channel_id=1, source_target_pairs={{0,1},{1,0},{2,3},{3,2},{4,5},{5,4},{6,7},{7,6},{8,9},{9,8},{10,11... | collective-permute-start | bytes 1769480 | tf_op jit(solution)/shard_map/ppermute | solution.py:44
  63.6 1.0 constant_dynamic-slice_fusion
  64.6 1.4 collective-permute-start.27
  66.0 1.4 multiply_reduce_fusion
  70.1 1.4 %fusion.2 = (s32[1]{0:T(128)}, s32[1]{0:T(128)}) fusion(s32[4]{0:T(128)} %param.34, s32[]{:T(128)S(6)} %select_n.21, s32[]{:T(128)S(6)} %select_n.19), kind=kLoop, calls=%fused_computation.7 | loop fusion | bytes 24 | tf_op jit(solution)/shard_map/dynamic_slice | solution.py:596
  71.5 3.6 %prepare.1 = (bf16[128,1024]{1,0:T(8,128)(2,1)}, f32[3,1024]{1,0:T(4,128)}, bf16[1024,256]{1,0:T(8,128)(2,1)}, f32[2,8,256]{2,1,0:T(8,128)}) custom-call(bf16[1,128,4096]{2,1,0:T(8,128)(2,1)} %h_ref.3, f32[3,4096]{1,0:T(4,128)} %bitcast.6, bf16[4096,256]{1,0:T(8,128)(2,1)} %weight_ref.3), custom_call_target="tpu_custom_call" | custom-call | flops 67108864 | bytes 4194304 | tf_op jit(solution)/shard_map/prepare/pallas_call | solution.py:271
  75.1 2.0 %fusion.1 = s32[]{:T(128)} fusion(s32[15]{0:T(128)} %constant.20.clone, s32[]{:T(128)} %get-tuple-element.98), kind=kLoop, calls=%fused_computation.4 | loop fusion | flops 44 | bytes 68 | tf_op jit(solution)/shard_map/reduce_sum | solution.py:544
  78.2 10.1 %attend.2 = (bf16[128,768]{1,0:T(8,128)(2,1)}, bf16[128,768]{1,0:T(8,128)(2,1)}, bf16[128,768]{1,0:T(8,128)(2,1)}, bf16[128,768]{1,0:T(8,128)(2,1)}) custom-call(s32[1]{0:T(128)} %get-tuple-element.73.frames_ref, bf16[3,128,768]{2,1,0:T(8,128)(2,1)} %get-tuple-element.75.rest_0_, bf16[3,128,768]{2,1,0:T(8,128)(2,1)} %collective-permute-done.15.rest_1_, ...), custom_call_target="tpu_custom_call" | custom-call | flops 2415919104 | bytes 6291456 | tf_op jit(solution)/shard_map/attend/pallas_call | solution.py:185
  88.3 3.7 %collective-permute-start.22 = (bf16[128,768]{1,0:T(8,128)(2,1)}, bf16[128,768]{1,0:T(8,128)(2,1)}, u32[]{:S(2)}, u32[]{:S(2)}) collective-permute-start(bf16[128,768]{1,0:T(8,128)(2,1)} %get-tuple-element.80), channel_id=1, source_target_pairs={{0,2},{1,3},{2,0},{3,1},{4,6},{5,7},{6,4},{7,5},{8,10},{9,11},{10,... | collective-permute-start | bytes 589832 | tf_op jit(solution)/shard_map/ppermute | solution.py:40
  92.0 1.3 collective-permute-start.24
  93.3 4.8 %attend.3 = (bf16[128,256]{1,0:T(8,128)(2,1)}, bf16[128,256]{1,0:T(8,128)(2,1)}, bf16[128,256]{1,0:T(8,128)(2,1)}, bf16[128,256]{1,0:T(8,128)(2,1)}) custom-call(s32[1]{0:T(128)} %get-tuple-element.73.frames_ref, bf16[3,128,256]{2,1,0:T(8,128)(2,1)} %get-tuple-element.90.rest_0_, bf16[3,128,256]{2,1,0:T(8,128)(2,1)} %copy-done, ...), custom_call_target="tpu_custom_call" | custom-call | flops 805306368 | bytes 2097152 | tf_op jit(solution)/shard_map/attend/pallas_call | solution.py:185
  98.1 2.3 %collective-permute-start.32 = (bf16[128,256]{1,0:T(8,128)(2,1)}, bf16[128,256]{1,0:T(8,128)(2,1)}, u32[]{:S(2)}, u32[]{:S(2)}) collective-permute-start(bf16[128,256]{1,0:T(8,128)(2,1)} %get-tuple-element.95), channel_id=1, source_target_pairs={{0,2},{1,3},{2,0},{3,1},{4,6},{5,7},{6,4},{7,5},{8,10},{9,11},{10,... | collective-permute-start | bytes 196616 | tf_op jit(solution)/shard_map/ppermute | solution.py:40
  100.4 1.3 collective-permute-start.34
  102.3 11.3 %collective-permute-done.24.rest_3_ = bf16[128,768]{1,0:T(8,128)(2,1)} collective-permute-done((bf16[128,768]{1,0:T(8,128)(2,1)}, bf16[128,768]{1,0:T(8,128)(2,1)}, u32[]{:S(2)}, u32[]{:S(2)}) %collective-permute-start.24) | collective-permute-done | bytes 196640 | tf_op jit(solution)/shard_map/ppermute | solution.py:40
  113.7 4.3 %project_early.1 = (f32[128,256]{1,0:T(8,128)}, f32[128,128]{1,0:T(8,128)}, f32[128,128]{1,0:T(8,128)}) custom-call(bf16[1,128,4096]{2,1,0:T(8,128)(2,1)} %h_ref.3, f32[3,4096]{1,0:T(4,128)} %bitcast.7, bf16[4096,256]{1,0:T(8,128)(2,1)} %weight_ref.3, bf16[128,768]{1,0:T(8,128)(2,1)} %get-tuple-element.79.rest_0_, ...), custom_call_target="tpu_custom_call" | custom-call | flops 201326592 | bytes 4194304 | tf_op jit(solution)/shard_map/project_early/pallas_call | solution.py:346
  118.0 3.2 %project_late.1 = bf16[128,256]{1,0:T(8,128)(2,1)} custom-call(s32[1]{0:T(128)} %get-tuple-element.73.frames_ref, f32[128,256]{1,0:T(8,128)} %get-tuple-element.83.rest_0_, f32[128,128]{1,0:T(8,128)} %get-tuple-element.84.rest_1_, f32[128,128]{1,0:T(8,128)} %get-tuple-element.85.rest_2_, bf16[128,1024]{1,0:T(8,128)(2,1)} %get-tuple-element.86.rest_3_, ...), custom_call_target="tpu_custom_call" | custom-call | flops 67108864 | bytes 524288 | tf_op jit(solution)/shard_map/project_late/pallas_call | solution.py:422
  121.2 4.4 %conditional.1 = (bf16[128,256]{1,0:T(8,128)(2,1)}) conditional(s32[]{:T(128)} %clamp.3, bf16[128,256]{1,0:T(8,128)(2,1)} %project_late.1, bf16[128,256]{1,0:T(8,128)(2,1)} %project_late.1, bf16[128,256]{1,0:T(8,128)(2,1)} %project_late.1, bf16[128,256]{1,0:T(8,128)(2,1)} %project_late.1, ...), branch_computations={%region_3.4_spmd, %region_4.5_spmd, %region_5.6_spmd, %region_6.7_... | conditional | bytes 262192 | solution.py:552
  121.5 4.1 %collective-permute-done.14 = bf16[128,256]{1,0:T(8,128)(2,1)} collective-permute-done((bf16[128,256]{1,0:T(8,128)(2,1)}, bf16[128,256]{1,0:T(8,128)(2,1)}, u32[]{:S(2)}, u32[]{:S(2)}) %collective-permute-start.14) | collective-permute-done | bytes 65568 | tf_op jit(solution)/shard_map/cond/branch_14_fun/ppermute | solution.py:550
  125.6 3.3 %collective-permute-start.35 = (bf16[128,256]{1,0:T(8,128)(2,1)}, bf16[128,256]{1,0:T(8,128)(2,1)}, u32[]{:S(2)}, u32[]{:S(2)}) collective-permute-start(bf16[128,256]{1,0:T(8,128)(2,1)} %get-tuple-element.102.mid_ref), channel_id=1, source_target_pairs={{0,1},{1,0},{2,3},{3,2},{4,5},{5,4},{6,7},{7,6},{8,9},{9,8},{10,11... | collective-permute-start | bytes 196616 | tf_op jit(solution)/shard_map/ppermute | solution.py:613
  129.0 2.0 %collective-permute-start.36 = (bf16[128,256]{1,0:T(8,128)(2,1)}, bf16[128,256]{1,0:T(8,128)(2,1)}, u32[]{:S(2)}, u32[]{:S(2)}) collective-permute-start(bf16[128,256]{1,0:T(8,128)(2,1)} %get-tuple-element.102.mid_ref), channel_id=1, source_target_pairs={{1,2},{3,4},{5,6},{2,1},{4,3},{6,5},{9,10},{11,12},{13,14},{10,9},... | collective-permute-start | bytes 196616 | tf_op jit(solution)/shard_map/ppermute | solution.py:615
  131.0 3.9 %collective-permute-done.36.odd_ref = bf16[128,256]{1,0:T(8,128)(2,1)} collective-permute-done((bf16[128,256]{1,0:T(8,128)(2,1)}, bf16[128,256]{1,0:T(8,128)(2,1)}, u32[]{:S(2)}, u32[]{:S(2)}) %collective-permute-start.36) | collective-permute-done | bytes 65568 | tf_op jit(solution)/shard_map/ppermute | solution.py:615
  134.9 4.3 %refine.1 = bf16[1,128,256]{2,1,0:T(8,128)(2,1)} custom-call(s32[1]{0:T(128)} %get-tuple-element.71.frames_ref, bf16[128,256]{1,0:T(8,128)(2,1)} %get-tuple-element.102.mid_ref, bf16[128,256]{1,0:T(8,128)(2,1)} %collective-permute-done.35.even_ref, bf16[128,256]{1,0:T(8,128)(2,1)} %collective-permute-done.36.odd_ref, bf16[3,2304,256]{2,1,0:T(8,128)(2,1)} %bitcast.5), custom_call_target="tpu_custom_call" | custom-call | flops 452984832 | bytes 3735552 | tf_op jit(solution)/shard_map/refine/pallas_call | solution.py:504
  (31 shorter events, 2.5 us)
Async XLA Ops:
  2.7 46.3 %collective-permute-start.15 = (bf16[3,128,768]{2,1,0:T(8,128)(2,1)}, bf16[3,128,768]{2,1,0:T(8,128)(2,1)}, u32[]{:S(2)}, u32[]{:S(2)}) collective-permute-start(bf16[3,128,768]{2,1,0:T(8,128)(2,1)} %get-tuple-element.76), channel_id=1, source_target_pairs={{0,2},{1,3},{2,0},{3,1},{4,6},{5,7},{6,4},{7,5},{8,10},{9,11},{10,... | collective-permute-start | bytes 1769480 | tf_op jit(solution)/shard_map/ppermute | solution.py:40
  2.9 47.9 %collective-permute-start.16 = (bf16[3,128,768]{2,1,0:T(8,128)(2,1)}, bf16[3,128,768]{2,1,0:T(8,128)(2,1)}, u32[]{:S(2)}, u32[]{:S(2)}) collective-permute-start(bf16[3,128,768]{2,1,0:T(8,128)(2,1)} %get-tuple-element.77), channel_id=1, source_target_pairs={{0,4},{1,5},{2,6},{3,7},{4,0},{5,1},{6,2},{7,3},{8,12},{9,13},{10,... | collective-permute-start | bytes 1769480 | tf_op jit(solution)/shard_map/ppermute | solution.py:40
  5.2 55.2 %collective-permute-start.17 = (bf16[3,128,768]{2,1,0:T(8,128)(2,1)}, bf16[3,128,768]{2,1,0:T(8,128)(2,1)}, u32[]{:S(2)}, u32[]{:S(2)}) collective-permute-start(bf16[3,128,768]{2,1,0:T(8,128)(2,1)} %get-tuple-element.78), channel_id=1, source_target_pairs={{0,6},{1,7},{2,4},{3,5},{4,2},{5,3},{6,0},{7,1},{8,14},{9,15},{10,... | collective-permute-start | bytes 1769480 | tf_op jit(solution)/shard_map/ppermute | solution.py:40
  7.4 39.4 %collective-permute-start.25 = (bf16[3,128,256]{2,1,0:T(8,128)(2,1)}, bf16[3,128,256]{2,1,0:T(8,128)(2,1)S(1)}, u32[]{:S(2)}, u32[]{:S(2)}) collective-permute-start(bf16[3,128,256]{2,1,0:T(8,128)(2,1)} %get-tuple-element.91), channel_id=1, source_target_pairs={{0,2},{1,3},{2,0},{3,1},{4,6},{5,7},{6,4},{7,5},{8,10},{9,11},{10,... | collective-permute-start | bytes 589832 | tf_op jit(solution)/shard_map/ppermute | solution.py:40
  8.6 68.8 %collective-permute-start.18 = (bf16[3,128,768]{2,1,0:T(8,128)(2,1)}, bf16[3,128,768]{2,1,0:T(8,128)(2,1)}, u32[]{:S(2)}, u32[]{:S(2)}) collective-permute-start(bf16[3,128,768]{2,1,0:T(8,128)(2,1)} %get-tuple-element.75.rest_0_), channel_id=1, source_target_pairs={{0,1},{1,0},{2,3},{3,2},{4,5},{5,4},{6,7},{7,6},{8,9},{9,8},{10,11... | collective-permute-start | bytes 1769480 | tf_op jit(solution)/shard_map/ppermute | solution.py:44
  46.9 13.6 %copy-start = (bf16[3,128,256]{2,1,0:T(8,128)(2,1)}, bf16[3,128,256]{2,1,0:T(8,128)(2,1)S(1)}, u32[]{:S(2)}) copy-start(bf16[3,128,256]{2,1,0:T(8,128)(2,1)S(1)} %collective-permute-done.25.rest_1_) | copy-start | bytes 589828
  46.9 17.8 %collective-permute-start.26 = (bf16[3,128,256]{2,1,0:T(8,128)(2,1)}, bf16[3,128,256]{2,1,0:T(8,128)(2,1)}, u32[]{:S(2)}, u32[]{:S(2)}) collective-permute-start(bf16[3,128,256]{2,1,0:T(8,128)(2,1)} %get-tuple-element.92), channel_id=1, source_target_pairs={{0,4},{1,5},{2,6},{3,7},{4,0},{5,1},{6,2},{7,3},{8,12},{9,13},{10,... | collective-permute-start | bytes 589832 | tf_op jit(solution)/shard_map/ppermute | solution.py:40
  49.0 28.6 %collective-permute-start.19 = (bf16[3,128,768]{2,1,0:T(8,128)(2,1)}, bf16[3,128,768]{2,1,0:T(8,128)(2,1)}, u32[]{:S(2)}, u32[]{:S(2)}) collective-permute-start(bf16[3,128,768]{2,1,0:T(8,128)(2,1)} %collective-permute-done.15.rest_1_), channel_id=1, source_target_pairs={{0,1},{1,0},{2,3},{3,2},{4,5},{5,4},{6,7},{7,6},{8,9},{9,8},{10,11... | collective-permute-start | bytes 1769480 | tf_op jit(solution)/shard_map/ppermute | solution.py:44
  50.8 27.1 %collective-permute-start.20 = (bf16[3,128,768]{2,1,0:T(8,128)(2,1)}, bf16[3,128,768]{2,1,0:T(8,128)(2,1)}, u32[]{:S(2)}, u32[]{:S(2)}) collective-permute-start(bf16[3,128,768]{2,1,0:T(8,128)(2,1)} %collective-permute-done.16.rest_2_), channel_id=1, source_target_pairs={{0,1},{1,0},{2,3},{3,2},{4,5},{5,4},{6,7},{7,6},{8,9},{9,8},{10,11... | collective-permute-start | bytes 1769480 | tf_op jit(solution)/shard_map/ppermute | solution.py:44
  60.5 17.7 %collective-permute-start.21 = (bf16[3,128,768]{2,1,0:T(8,128)(2,1)}, bf16[3,128,768]{2,1,0:T(8,128)(2,1)}, u32[]{:S(2)}, u32[]{:S(2)}) collective-permute-start(bf16[3,128,768]{2,1,0:T(8,128)(2,1)} %collective-permute-done.17.rest_3_), channel_id=1, source_target_pairs={{0,1},{1,0},{2,3},{3,2},{4,5},{5,4},{6,7},{7,6},{8,9},{9,8},{10,11... | collective-permute-start | bytes 1769480 | tf_op jit(solution)/shard_map/ppermute | solution.py:44
  64.6 12.5 %collective-permute-start.27 = (bf16[3,128,256]{2,1,0:T(8,128)(2,1)}, bf16[3,128,256]{2,1,0:T(8,128)(2,1)}, u32[]{:S(2)}, u32[]{:S(2)}) collective-permute-start(bf16[3,128,256]{2,1,0:T(8,128)(2,1)} %get-tuple-element.93), channel_id=1, source_target_pairs={{0,6},{1,7},{2,4},{3,5},{4,2},{5,3},{6,0},{7,1},{8,14},{9,15},{10,... | collective-permute-start | bytes 589832 | tf_op jit(solution)/shard_map/ppermute | solution.py:40
  77.1 14.8 %collective-permute-start.28 = (bf16[3,128,256]{2,1,0:T(8,128)(2,1)}, bf16[3,128,256]{2,1,0:T(8,128)(2,1)}, u32[]{:S(2)}, u32[]{:S(2)}) collective-permute-start(bf16[3,128,256]{2,1,0:T(8,128)(2,1)} %get-tuple-element.90.rest_0_), channel_id=1, source_target_pairs={{0,1},{1,0},{2,3},{3,2},{4,5},{5,4},{6,7},{7,6},{8,9},{9,8},{10,11... | collective-permute-start | bytes 589832 | tf_op jit(solution)/shard_map/ppermute | solution.py:44
  77.4 14.6 %collective-permute-start.29 = (bf16[3,128,256]{2,1,0:T(8,128)(2,1)}, bf16[3,128,256]{2,1,0:T(8,128)(2,1)}, u32[]{:S(2)}, u32[]{:S(2)}) collective-permute-start(bf16[3,128,256]{2,1,0:T(8,128)(2,1)} %copy-done), channel_id=1, source_target_pairs={{0,1},{1,0},{2,3},{3,2},{4,5},{5,4},{6,7},{7,6},{8,9},{9,8},{10,11... | collective-permute-start | bytes 589832 | tf_op jit(solution)/shard_map/ppermute | solution.py:44
  77.7 15.6 %collective-permute-start.30 = (bf16[3,128,256]{2,1,0:T(8,128)(2,1)}, bf16[3,128,256]{2,1,0:T(8,128)(2,1)}, u32[]{:S(2)}, u32[]{:S(2)}) collective-permute-start(bf16[3,128,256]{2,1,0:T(8,128)(2,1)} %collective-permute-done.26.rest_2_), channel_id=1, source_target_pairs={{0,1},{1,0},{2,3},{3,2},{4,5},{5,4},{6,7},{7,6},{8,9},{9,8},{10,11... | collective-permute-start | bytes 589832 | tf_op jit(solution)/shard_map/ppermute | solution.py:44
  77.9 15.3 %collective-permute-start.31 = (bf16[3,128,256]{2,1,0:T(8,128)(2,1)}, bf16[3,128,256]{2,1,0:T(8,128)(2,1)}, u32[]{:S(2)}, u32[]{:S(2)}) collective-permute-start(bf16[3,128,256]{2,1,0:T(8,128)(2,1)} %collective-permute-done.27.rest_3_), channel_id=1, source_target_pairs={{0,1},{1,0},{2,3},{3,2},{4,5},{5,4},{6,7},{7,6},{8,9},{9,8},{10,11... | collective-permute-start | bytes 589832 | tf_op jit(solution)/shard_map/ppermute | solution.py:44
  88.3 12.2 %collective-permute-start.22 = (bf16[128,768]{1,0:T(8,128)(2,1)}, bf16[128,768]{1,0:T(8,128)(2,1)}, u32[]{:S(2)}, u32[]{:S(2)}) collective-permute-start(bf16[128,768]{1,0:T(8,128)(2,1)} %get-tuple-element.80), channel_id=1, source_target_pairs={{0,2},{1,3},{2,0},{3,1},{4,6},{5,7},{6,4},{7,5},{8,10},{9,11},{10,... | collective-permute-start | bytes 589832 | tf_op jit(solution)/shard_map/ppermute | solution.py:40
  92.0 10.3 %collective-permute-start.23 = (bf16[128,768]{1,0:T(8,128)(2,1)}, bf16[128,768]{1,0:T(8,128)(2,1)}, u32[]{:S(2)}, u32[]{:S(2)}) collective-permute-start(bf16[128,768]{1,0:T(8,128)(2,1)} %get-tuple-element.81), channel_id=1, source_target_pairs={{0,4},{1,5},{2,6},{3,7},{4,0},{5,1},{6,2},{7,3},{8,12},{9,13},{10,... | collective-permute-start | bytes 589832 | tf_op jit(solution)/shard_map/ppermute | solution.py:40
  92.0 21.7 %collective-permute-start.24 = (bf16[128,768]{1,0:T(8,128)(2,1)}, bf16[128,768]{1,0:T(8,128)(2,1)}, u32[]{:S(2)}, u32[]{:S(2)}) collective-permute-start(bf16[128,768]{1,0:T(8,128)(2,1)} %get-tuple-element.82), channel_id=1, source_target_pairs={{0,6},{1,7},{2,4},{3,5},{4,2},{5,3},{6,0},{7,1},{8,14},{9,15},{10,... | collective-permute-start | bytes 589832 | tf_op jit(solution)/shard_map/ppermute | solution.py:40
  98.1 19.9 %collective-permute-start.32 = (bf16[128,256]{1,0:T(8,128)(2,1)}, bf16[128,256]{1,0:T(8,128)(2,1)}, u32[]{:S(2)}, u32[]{:S(2)}) collective-permute-start(bf16[128,256]{1,0:T(8,128)(2,1)} %get-tuple-element.95), channel_id=1, source_target_pairs={{0,2},{1,3},{2,0},{3,1},{4,6},{5,7},{6,4},{7,5},{8,10},{9,11},{10,... | collective-permute-start | bytes 196616 | tf_op jit(solution)/shard_map/ppermute | solution.py:40
  100.4 17.5 %collective-permute-start.33 = (bf16[128,256]{1,0:T(8,128)(2,1)}, bf16[128,256]{1,0:T(8,128)(2,1)}, u32[]{:S(2)}, u32[]{:S(2)}) collective-permute-start(bf16[128,256]{1,0:T(8,128)(2,1)} %get-tuple-element.96), channel_id=1, source_target_pairs={{0,4},{1,5},{2,6},{3,7},{4,0},{5,1},{6,2},{7,3},{8,12},{9,13},{10,... | collective-permute-start | bytes 196616 | tf_op jit(solution)/shard_map/ppermute | solution.py:40
  100.4 17.5 %collective-permute-start.34 = (bf16[128,256]{1,0:T(8,128)(2,1)}, bf16[128,256]{1,0:T(8,128)(2,1)}, u32[]{:S(2)}, u32[]{:S(2)}) collective-permute-start(bf16[128,256]{1,0:T(8,128)(2,1)} %get-tuple-element.97), channel_id=1, source_target_pairs={{0,6},{1,7},{2,4},{3,5},{4,2},{5,3},{6,0},{7,1},{8,14},{9,15},{10,... | collective-permute-start | bytes 196616 | tf_op jit(solution)/shard_map/ppermute | solution.py:40
  121.2 4.4 %collective-permute-start.14 = (bf16[128,256]{1,0:T(8,128)(2,1)}, bf16[128,256]{1,0:T(8,128)(2,1)}, u32[]{:S(2)}, u32[]{:S(2)}) collective-permute-start(bf16[128,256]{1,0:T(8,128)(2,1)} %param.14), channel_id=1, source_target_pairs={{0,24},{8,16},{16,0},{24,8},{1,25},{9,17},{17,1},{25,9},{2,26},{10... | collective-permute-start | bytes 196616 | tf_op jit(solution)/shard_map/cond/branch_14_fun/ppermute | solution.py:550
  125.6 5.3 %collective-permute-start.35 = (bf16[128,256]{1,0:T(8,128)(2,1)}, bf16[128,256]{1,0:T(8,128)(2,1)}, u32[]{:S(2)}, u32[]{:S(2)}) collective-permute-start(bf16[128,256]{1,0:T(8,128)(2,1)} %get-tuple-element.102.mid_ref), channel_id=1, source_target_pairs={{0,1},{1,0},{2,3},{3,2},{4,5},{5,4},{6,7},{7,6},{8,9},{9,8},{10,11... | collective-permute-start | bytes 196616 | tf_op jit(solution)/shard_map/ppermute | solution.py:613
  129.0 5.9 %collective-permute-start.36 = (bf16[128,256]{1,0:T(8,128)(2,1)}, bf16[128,256]{1,0:T(8,128)(2,1)}, u32[]{:S(2)}, u32[]{:S(2)}) collective-permute-start(bf16[128,256]{1,0:T(8,128)(2,1)} %get-tuple-element.102.mid_ref), channel_id=1, source_target_pairs={{1,2},{3,4},{5,6},{2,1},{4,3},{6,5},{9,10},{11,12},{13,14},{10,9},... | collective-permute-start | bytes 196616 | tf_op jit(solution)/shard_map/ppermute | solution.py:615
where the time goes:
time: 140 us; the launch traced here: 139 us
  waiting for transfers between devices  62.3 us (44%)
  Pallas kernels  35 us (25%)
  starting transfers between devices  29.4 us (21%)
  between operations  4.78 us (3%)
  local copies, waits for them, and re-layouts  4.33 us (3%)
  other arithmetic  3.43 us (2%)
    ppermute x12, waiting for transfers between devices, send(): return lax.ppermute(value, 'ctx', pairs)  54.3 us
    ppermute x12, starting transfers between devices, send(): return lax.ppermute(value, 'ctx', pairs)  16 us
    pallas_call x2, Pallas kernels, attend(): pl.pallas_call(functools.partial(attend_kernel, chips, heads, block_rows)...  14.9 us
    ppermute x8, starting transfers between devices, across(): return lax.ppermute(value, 'ctx', [(i, i ^ 1) for i in range(2 * chips)])  7.76 us
    pallas_call x2, Pallas kernels, pack(): pl.pallas_call(functools.partial(pack_kernel, chips, kinds, head_cols, fi...  4.7 us
    pallas_call x1, Pallas kernels, refine(): pl.pallas_call(refine_kernel, out_shape=jax.ShapeDtypeStruct((1, rows, ch...  4.35 us
    pallas_call x1, Pallas kernels, project_early(): pl.pallas_call(functools.partial(early_kernel, chips, model // chips), ou...  4.28 us
    ppermute x1, waiting for transfers between devices, take(): return lambda value: lax.ppermute(value, 'sec', list(enumerate(order)))  4.1 us
  transfers between devices with their start and end apart: 23, of which 5 were waited for; matrix products, arithmetic and copies ran while one was open for 6% of the time, Pallas kernels for 18%

commit v1 on v0

--- a/solution.py
+++ b/solution.py
@@ -33,6 +33,11 @@
     return [(i, (i + step) % count) for i in range(count)]
 
 
+def far_first(chips):
+    far = list(range(chips - 1, max(chips // 2, 1) - 1, -1))
+    return far + list(range(chips // 2 - 1, 0, -1)), far[-1]
+
+
 def send(value, step, chips):
     pairs = [
         (2 * one + core, 2 * two + core) for one, two in ring(step, chips) for core in range(2)
@@ -48,12 +53,13 @@
     return partner(lax.axis_index("ctx") // 2, step, chips)
 
 
-def pack_kernel(chips, kinds, head_cols, first_col, width, *rest):
-    sources, outs, (buf, in_sem, out_sem) = rest[:kinds], rest[kinds : kinds + chips], rest[kinds + chips :]
-    order = list(range(chips - 1, -1, -1))
+def pack_kernel(steps, chips, kinds, head_cols, first_col, width, *rest):
+    sources, outs = rest[:kinds], rest[kinds : kinds + len(steps)]
+    buf, in_sem, out_sem = rest[kinds + len(steps) :]
+    order = range(len(steps))
 
     def load(step, kind):
-        col = pl.multiple_of(my_chip(step, chips)[0] * head_cols + first_col, 128)
+        col = pl.multiple_of(my_chip(steps[step], chips)[0] * head_cols + first_col, 128)
         return pltpu.make_async_copy(
             sources[kind].at[0, :, pl.ds(col, width)], buf.at[step, kind], in_sem.at[step, kind]
         )
@@ -72,22 +78,22 @@
         save(step).wait()
 
 
-def pack(sources, chips, head_cols, first_col, width):
+def pack(sources, steps, chips, head_cols, first_col, width):
     rows = sources[0].shape[1]
     kinds = len(sources)
     piece = jax.ShapeDtypeStruct((kinds, rows, width), sources[0].dtype)
     return pl.pallas_call(
-        functools.partial(pack_kernel, chips, kinds, head_cols, first_col, width),
-        out_shape=[piece] * chips,
+        functools.partial(pack_kernel, steps, chips, kinds, head_cols, first_col, width),
+        out_shape=[piece] * len(steps),
         in_specs=[pl.BlockSpec(memory_space=pltpu.HBM)] * kinds,
-        out_specs=[pl.BlockSpec(memory_space=pltpu.HBM)] * chips,
+        out_specs=[pl.BlockSpec(memory_space=pltpu.HBM)] * len(steps),
         scratch_shapes=[
-            pltpu.VMEM((chips, kinds, rows, width), sources[0].dtype),
-            pltpu.SemaphoreType.DMA((chips, kinds)),
-            pltpu.SemaphoreType.DMA((chips,)),
+            pltpu.VMEM((len(steps), kinds, rows, width), sources[0].dtype),
+            pltpu.SemaphoreType.DMA((len(steps), kinds)),
+            pltpu.SemaphoreType.DMA((len(steps),)),
         ],
         cost_estimate=pl.CostEstimate(
-            flops=0, bytes_accessed=4 * kinds * chips * rows * width, transcendentals=0
+            flops=0, bytes_accessed=4 * kinds * len(steps) * rows * width, transcendentals=0
         ),
         compiler_params=pltpu.CompilerParams(vmem_limit_bytes=VMEM_BYTES),
         name="pack",
@@ -585,7 +591,12 @@
 
     own, beside = [], []
     for chunk, width in enumerate(widths):
-        packed = pack(tensors, chips, head_cols, sum(widths[:chunk]), width)
+        packed = [None] * chips
+        order = far_first(chips)[0]
+        for batch in (order[:1], order[1:] + [0]) if chunk == 0 else (order + [0],):
+            pieces = pack(tensors, batch, chips, head_cols, sum(widths[:chunk]), width)
+            for step, piece in zip(batch, pieces):
+                packed[step] = piece
         beside.append([across(packed[0], chips)])
         own.append([packed[0]] + [send(packed[step], step, chips) for step in steps])
         beside[chunk] += [across(own[chunk][step], chips) for step in steps]

time: 140 us -> 140 us (level)
  the two profiles are of different devices: /device:TPU:13 before, /device:TPU:15 now
where the time goes in v1:
time: 140 us; the launch traced here: 139 us
  waiting for transfers between devices  60.3 us (43%)
  Pallas kernels  36.7 us (26%)
  starting transfers between devices  29.4 us (21%)
  between operations  4.79 us (3%)
  local copies, waits for them, and re-layouts  4.33 us (3%)
  other arithmetic  3.43 us (2%)
    ppermute x12, waiting for transfers between devices, send(): return lax.ppermute(value, 'ctx', pairs)  52.2 us
    ppermute x12, starting transfers between devices, send(): return lax.ppermute(value, 'ctx', pairs)  16.1 us
    pallas_call x2, Pallas kernels, attend(): pl.pallas_call(functools.partial(attend_kernel, chips, heads, block_rows)...  14.9 us
    ppermute x8, starting transfers between devices, across(): return lax.ppermute(value, 'ctx', [(i, i ^ 1) for i in range(2 * chips)])  7.73 us
    pallas_call x3, Pallas kernels, pack(): pl.pallas_call(functools.partial(pack_kernel, steps, chips, kinds, head_c...  6.42 us
    pallas_call x1, Pallas kernels, refine(): pl.pallas_call(refine_kernel, out_shape=jax.ShapeDtypeStruct((1, rows, ch...  4.35 us
    pallas_call x1, Pallas kernels, project_early(): pl.pallas_call(functools.partial(early_kernel, chips, model // chips), ou...  4.28 us
    ppermute x1, waiting for transfers between devices, take(): return lambda value: lax.ppermute(value, 'sec', list(enumerate(order)))  4.1 us
  transfers between devices with their start and end apart: 23, of which 5 were waited for; matrix products, arithmetic and copies ran while one was open for 6% of the time, Pallas kernels for 19%

profile of v1, /device:TPU:15, one launch (start us, length us, event | category | flops | bytes accessed | tf_op | source)
XLA Modules:
  0.0 139.0 jit_solution(15444567442360735138)
XLA Ops:
  0.0 2.4 %pack.3 = (bf16[3,128,768]{2,1,0:T(8,128)(2,1)}, bf16[3,128,768]{2,1,0:T(8,128)(2,1)}, bf16[3,128,768]{2,1,0:T(8,128)(2,1)}) custom-call(bf16[1,128,4096]{2,1,0:T(8,128)(2,1)} %rest_0_.5, bf16[1,128,4096]{2,1,0:T(8,128)(2,1)} %rest_1_.5, bf16[1,128,4096]{2,1,0:T(8,128)(2,1)} %rest_2_.5), custom_call_target="tpu_custom_call" | custom-call | bytes 3538944 | tf_op jit(solution)/shard_map/pack/pallas_call | solution.py:85
  2.7 2.3 %collective-permute-start.16 = (bf16[3,128,768]{2,1,0:T(8,128)(2,1)}, bf16[3,128,768]{2,1,0:T(8,128)(2,1)}, u32[]{:S(2)}, u32[]{:S(2)}) collective-permute-start(bf16[3,128,768]{2,1,0:T(8,128)(2,1)} %get-tuple-element.76), channel_id=1, source_target_pairs={{0,4},{1,5},{2,6},{3,7},{4,0},{5,1},{6,2},{7,3},{8,12},{9,13},{10,... | collective-permute-start | bytes 1769480 | tf_op jit(solution)/shard_map/ppermute | solution.py:45
  5.0 2.0 %pack.4 = bf16[3,128,768]{2,1,0:T(8,128)(2,1)} custom-call(bf16[1,128,4096]{2,1,0:T(8,128)(2,1)} %rest_0_.5, bf16[1,128,4096]{2,1,0:T(8,128)(2,1)} %rest_1_.5, bf16[1,128,4096]{2,1,0:T(8,128)(2,1)} %rest_2_.5), custom_call_target="tpu_custom_call" | custom-call | bytes 1179648 | tf_op jit(solution)/shard_map/pack/pallas_call | solution.py:85
  7.2 2.0 %pack.5 = (bf16[3,128,256]{2,1,0:T(8,128)(2,1)}, bf16[3,128,256]{2,1,0:T(8,128)(2,1)}, bf16[3,128,256]{2,1,0:T(8,128)(2,1)}, bf16[3,128,256]{2,1,0:T(8,128)(2,1)}) custom-call(bf16[1,128,4096]{2,1,0:T(8,128)(2,1)} %rest_0_.5, bf16[1,128,4096]{2,1,0:T(8,128)(2,1)} %rest_1_.5, bf16[1,128,4096]{2,1,0:T(8,128)(2,1)} %rest_2_.5), custom_call_target="tpu_custom_call" | custom-call | bytes 1572864 | tf_op jit(solution)/shard_map/pack/pallas_call | solution.py:85
  9.2 1.2 collective-permute-start.25
  10.5 1.7 %collective-permute-start.18 = (bf16[3,128,768]{2,1,0:T(8,128)(2,1)}, bf16[3,128,768]{2,1,0:T(8,128)(2,1)}, u32[]{:S(2)}, u32[]{:S(2)}) collective-permute-start(bf16[3,128,768]{2,1,0:T(8,128)(2,1)} %get-tuple-element.74.rest_0_), channel_id=1, source_target_pairs={{0,1},{1,0},{2,3},{3,2},{4,5},{5,4},{6,7},{7,6},{8,9},{9,8},{10,11... | collective-permute-start | bytes 1769480 | tf_op jit(solution)/shard_map/ppermute | solution.py:49
  12.2 1.2 dynamic_slice.15
  15.3 31.3 %collective-permute-done.25.rest_1_ = bf16[3,128,256]{2,1,0:T(8,128)(2,1)S(1)} collective-permute-done((bf16[3,128,256]{2,1,0:T(8,128)(2,1)}, bf16[3,128,256]{2,1,0:T(8,128)(2,1)S(1)}, u32[]{:S(2)}, u32[]{:S(2)}) %collective-permute-start.25) | collective-permute-done | bytes 196640 | tf_op jit(solution)/shard_map/ppermute | solution.py:45
  46.6 2.1 %collective-permute-start.26 = (bf16[3,128,256]{2,1,0:T(8,128)(2,1)}, bf16[3,128,256]{2,1,0:T(8,128)(2,1)}, u32[]{:S(2)}, u32[]{:S(2)}) collective-permute-start(bf16[3,128,256]{2,1,0:T(8,128)(2,1)} %get-tuple-element.90), channel_id=1, source_target_pairs={{0,4},{1,5},{2,6},{3,7},{4,0},{5,1},{6,2},{7,3},{8,12},{9,13},{10,... | collective-permute-start | bytes 589832 | tf_op jit(solution)/shard_map/ppermute | solution.py:45
  48.8 1.8 %collective-permute-start.19 = (bf16[3,128,768]{2,1,0:T(8,128)(2,1)}, bf16[3,128,768]{2,1,0:T(8,128)(2,1)}, u32[]{:S(2)}, u32[]{:S(2)}) collective-permute-start(bf16[3,128,768]{2,1,0:T(8,128)(2,1)} %collective-permute-done.15.rest_1_), channel_id=1, source_target_pairs={{0,1},{1,0},{2,3},{3,2},{4,5},{5,4},{6,7},{7,6},{8,9},{9,8},{10,11... | collective-permute-start | bytes 1769480 | tf_op jit(solution)/shard_map/ppermute | solution.py:49
  50.6 9.6 %collective-permute-done.17.rest_3_ = bf16[3,128,768]{2,1,0:T(8,128)(2,1)} collective-permute-done((bf16[3,128,768]{2,1,0:T(8,128)(2,1)}, bf16[3,128,768]{2,1,0:T(8,128)(2,1)}, u32[]{:S(2)}, u32[]{:S(2)}) %collective-permute-start.17) | collective-permute-done | bytes 589856 | tf_op jit(solution)/shard_map/ppermute | solution.py:45
  60.2 3.1 %collective-permute-start.21 = (bf16[3,128,768]{2,1,0:T(8,128)(2,1)}, bf16[3,128,768]{2,1,0:T(8,128)(2,1)}, u32[]{:S(2)}, u32[]{:S(2)}) collective-permute-start(bf16[3,128,768]{2,1,0:T(8,128)(2,1)} %collective-permute-done.17.rest_3_), channel_id=1, source_target_pairs={{0,1},{1,0},{2,3},{3,2},{4,5},{5,4},{6,7},{7,6},{8,9},{9,8},{10,11... | collective-permute-start | bytes 1769480 | tf_op jit(solution)/shard_map/ppermute | solution.py:49
  64.4 1.4 collective-permute-start.27
  65.8 1.4 %multiply_reduce_fusion = (s32[]{:T(128)}, s32[]{:T(128)}) fusion(s32[4]{0:T(128)} %param.35, s32[4]{0:T(128)} %constant.21.clone, s32[]{:T(128)S(6)} %axis_index.15), kind=kLoop, calls=%fused_computation.5 | loop fusion | flops 18 | bytes 44 | tf_op jit(solution)/shard_map/reduce_sum | solution.py:549
  69.9 1.4 %fusion.2 = (s32[1]{0:T(128)}, s32[1]{0:T(128)}) fusion(s32[4]{0:T(128)} %param.34, s32[]{:T(128)S(6)} %select_n.21, s32[]{:T(128)S(6)} %select_n.19), kind=kLoop, calls=%fused_computation.7 | loop fusion | bytes 24 | tf_op jit(solution)/shard_map/dynamic_slice | solution.py:607
  71.3 3.6 %prepare.1 = (bf16[128,1024]{1,0:T(8,128)(2,1)}, f32[3,1024]{1,0:T(4,128)}, bf16[1024,256]{1,0:T(8,128)(2,1)}, f32[2,8,256]{2,1,0:T(8,128)}) custom-call(bf16[1,128,4096]{2,1,0:T(8,128)(2,1)} %h_ref.3, f32[3,4096]{1,0:T(4,128)} %bitcast.6, bf16[4096,256]{1,0:T(8,128)(2,1)} %weight_ref.3), custom_call_target="tpu_custom_call" | custom-call | flops 67108864 | bytes 4194304 | tf_op jit(solution)/shard_map/prepare/pallas_call | solution.py:277
  74.9 2.0 %fusion.1 = s32[]{:T(128)} fusion(s32[15]{0:T(128)} %constant.20.clone, s32[]{:T(128)} %get-tuple-element.96), kind=kLoop, calls=%fused_computation.4 | loop fusion | flops 44 | bytes 68 | tf_op jit(solution)/shard_map/reduce_sum | solution.py:550
  77.9 10.1 %attend.2 = (bf16[128,768]{1,0:T(8,128)(2,1)}, bf16[128,768]{1,0:T(8,128)(2,1)}, bf16[128,768]{1,0:T(8,128)(2,1)}, bf16[128,768]{1,0:T(8,128)(2,1)}) custom-call(s32[1]{0:T(128)} %get-tuple-element.72.frames_ref, bf16[3,128,768]{2,1,0:T(8,128)(2,1)} %get-tuple-element.74.rest_0_, bf16[3,128,768]{2,1,0:T(8,128)(2,1)} %collective-permute-done.15.rest_1_, ...), custom_call_target="tpu_custom_call" | custom-call | flops 2415919104 | bytes 6291456 | tf_op jit(solution)/shard_map/attend/pallas_call | solution.py:191
  88.0 3.7 %collective-permute-start.22 = (bf16[128,768]{1,0:T(8,128)(2,1)}, bf16[128,768]{1,0:T(8,128)(2,1)}, u32[]{:S(2)}, u32[]{:S(2)}) collective-permute-start(bf16[128,768]{1,0:T(8,128)(2,1)} %get-tuple-element.78), channel_id=1, source_target_pairs={{0,2},{1,3},{2,0},{3,1},{4,6},{5,7},{6,4},{7,5},{8,10},{9,11},{10,... | collective-permute-start | bytes 589832 | tf_op jit(solution)/shard_map/ppermute | solution.py:45
  91.8 1.3 collective-permute-start.24
  93.0 4.8 %attend.3 = (bf16[128,256]{1,0:T(8,128)(2,1)}, bf16[128,256]{1,0:T(8,128)(2,1)}, bf16[128,256]{1,0:T(8,128)(2,1)}, bf16[128,256]{1,0:T(8,128)(2,1)}) custom-call(s32[1]{0:T(128)} %get-tuple-element.72.frames_ref, bf16[3,128,256]{2,1,0:T(8,128)(2,1)} %get-tuple-element.88.rest_0_, bf16[3,128,256]{2,1,0:T(8,128)(2,1)} %copy-done, ...), custom_call_target="tpu_custom_call" | custom-call | flops 805306368 | bytes 2097152 | tf_op jit(solution)/shard_map/attend/pallas_call | solution.py:191
  97.8 2.3 %collective-permute-start.32 = (bf16[128,256]{1,0:T(8,128)(2,1)}, bf16[128,256]{1,0:T(8,128)(2,1)}, u32[]{:S(2)}, u32[]{:S(2)}) collective-permute-start(bf16[128,256]{1,0:T(8,128)(2,1)} %get-tuple-element.93), channel_id=1, source_target_pairs={{0,2},{1,3},{2,0},{3,1},{4,6},{5,7},{6,4},{7,5},{8,10},{9,11},{10,... | collective-permute-start | bytes 196616 | tf_op jit(solution)/shard_map/ppermute | solution.py:45
  100.2 1.3 collective-permute-start.34
  102.1 11.3 %collective-permute-done.24.rest_3_ = bf16[128,768]{1,0:T(8,128)(2,1)} collective-permute-done((bf16[128,768]{1,0:T(8,128)(2,1)}, bf16[128,768]{1,0:T(8,128)(2,1)}, u32[]{:S(2)}, u32[]{:S(2)}) %collective-permute-start.24) | collective-permute-done | bytes 196640 | tf_op jit(solution)/shard_map/ppermute | solution.py:45
  113.4 4.3 %project_early.1 = (f32[128,256]{1,0:T(8,128)}, f32[128,128]{1,0:T(8,128)}, f32[128,128]{1,0:T(8,128)}) custom-call(bf16[1,128,4096]{2,1,0:T(8,128)(2,1)} %h_ref.3, f32[3,4096]{1,0:T(4,128)} %bitcast.7, bf16[4096,256]{1,0:T(8,128)(2,1)} %weight_ref.3, bf16[128,768]{1,0:T(8,128)(2,1)} %get-tuple-element.77.rest_0_, ...), custom_call_target="tpu_custom_call" | custom-call | flops 201326592 | bytes 4194304 | tf_op jit(solution)/shard_map/project_early/pallas_call | solution.py:352
  117.7 3.2 %project_late.1 = bf16[128,256]{1,0:T(8,128)(2,1)} custom-call(s32[1]{0:T(128)} %get-tuple-element.72.frames_ref, f32[128,256]{1,0:T(8,128)} %get-tuple-element.81.rest_0_, f32[128,128]{1,0:T(8,128)} %get-tuple-element.82.rest_1_, f32[128,128]{1,0:T(8,128)} %get-tuple-element.83.rest_2_, bf16[128,1024]{1,0:T(8,128)(2,1)} %get-tuple-element.84.rest_3_, ...), custom_call_target="tpu_custom_call" | custom-call | flops 67108864 | bytes 524288 | tf_op jit(solution)/shard_map/project_late/pallas_call | solution.py:428
  120.9 4.4 %conditional.1 = (bf16[128,256]{1,0:T(8,128)(2,1)}) conditional(s32[]{:T(128)} %clamp.3, bf16[128,256]{1,0:T(8,128)(2,1)} %project_late.1, bf16[128,256]{1,0:T(8,128)(2,1)} %project_late.1, bf16[128,256]{1,0:T(8,128)(2,1)} %project_late.1, bf16[128,256]{1,0:T(8,128)(2,1)} %project_late.1, ...), branch_computations={%region_3.4_spmd, %region_4.5_spmd, %region_5.6_spmd, %region_6.7_... | conditional | bytes 262192 | solution.py:558
  121.3 4.1 %collective-permute-done.14 = bf16[128,256]{1,0:T(8,128)(2,1)} collective-permute-done((bf16[128,256]{1,0:T(8,128)(2,1)}, bf16[128,256]{1,0:T(8,128)(2,1)}, u32[]{:S(2)}, u32[]{:S(2)}) %collective-permute-start.14) | collective-permute-done | bytes 65568 | tf_op jit(solution)/shard_map/cond/branch_14_fun/ppermute | solution.py:556
  125.4 3.3 %collective-permute-start.35 = (bf16[128,256]{1,0:T(8,128)(2,1)}, bf16[128,256]{1,0:T(8,128)(2,1)}, u32[]{:S(2)}, u32[]{:S(2)}) collective-permute-start(bf16[128,256]{1,0:T(8,128)(2,1)} %get-tuple-element.100.mid_ref), channel_id=1, source_target_pairs={{0,1},{1,0},{2,3},{3,2},{4,5},{5,4},{6,7},{7,6},{8,9},{9,8},{10,11... | collective-permute-start | bytes 196616 | tf_op jit(solution)/shard_map/ppermute | solution.py:624
  128.7 2.0 %collective-permute-start.36 = (bf16[128,256]{1,0:T(8,128)(2,1)}, bf16[128,256]{1,0:T(8,128)(2,1)}, u32[]{:S(2)}, u32[]{:S(2)}) collective-permute-start(bf16[128,256]{1,0:T(8,128)(2,1)} %get-tuple-element.100.mid_ref), channel_id=1, source_target_pairs={{1,2},{3,4},{5,6},{2,1},{4,3},{6,5},{9,10},{11,12},{13,14},{10,9},... | collective-permute-start | bytes 196616 | tf_op jit(solution)/shard_map/ppermute | solution.py:626
  130.7 3.9 %collective-permute-done.36.odd_ref = bf16[128,256]{1,0:T(8,128)(2,1)} collective-permute-done((bf16[128,256]{1,0:T(8,128)(2,1)}, bf16[128,256]{1,0:T(8,128)(2,1)}, u32[]{:S(2)}, u32[]{:S(2)}) %collective-permute-start.36) | collective-permute-done | bytes 65568 | tf_op jit(solution)/shard_map/ppermute | solution.py:626
  134.6 4.3 %refine.1 = bf16[1,128,256]{2,1,0:T(8,128)(2,1)} custom-call(s32[1]{0:T(128)} %get-tuple-element.70.frames_ref, bf16[128,256]{1,0:T(8,128)(2,1)} %get-tuple-element.100.mid_ref, bf16[128,256]{1,0:T(8,128)(2,1)} %collective-permute-done.35.even_ref, bf16[128,256]{1,0:T(8,128)(2,1)} %collective-permute-done.36.odd_ref, bf16[3,2304,256]{2,1,0:T(8,128)(2,1)} %bitcast.5), custom_call_target="tpu_custom_call" | custom-call | flops 452984832 | bytes 3735552 | tf_op jit(solution)/shard_map/refine/pallas_call | solution.py:510
  (32 shorter events, 3.6 us)
Async XLA Ops:
  2.5 46.3 %collective-permute-start.15 = (bf16[3,128,768]{2,1,0:T(8,128)(2,1)}, bf16[3,128,768]{2,1,0:T(8,128)(2,1)}, u32[]{:S(2)}, u32[]{:S(2)}) collective-permute-start(bf16[3,128,768]{2,1,0:T(8,128)(2,1)} %get-tuple-element.75), channel_id=1, source_target_pairs={{0,2},{1,3},{2,0},{3,1},{4,6},{5,7},{6,4},{7,5},{8,10},{9,11},{10,... | collective-permute-start | bytes 1769480 | tf_op jit(solution)/shard_map/ppermute | solution.py:45
  2.7 47.9 %collective-permute-start.16 = (bf16[3,128,768]{2,1,0:T(8,128)(2,1)}, bf16[3,128,768]{2,1,0:T(8,128)(2,1)}, u32[]{:S(2)}, u32[]{:S(2)}) collective-permute-start(bf16[3,128,768]{2,1,0:T(8,128)(2,1)} %get-tuple-element.76), channel_id=1, source_target_pairs={{0,4},{1,5},{2,6},{3,7},{4,0},{5,1},{6,2},{7,3},{8,12},{9,13},{10,... | collective-permute-start | bytes 1769480 | tf_op jit(solution)/shard_map/ppermute | solution.py:45
  7.0 53.2 %collective-permute-start.17 = (bf16[3,128,768]{2,1,0:T(8,128)(2,1)}, bf16[3,128,768]{2,1,0:T(8,128)(2,1)}, u32[]{:S(2)}, u32[]{:S(2)}) collective-permute-start(bf16[3,128,768]{2,1,0:T(8,128)(2,1)} %pack.4), channel_id=1, source_target_pairs={{0,6},{1,7},{2,4},{3,5},{4,2},{5,3},{6,0},{7,1},{8,14},{9,15},{10,... | collective-permute-start | bytes 1769480 | tf_op jit(solution)/shard_map/ppermute | solution.py:45
  9.2 37.4 %collective-permute-start.25 = (bf16[3,128,256]{2,1,0:T(8,128)(2,1)}, bf16[3,128,256]{2,1,0:T(8,128)(2,1)S(1)}, u32[]{:S(2)}, u32[]{:S(2)}) collective-permute-start(bf16[3,128,256]{2,1,0:T(8,128)(2,1)} %get-tuple-element.89), channel_id=1, source_target_pairs={{0,2},{1,3},{2,0},{3,1},{4,6},{5,7},{6,4},{7,5},{8,10},{9,11},{10,... | collective-permute-start | bytes 589832 | tf_op jit(solution)/shard_map/ppermute | solution.py:45
  10.5 66.7 %collective-permute-start.18 = (bf16[3,128,768]{2,1,0:T(8,128)(2,1)}, bf16[3,128,768]{2,1,0:T(8,128)(2,1)}, u32[]{:S(2)}, u32[]{:S(2)}) collective-permute-start(bf16[3,128,768]{2,1,0:T(8,128)(2,1)} %get-tuple-element.74.rest_0_), channel_id=1, source_target_pairs={{0,1},{1,0},{2,3},{3,2},{4,5},{5,4},{6,7},{7,6},{8,9},{9,8},{10,11... | collective-permute-start | bytes 1769480 | tf_op jit(solution)/shard_map/ppermute | solution.py:49
  46.6 13.6 %copy-start = (bf16[3,128,256]{2,1,0:T(8,128)(2,1)}, bf16[3,128,256]{2,1,0:T(8,128)(2,1)S(1)}, u32[]{:S(2)}) copy-start(bf16[3,128,256]{2,1,0:T(8,128)(2,1)S(1)} %collective-permute-done.25.rest_1_) | copy-start | bytes 589828
  46.6 17.8 %collective-permute-start.26 = (bf16[3,128,256]{2,1,0:T(8,128)(2,1)}, bf16[3,128,256]{2,1,0:T(8,128)(2,1)}, u32[]{:S(2)}, u32[]{:S(2)}) collective-permute-start(bf16[3,128,256]{2,1,0:T(8,128)(2,1)} %get-tuple-element.90), channel_id=1, source_target_pairs={{0,4},{1,5},{2,6},{3,7},{4,0},{5,1},{6,2},{7,3},{8,12},{9,13},{10,... | collective-permute-start | bytes 589832 | tf_op jit(solution)/shard_map/ppermute | solution.py:45
  48.8 28.6 %collective-permute-start.19 = (bf16[3,128,768]{2,1,0:T(8,128)(2,1)}, bf16[3,128,768]{2,1,0:T(8,128)(2,1)}, u32[]{:S(2)}, u32[]{:S(2)}) collective-permute-start(bf16[3,128,768]{2,1,0:T(8,128)(2,1)} %collective-permute-done.15.rest_1_), channel_id=1, source_target_pairs={{0,1},{1,0},{2,3},{3,2},{4,5},{5,4},{6,7},{7,6},{8,9},{9,8},{10,11... | collective-permute-start | bytes 1769480 | tf_op jit(solution)/shard_map/ppermute | solution.py:49
  50.6 27.1 %collective-permute-start.20 = (bf16[3,128,768]{2,1,0:T(8,128)(2,1)}, bf16[3,128,768]{2,1,0:T(8,128)(2,1)}, u32[]{:S(2)}, u32[]{:S(2)}) collective-permute-start(bf16[3,128,768]{2,1,0:T(8,128)(2,1)} %collective-permute-done.16.rest_2_), channel_id=1, source_target_pairs={{0,1},{1,0},{2,3},{3,2},{4,5},{5,4},{6,7},{7,6},{8,9},{9,8},{10,11... | collective-permute-start | bytes 1769480 | tf_op jit(solution)/shard_map/ppermute | solution.py:49
  60.2 17.7 %collective-permute-start.21 = (bf16[3,128,768]{2,1,0:T(8,128)(2,1)}, bf16[3,128,768]{2,1,0:T(8,128)(2,1)}, u32[]{:S(2)}, u32[]{:S(2)}) collective-permute-start(bf16[3,128,768]{2,1,0:T(8,128)(2,1)} %collective-permute-done.17.rest_3_), channel_id=1, source_target_pairs={{0,1},{1,0},{2,3},{3,2},{4,5},{5,4},{6,7},{7,6},{8,9},{9,8},{10,11... | collective-permute-start | bytes 1769480 | tf_op jit(solution)/shard_map/ppermute | solution.py:49
  64.4 12.5 %collective-permute-start.27 = (bf16[3,128,256]{2,1,0:T(8,128)(2,1)}, bf16[3,128,256]{2,1,0:T(8,128)(2,1)}, u32[]{:S(2)}, u32[]{:S(2)}) collective-permute-start(bf16[3,128,256]{2,1,0:T(8,128)(2,1)} %get-tuple-element.91), channel_id=1, source_target_pairs={{0,6},{1,7},{2,4},{3,5},{4,2},{5,3},{6,0},{7,1},{8,14},{9,15},{10,... | collective-permute-start | bytes 589832 | tf_op jit(solution)/shard_map/ppermute | solution.py:45
  76.9 14.8 %collective-permute-start.28 = (bf16[3,128,256]{2,1,0:T(8,128)(2,1)}, bf16[3,128,256]{2,1,0:T(8,128)(2,1)}, u32[]{:S(2)}, u32[]{:S(2)}) collective-permute-start(bf16[3,128,256]{2,1,0:T(8,128)(2,1)} %get-tuple-element.88.rest_0_), channel_id=1, source_target_pairs={{0,1},{1,0},{2,3},{3,2},{4,5},{5,4},{6,7},{7,6},{8,9},{9,8},{10,11... | collective-permute-start | bytes 589832 | tf_op jit(solution)/shard_map/ppermute | solution.py:49
  77.2 14.6 %collective-permute-start.29 = (bf16[3,128,256]{2,1,0:T(8,128)(2,1)}, bf16[3,128,256]{2,1,0:T(8,128)(2,1)}, u32[]{:S(2)}, u32[]{:S(2)}) collective-permute-start(bf16[3,128,256]{2,1,0:T(8,128)(2,1)} %copy-done), channel_id=1, source_target_pairs={{0,1},{1,0},{2,3},{3,2},{4,5},{5,4},{6,7},{7,6},{8,9},{9,8},{10,11... | collective-permute-start | bytes 589832 | tf_op jit(solution)/shard_map/ppermute | solution.py:49
  77.4 15.6 %collective-permute-start.30 = (bf16[3,128,256]{2,1,0:T(8,128)(2,1)}, bf16[3,128,256]{2,1,0:T(8,128)(2,1)}, u32[]{:S(2)}, u32[]{:S(2)}) collective-permute-start(bf16[3,128,256]{2,1,0:T(8,128)(2,1)} %collective-permute-done.26.rest_2_), channel_id=1, source_target_pairs={{0,1},{1,0},{2,3},{3,2},{4,5},{5,4},{6,7},{7,6},{8,9},{9,8},{10,11... | collective-permute-start | bytes 589832 | tf_op jit(solution)/shard_map/ppermute | solution.py:49
  77.7 15.3 %collective-permute-start.31 = (bf16[3,128,256]{2,1,0:T(8,128)(2,1)}, bf16[3,128,256]{2,1,0:T(8,128)(2,1)}, u32[]{:S(2)}, u32[]{:S(2)}) collective-permute-start(bf16[3,128,256]{2,1,0:T(8,128)(2,1)} %collective-permute-done.27.rest_3_), channel_id=1, source_target_pairs={{0,1},{1,0},{2,3},{3,2},{4,5},{5,4},{6,7},{7,6},{8,9},{9,8},{10,11... | collective-permute-start | bytes 589832 | tf_op jit(solution)/shard_map/ppermute | solution.py:49
  88.0 12.2 %collective-permute-start.22 = (bf16[128,768]{1,0:T(8,128)(2,1)}, bf16[128,768]{1,0:T(8,128)(2,1)}, u32[]{:S(2)}, u32[]{:S(2)}) collective-permute-start(bf16[128,768]{1,0:T(8,128)(2,1)} %get-tuple-element.78), channel_id=1, source_target_pairs={{0,2},{1,3},{2,0},{3,1},{4,6},{5,7},{6,4},{7,5},{8,10},{9,11},{10,... | collective-permute-start | bytes 589832 | tf_op jit(solution)/shard_map/ppermute | solution.py:45
  91.7 10.3 %collective-permute-start.23 = (bf16[128,768]{1,0:T(8,128)(2,1)}, bf16[128,768]{1,0:T(8,128)(2,1)}, u32[]{:S(2)}, u32[]{:S(2)}) collective-permute-start(bf16[128,768]{1,0:T(8,128)(2,1)} %get-tuple-element.79), channel_id=1, source_target_pairs={{0,4},{1,5},{2,6},{3,7},{4,0},{5,1},{6,2},{7,3},{8,12},{9,13},{10,... | collective-permute-start | bytes 589832 | tf_op jit(solution)/shard_map/ppermute | solution.py:45
  91.8 21.7 %collective-permute-start.24 = (bf16[128,768]{1,0:T(8,128)(2,1)}, bf16[128,768]{1,0:T(8,128)(2,1)}, u32[]{:S(2)}, u32[]{:S(2)}) collective-permute-start(bf16[128,768]{1,0:T(8,128)(2,1)} %get-tuple-element.80), channel_id=1, source_target_pairs={{0,6},{1,7},{2,4},{3,5},{4,2},{5,3},{6,0},{7,1},{8,14},{9,15},{10,... | collective-permute-start | bytes 589832 | tf_op jit(solution)/shard_map/ppermute | solution.py:45
  97.8 19.9 %collective-permute-start.32 = (bf16[128,256]{1,0:T(8,128)(2,1)}, bf16[128,256]{1,0:T(8,128)(2,1)}, u32[]{:S(2)}, u32[]{:S(2)}) collective-permute-start(bf16[128,256]{1,0:T(8,128)(2,1)} %get-tuple-element.93), channel_id=1, source_target_pairs={{0,2},{1,3},{2,0},{3,1},{4,6},{5,7},{6,4},{7,5},{8,10},{9,11},{10,... | collective-permute-start | bytes 196616 | tf_op jit(solution)/shard_map/ppermute | solution.py:45
  100.2 17.5 %collective-permute-start.33 = (bf16[128,256]{1,0:T(8,128)(2,1)}, bf16[128,256]{1,0:T(8,128)(2,1)}, u32[]{:S(2)}, u32[]{:S(2)}) collective-permute-start(bf16[128,256]{1,0:T(8,128)(2,1)} %get-tuple-element.94), channel_id=1, source_target_pairs={{0,4},{1,5},{2,6},{3,7},{4,0},{5,1},{6,2},{7,3},{8,12},{9,13},{10,... | collective-permute-start | bytes 196616 | tf_op jit(solution)/shard_map/ppermute | solution.py:45
  100.2 17.5 %collective-permute-start.34 = (bf16[128,256]{1,0:T(8,128)(2,1)}, bf16[128,256]{1,0:T(8,128)(2,1)}, u32[]{:S(2)}, u32[]{:S(2)}) collective-permute-start(bf16[128,256]{1,0:T(8,128)(2,1)} %get-tuple-element.95), channel_id=1, source_target_pairs={{0,6},{1,7},{2,4},{3,5},{4,2},{5,3},{6,0},{7,1},{8,14},{9,15},{10,... | collective-permute-start | bytes 196616 | tf_op jit(solution)/shard_map/ppermute | solution.py:45
  121.0 4.4 %collective-permute-start.14 = (bf16[128,256]{1,0:T(8,128)(2,1)}, bf16[128,256]{1,0:T(8,128)(2,1)}, u32[]{:S(2)}, u32[]{:S(2)}) collective-permute-start(bf16[128,256]{1,0:T(8,128)(2,1)} %param.14), channel_id=1, source_target_pairs={{0,24},{8,16},{16,0},{24,8},{1,25},{9,17},{17,1},{25,9},{2,26},{10... | collective-permute-start | bytes 196616 | tf_op jit(solution)/shard_map/cond/branch_14_fun/ppermute | solution.py:556
  125.4 5.3 %collective-permute-start.35 = (bf16[128,256]{1,0:T(8,128)(2,1)}, bf16[128,256]{1,0:T(8,128)(2,1)}, u32[]{:S(2)}, u32[]{:S(2)}) collective-permute-start(bf16[128,256]{1,0:T(8,128)(2,1)} %get-tuple-element.100.mid_ref), channel_id=1, source_target_pairs={{0,1},{1,0},{2,3},{3,2},{4,5},{5,4},{6,7},{7,6},{8,9},{9,8},{10,11... | collective-permute-start | bytes 196616 | tf_op jit(solution)/shard_map/ppermute | solution.py:624
  128.7 5.9 %collective-permute-start.36 = (bf16[128,256]{1,0:T(8,128)(2,1)}, bf16[128,256]{1,0:T(8,128)(2,1)}, u32[]{:S(2)}, u32[]{:S(2)}) collective-permute-start(bf16[128,256]{1,0:T(8,128)(2,1)} %get-tuple-element.100.mid_ref), channel_id=1, source_target_pairs={{1,2},{3,4},{5,6},{2,1},{4,3},{6,5},{9,10},{11,12},{13,14},{10,9},... | collective-permute-start | bytes 196616 | tf_op jit(solution)/shard_map/ppermute | solution.py:626

commit v2 on v1

--- a/solution.py
+++ b/solution.py
@@ -12,6 +12,7 @@
 
 HEADS = 32
 VMEM_BYTES = 67043328
+SPARE_BYTES = 128 * 1024
 HH = 8
 WW = 8
 
@@ -295,10 +296,15 @@
     )(hidden_state, mod_rows, down_weight)
 
 
+def share(rows, channels, later):
+    kept = sum(array.size * array.dtype.itemsize for array in later)
+    return VMEM_BYTES - kept - 4 * rows * (channels + 256) - SPARE_BYTES
+
+
 def early_kernel(chips, head_cols, h_ref, mod_ref, weight_ref, *rest):
-    pieces, rest = rest[:chips], rest[chips:]
+    pieces, later, rest = rest[:chips], rest[chips : chips + 5], rest[chips + 5 :]
     acc_ref, centre_ref, square_ref = rest[:3]
-    attended, hidden, weight, mod, sem = rest[3:]
+    kept, (attended, hidden, weight, mod, sem, keep_sem) = rest[3:8], rest[8:]
     rows, width = pieces[0].shape
     block_rows = 16
 
@@ -313,9 +319,14 @@
         )[which]
         return pltpu.make_async_copy(source, target, sem.at[which, step])
 
+    def keep(which):
+        return pltpu.make_async_copy(later[which], kept[which], keep_sem.at[which])
+
     for which in range(4):
         for step in range(chips):
             pull(step, which).start()
+    for which in range(5):
+        keep(which).start()
     for which in range(3):
         for step in range(chips):
             pull(step, which).wait()
@@ -338,13 +349,15 @@
         square_ref[here, :] = jnp.broadcast_to(square, (block_rows, 128))
         return carry
 
-    lax.fori_loop(0, rows // block_rows, rows_of, 0, unroll=2)
+    lax.fori_loop(0, rows // block_rows, rows_of, 0, unroll=4)
     for step in range(chips):
         pull(step, 3).wait()
     acc_ref[...] = jnp.dot(attended[...], weight[...], preferred_element_type=jnp.float32)
-
-
-def project_early(hidden_state, mod_rows, down_weight, pieces):
+    for which in range(5):
+        keep(which).wait()
+
+
+def project_early(hidden_state, mod_rows, down_weight, pieces, later):
     chips = len(pieces)
     _, rows, model = hidden_state.shape
     channels = down_weight.shape[1]
@@ -352,32 +365,33 @@
     return pl.pallas_call(
         functools.partial(early_kernel, chips, model // chips),
         out_shape=[
-            jax.ShapeDtypeStruct((rows, channels), jnp.float32),
-            jax.ShapeDtypeStruct((rows, 128), jnp.float32),
-            jax.ShapeDtypeStruct((rows, 128), jnp.float32),
-        ],
-        in_specs=[pl.BlockSpec(memory_space=pltpu.HBM)] * (chips + 3),
-        out_specs=[pl.BlockSpec(memory_space=pltpu.VMEM)] * 3,
+            pltpu.VMEM((rows, channels), jnp.float32),
+            pltpu.VMEM((rows, 128), jnp.float32),
+            pltpu.VMEM((rows, 128), jnp.float32),
+        ]
+        + [pltpu.VMEM(array.shape, array.dtype) for array in later],
+        in_specs=[pl.BlockSpec(memory_space=pltpu.HBM)] * (chips + 8),
+        out_specs=[pl.BlockSpec(memory_space=pltpu.VMEM)] * 8,
         scratch_shapes=[
             pltpu.VMEM((rows, chips * width), jnp.bfloat16),
             pltpu.VMEM((rows, chips * width), jnp.bfloat16),
             pltpu.VMEM((chips * width, channels), jnp.bfloat16),
             pltpu.VMEM((3, chips * width), jnp.float32),
             pltpu.SemaphoreType.DMA((4, chips)),
+            pltpu.SemaphoreType.DMA((5,)),
         ],
         cost_estimate=pl.CostEstimate(
             flops=2 * rows * chips * width * channels,
             bytes_accessed=4 * rows * model + 2 * model * channels,
             transcendentals=0,
         ),
-        compiler_params=pltpu.CompilerParams(vmem_limit_bytes=VMEM_BYTES),
+        compiler_params=pltpu.CompilerParams(vmem_limit_bytes=share(rows, channels, later)),
         name="project_early",
-    )(hidden_state, mod_rows, down_weight, *pieces)
+    )(hidden_state, mod_rows, down_weight, *pieces, *later)
 
 
 def late_kernel(count, early, frames_ref, *rest):
-    sources, pieces, rest = rest[:7], rest[7 : 7 + count], rest[7 + count :]
-    out_ref, attended, held, in_sem, held_sem = rest[0], rest[1], rest[2:9], rest[9], rest[10]
+    held, pieces, (out_ref, attended, in_sem) = rest[:7], rest[7 : 7 + count], rest[7 + count :]
     acc_ref, centre_ref, square_ref, h_ref, mod_ref, weight_ref, const_ref = held
     rows, width = pieces[0].shape
     late = count * width
@@ -388,15 +402,8 @@
             pieces[step], attended.at[:, pl.ds(step * width, width)], in_sem.at[step]
         )
 
-    def hold(which):
-        return pltpu.make_async_copy(sources[which], held[which], held_sem.at[which])
-
     for step in range(count):
         load(step).start()
-    for which in (3, 4, 1, 2, 5, 0, 6):
-        hold(which).start()
-    for which in (3, 4, 1, 2):
-        hold(which).wait()
     for step in range(count):
         load(step).wait()
     wide = (
@@ -406,8 +413,6 @@
     )
     first = centre_ref[:, :1]
     scaled = ((wide - first) * (1.0 + mod_ref[1:2, :])).astype(jnp.bfloat16)
-    for which in (5, 0, 6):
-        hold(which).wait()
     total = acc_ref[...] + jnp.dot(scaled, weight_ref[...], preferred_element_type=jnp.float32)
     own = jnp.mean(wide, axis=-1, keepdims=True)
     square = jnp.sum(jnp.square(wide - own), axis=-1, keepdims=True)
@@ -420,27 +425,29 @@
     out_ref[...] = jnp.where(token < frames_ref[0] * (HH * WW), total, 0.0).astype(out_ref.dtype)
 
 
-def project_late(frames, early, consts, pieces, count, model):
+def project_late(frames, held, pieces, model, limit):
+    count = len(pieces)
     rows, width = pieces[0].shape
-    channels = consts.shape[-1]
-    hbm = pl.BlockSpec(memory_space=pltpu.HBM)
-    sources = (*early, consts)
+    channels = held[0].shape[1]
     return pl.pallas_call(
         functools.partial(late_kernel, count, model - count * width),
         out_shape=jax.ShapeDtypeStruct((rows, channels), jnp.bfloat16),
-        in_specs=[pl.BlockSpec(memory_space=pltpu.SMEM)] + [hbm] * (7 + count),
+        in_specs=[pl.BlockSpec(memory_space=pltpu.SMEM)]
+        + [pl.BlockSpec(memory_space=pltpu.VMEM)] * 7
+        + [pl.BlockSpec(memory_space=pltpu.HBM)] * count,
         out_specs=pl.BlockSpec(memory_space=pltpu.VMEM),
-        scratch_shapes=[pltpu.VMEM((rows, count * width), jnp.bfloat16)]
-        + [pltpu.VMEM(source.shape, source.dtype) for source in sources]
-        + [pltpu.SemaphoreType.DMA((count,)), pltpu.SemaphoreType.DMA((7,))],
+        scratch_shapes=[
+            pltpu.VMEM((rows, count * width), jnp.bfloat16),
+            pltpu.SemaphoreType.DMA((count,)),
+        ],
         cost_estimate=pl.CostEstimate(
             flops=2 * rows * count * width * channels,
             bytes_accessed=4 * rows * count * width,
             transcendentals=0,
         ),
-        compiler_params=pltpu.CompilerParams(vmem_limit_bytes=VMEM_BYTES),
+        compiler_params=pltpu.CompilerParams(vmem_limit_bytes=limit),
         name="project_late",
-    )(frames, *sources, *pieces)
+    )(frames, *[pltpu.with_memory_space_constraint(one, pltpu.VMEM) for one in held], *pieces)
 
 
 def gather_taps(frames, taps):
@@ -462,7 +469,7 @@
                 ] = cell[down * WW : down * WW + cells].astype(jnp.bfloat16)
 
 
-def refine_kernel(frames_ref, mid_ref, even_ref, odd_ref, weight_ref, out_ref, held, taps, weight, sem, weight_sem):
+def refine_kernel(frames_ref, mid_ref, even_ref, odd_ref, weight, out_ref, held, taps, sem):
     cells = HH * WW
     rows, _ = mid_ref.shape
     me = lax.axis_index("ctx")
@@ -482,13 +489,8 @@
         ),
     )
 
-    def fetch(ahead):
-        return pltpu.make_async_copy(weight_ref.at[ahead], weight.at[ahead], weight_sem.at[ahead])
-
     for copy in copies:
         copy.start()
-    for ahead in range(3):
-        fetch(ahead).start()
     for copy in copies:
         copy.wait()
     gather_taps(
@@ -496,7 +498,6 @@
     )
     total = held[pl.ds(cells, rows), :].astype(jnp.float32)
     for ahead in range(3):
-        fetch(ahead).wait()
         total = total + jnp.dot(
             taps[pl.ds(ahead * cells, rows), :], weight[ahead], preferred_element_type=jnp.float32
         )
@@ -504,20 +505,18 @@
     out_ref[0] = jnp.where(token < frames_ref[0] * cells, total, 0.0).astype(out_ref.dtype)
 
 
-def refine(frames, mid, even, odd, conv_weight):
+def refine(frames, mid, even, odd, taps, limit):
     rows, channels = mid.shape
-    taps = conv_weight.reshape(3, 9 * channels, channels)
     return pl.pallas_call(
         refine_kernel,
         out_shape=jax.ShapeDtypeStruct((1, rows, channels), jnp.bfloat16),
         in_specs=[pl.BlockSpec(memory_space=pltpu.SMEM)]
-        + [pl.BlockSpec(memory_space=pltpu.HBM)] * 4,
+        + [pl.BlockSpec(memory_space=pl.ANY)] * 3
+        + [pl.BlockSpec(memory_space=pltpu.VMEM)],
         out_specs=pl.BlockSpec(memory_space=pltpu.VMEM),
         scratch_shapes=[
             pltpu.VMEM((rows + 2 * HH * WW, channels), jnp.bfloat16),
             pltpu.VMEM((rows + 2 * HH * WW, 9 * channels), jnp.bfloat16),
-            pltpu.VMEM(taps.shape, taps.dtype),
-            pltpu.SemaphoreType.DMA((3,)),
             pltpu.SemaphoreType.DMA((3,)),
         ],
         cost_estimate=pl.CostEstimate(
@@ -525,9 +524,9 @@
             bytes_accessed=2 * taps.size + 6 * rows * channels,
             transcendentals=0,
         ),
-        compiler_params=pltpu.CompilerParams(vmem_limit_bytes=VMEM_BYTES),
+        compiler_params=pltpu.CompilerParams(vmem_limit_bytes=limit),
         name="refine",
-    )(frames, mid, even, odd, taps)
+    )(frames, mid, even, odd, pltpu.with_memory_space_constraint(taps, pltpu.VMEM))
 
 
 def clip_orders(sec_count):
@@ -616,15 +615,16 @@
     for chunk, heads in enumerate(chunks):
         outs = attend(own_frames, own[chunk], beside[chunk], heads)
         returned.append([outs[0]] + [send(outs[step], step, chips) for step in steps])
-    early = project_early(hidden_state, mod_rows, down_weight, returned[0])
-    projected = project_late(
-        own_frames, (*early, *tuple(ready[:3])), ready[3], returned[1], chips, model_width
-    )
+    channels = down_weight.shape[1]
+    later = (*ready, conv_weight.reshape(3, 9 * channels, channels))
+    kept = project_early(hidden_state, mod_rows, down_weight, returned[0], later)
+    limit = share(hidden_state.shape[1], channels, later)
+    projected = project_late(own_frames, kept[:7], returned[1], model_width, limit)
     mid = handoff(projected, which, source, sec_count)
     even = lax.ppermute(mid, "ctx", [(i, i ^ 1) for i in range(count)])
     joints = [(i, i + 1) for i in range(1, count - 1, 2)]
     odd = lax.ppermute(mid, "ctx", joints + [(two, one) for one, two in joints])
-    return refine(clip_length, mid, even, odd, conv_weight)
+    return refine(clip_length, mid, even, odd, kept[7], limit)
 
 
 def solution(mesh):

time: 140 us -> 136 us (0.971)
  Pallas kernels: 36.7 us -> 32.9 us
    pallas_call x1, Pallas kernels: 4.35 us -> 2.78 us  [refine(): pl.pallas_call(refine_kernel, out_shape=jax.ShapeDtypeStruct((1, rows, ch...]
where the time goes in v2:
time: 136 us
  waiting for transfers between devices  60 us (44%)
  Pallas kernels  32.9 us (24%)
  starting transfers between devices  29.4 us (22%)
  local copies, waits for them, and re-layouts  4.94 us (4%)
  between operations  4.89 us (4%)
  other arithmetic  3.46 us (3%)
    ppermute x12, waiting for transfers between devices, send(): return lax.ppermute(value, 'ctx', pairs)  52.3 us
    ppermute x12, starting transfers between devices, send(): return lax.ppermute(value, 'ctx', pairs)  16.1 us
    pallas_call x2, Pallas kernels, attend(): pl.pallas_call(functools.partial(attend_kernel, chips, heads, block_rows)...  14.6 us
    ppermute x8, starting transfers between devices, across(): return lax.ppermute(value, 'ctx', [(i, i ^ 1) for i in range(2 * chips)])  7.73 us
    pallas_call x3, Pallas kernels, pack(): pl.pallas_call(functools.partial(pack_kernel, steps, chips, kinds, head_c...  6.42 us
    ppermute x1, waiting for transfers between devices, take(): return lambda value: lax.ppermute(value, 'sec', list(enumerate(order)))  3.9 us
    ppermute x1, waiting for transfers between devices, body(): odd = lax.ppermute(mid, 'ctx', joints + [(two, one) for one, two in joints])  3.77 us
    pallas_call x1, Pallas kernels, prepare(): pl.pallas_call(functools.partial(prepare_kernel, chips, head_cols, width)...  3.57 us
  transfers between devices with their start and end apart: 23, of which 5 were waited for; matrix products, arithmetic and copies ran while one was open for 6% of the time, Pallas kernels for 19%

profile of v2, /device:TPU:15, one launch (start us, length us, event | category | flops | bytes accessed | tf_op | source)
XLA Modules:
  0.0 135.6 jit_solution(4936160217536397305)
XLA Ops:
  0.0 2.5 %pack.3 = (bf16[3,128,768]{2,1,0:T(8,128)(2,1)}, bf16[3,128,768]{2,1,0:T(8,128)(2,1)}, bf16[3,128,768]{2,1,0:T(8,128)(2,1)}) custom-call(bf16[1,128,4096]{2,1,0:T(8,128)(2,1)} %rest_0_.5, bf16[1,128,4096]{2,1,0:T(8,128)(2,1)} %rest_1_.5, bf16[1,128,4096]{2,1,0:T(8,128)(2,1)} %rest_2_.5), custom_call_target="tpu_custom_call" | custom-call | bytes 3538944 | tf_op jit(solution)/shard_map/pack/pallas_call | solution.py:86
  2.7 2.3 %collective-permute-start.16 = (bf16[3,128,768]{2,1,0:T(8,128)(2,1)}, bf16[3,128,768]{2,1,0:T(8,128)(2,1)}, u32[]{:S(2)}, u32[]{:S(2)}) collective-permute-start(bf16[3,128,768]{2,1,0:T(8,128)(2,1)} %get-tuple-element.81), channel_id=1, source_target_pairs={{0,4},{1,5},{2,6},{3,7},{4,0},{5,1},{6,2},{7,3},{8,12},{9,13},{10,... | collective-permute-start | bytes 1769480 | tf_op jit(solution)/shard_map/ppermute | solution.py:46
  5.0 2.0 %pack.4 = bf16[3,128,768]{2,1,0:T(8,128)(2,1)} custom-call(bf16[1,128,4096]{2,1,0:T(8,128)(2,1)} %rest_0_.5, bf16[1,128,4096]{2,1,0:T(8,128)(2,1)} %rest_1_.5, bf16[1,128,4096]{2,1,0:T(8,128)(2,1)} %rest_2_.5), custom_call_target="tpu_custom_call" | custom-call | bytes 1179648 | tf_op jit(solution)/shard_map/pack/pallas_call | solution.py:86
  7.2 2.0 %pack.5 = (bf16[3,128,256]{2,1,0:T(8,128)(2,1)}, bf16[3,128,256]{2,1,0:T(8,128)(2,1)}, bf16[3,128,256]{2,1,0:T(8,128)(2,1)}, bf16[3,128,256]{2,1,0:T(8,128)(2,1)}) custom-call(bf16[1,128,4096]{2,1,0:T(8,128)(2,1)} %rest_0_.5, bf16[1,128,4096]{2,1,0:T(8,128)(2,1)} %rest_1_.5, bf16[1,128,4096]{2,1,0:T(8,128)(2,1)} %rest_2_.5), custom_call_target="tpu_custom_call" | custom-call | bytes 1572864 | tf_op jit(solution)/shard_map/pack/pallas_call | solution.py:86
  9.2 1.2 collective-permute-start.25
  10.5 1.7 %collective-permute-start.18 = (bf16[3,128,768]{2,1,0:T(8,128)(2,1)}, bf16[3,128,768]{2,1,0:T(8,128)(2,1)}, u32[]{:S(2)}, u32[]{:S(2)}) collective-permute-start(bf16[3,128,768]{2,1,0:T(8,128)(2,1)} %get-tuple-element.79.rest_0_), channel_id=1, source_target_pairs={{0,1},{1,0},{2,3},{3,2},{4,5},{5,4},{6,7},{7,6},{8,9},{9,8},{10,11... | collective-permute-start | bytes 1769480 | tf_op jit(solution)/shard_map/ppermute | solution.py:50
  12.2 1.2 dynamic_slice.15
  15.3 31.3 %collective-permute-done.25.rest_1_ = bf16[3,128,256]{2,1,0:T(8,128)(2,1)S(1)} collective-permute-done((bf16[3,128,256]{2,1,0:T(8,128)(2,1)}, bf16[3,128,256]{2,1,0:T(8,128)(2,1)S(1)}, u32[]{:S(2)}, u32[]{:S(2)}) %collective-permute-start.25) | collective-permute-done | bytes 196640 | tf_op jit(solution)/shard_map/ppermute | solution.py:46
  46.7 2.1 %collective-permute-start.26 = (bf16[3,128,256]{2,1,0:T(8,128)(2,1)}, bf16[3,128,256]{2,1,0:T(8,128)(2,1)}, u32[]{:S(2)}, u32[]{:S(2)}) collective-permute-start(bf16[3,128,256]{2,1,0:T(8,128)(2,1)} %get-tuple-element.99), channel_id=1, source_target_pairs={{0,4},{1,5},{2,6},{3,7},{4,0},{5,1},{6,2},{7,3},{8,12},{9,13},{10,... | collective-permute-start | bytes 589832 | tf_op jit(solution)/shard_map/ppermute | solution.py:46
  48.8 1.8 %collective-permute-start.19 = (bf16[3,128,768]{2,1,0:T(8,128)(2,1)}, bf16[3,128,768]{2,1,0:T(8,128)(2,1)}, u32[]{:S(2)}, u32[]{:S(2)}) collective-permute-start(bf16[3,128,768]{2,1,0:T(8,128)(2,1)} %collective-permute-done.15.rest_1_), channel_id=1, source_target_pairs={{0,1},{1,0},{2,3},{3,2},{4,5},{5,4},{6,7},{7,6},{8,9},{9,8},{10,11... | collective-permute-start | bytes 1769480 | tf_op jit(solution)/shard_map/ppermute | solution.py:50
  50.7 9.6 %collective-permute-done.17.rest_3_ = bf16[3,128,768]{2,1,0:T(8,128)(2,1)} collective-permute-done((bf16[3,128,768]{2,1,0:T(8,128)(2,1)}, bf16[3,128,768]{2,1,0:T(8,128)(2,1)}, u32[]{:S(2)}, u32[]{:S(2)}) %collective-permute-start.17) | collective-permute-done | bytes 589856 | tf_op jit(solution)/shard_map/ppermute | solution.py:46
  60.2 3.1 %collective-permute-start.21 = (bf16[3,128,768]{2,1,0:T(8,128)(2,1)}, bf16[3,128,768]{2,1,0:T(8,128)(2,1)}, u32[]{:S(2)}, u32[]{:S(2)}) collective-permute-start(bf16[3,128,768]{2,1,0:T(8,128)(2,1)} %collective-permute-done.17.rest_3_), channel_id=1, source_target_pairs={{0,1},{1,0},{2,3},{3,2},{4,5},{5,4},{6,7},{7,6},{8,9},{9,8},{10,11... | collective-permute-start | bytes 1769480 | tf_op jit(solution)/shard_map/ppermute | solution.py:50
  64.4 1.4 %collective-permute-start.27 = (bf16[3,128,256]{2,1,0:T(8,128)(2,1)}, bf16[3,128,256]{2,1,0:T(8,128)(2,1)}, u32[]{:S(2)}, u32[]{:S(2)}) collective-permute-start(bf16[3,128,256]{2,1,0:T(8,128)(2,1)} %get-tuple-element.100), channel_id=1, source_target_pairs={{0,6},{1,7},{2,4},{3,5},{4,2},{5,3},{6,0},{7,1},{8,14},{9,15},{10,... | collective-permute-start | bytes 589832 | tf_op jit(solution)/shard_map/ppermute | solution.py:46
  65.8 1.4 %multiply_reduce_fusion = (s32[]{:T(128)}, s32[]{:T(128)}) fusion(s32[4]{0:T(128)} %param.35, s32[4]{0:T(128)} %constant.21.clone, s32[]{:T(128)S(6)} %axis_index.15), kind=kLoop, calls=%fused_computation.5 | loop fusion | flops 18 | bytes 44 | tf_op jit(solution)/shard_map/reduce_sum | solution.py:548
  69.9 1.4 %fusion.2 = (s32[1]{0:T(128)}, s32[1]{0:T(128)}) fusion(s32[4]{0:T(128)} %param.34, s32[]{:T(128)S(6)} %select_n.21, s32[]{:T(128)S(6)} %select_n.19), kind=kLoop, calls=%fused_computation.7 | loop fusion | bytes 24 | tf_op jit(solution)/shard_map/dynamic_slice | solution.py:606
  71.3 3.6 %prepare.1 = (bf16[128,1024]{1,0:T(8,128)(2,1)}, f32[3,1024]{1,0:T(4,128)}, bf16[1024,256]{1,0:T(8,128)(2,1)}, f32[2,8,256]{2,1,0:T(8,128)}) custom-call(bf16[1,128,4096]{2,1,0:T(8,128)(2,1)} %h_ref.3, f32[3,4096]{1,0:T(4,128)} %bitcast.6, bf16[4096,256]{1,0:T(8,128)(2,1)} %weight_ref.3), custom_call_target="tpu_custom_call" | custom-call | flops 67108864 | bytes 4194304 | tf_op jit(solution)/shard_map/prepare/pallas_call | solution.py:278
  74.9 2.1 %fusion.1 = s32[]{:T(128)} fusion(s32[15]{0:T(128)} %constant.20.clone, s32[]{:T(128)} %get-tuple-element.106), kind=kLoop, calls=%fused_computation.4 | loop fusion | flops 44 | bytes 68 | tf_op jit(solution)/shard_map/reduce_sum | solution.py:549
  78.0 9.9 %attend.2 = (bf16[128,768]{1,0:T(8,128)(2,1)}, bf16[128,768]{1,0:T(8,128)(2,1)}, bf16[128,768]{1,0:T(8,128)(2,1)}, bf16[128,768]{1,0:T(8,128)(2,1)}) custom-call(s32[1]{0:T(128)} %get-tuple-element.77.frames_ref, bf16[3,128,768]{2,1,0:T(8,128)(2,1)} %get-tuple-element.79.rest_0_, bf16[3,128,768]{2,1,0:T(8,128)(2,1)} %collective-permute-done.15.rest_1_, ...), custom_call_target="tpu_custom_call" | custom-call | flops 2415919104 | bytes 6291456 | tf_op jit(solution)/shard_map/attend/pallas_call | solution.py:192
  87.9 3.7 %collective-permute-start.22 = (bf16[128,768]{1,0:T(8,128)(2,1)}, bf16[128,768]{1,0:T(8,128)(2,1)}, u32[]{:S(2)}, u32[]{:S(2)}) collective-permute-start(bf16[128,768]{1,0:T(8,128)(2,1)} %get-tuple-element.83), channel_id=1, source_target_pairs={{0,2},{1,3},{2,0},{3,1},{4,6},{5,7},{6,4},{7,5},{8,10},{9,11},{10,... | collective-permute-start | bytes 589832 | tf_op jit(solution)/shard_map/ppermute | solution.py:46
  91.7 1.3 collective-permute-start.24
  92.9 4.7 %attend.3 = (bf16[128,256]{1,0:T(8,128)(2,1)}, bf16[128,256]{1,0:T(8,128)(2,1)}, bf16[128,256]{1,0:T(8,128)(2,1)}, bf16[128,256]{1,0:T(8,128)(2,1)}) custom-call(s32[1]{0:T(128)} %get-tuple-element.77.frames_ref, bf16[3,128,256]{2,1,0:T(8,128)(2,1)} %get-tuple-element.97.rest_0_, bf16[3,128,256]{2,1,0:T(8,128)(2,1)} %copy-done.2, ...), custom_call_target="tpu_custom_call" | custom-call | flops 805306368 | bytes 2097152 | tf_op jit(solution)/shard_map/attend/pallas_call | solution.py:192
  97.6 2.3 %collective-permute-start.32 = (bf16[128,256]{1,0:T(8,128)(2,1)}, bf16[128,256]{1,0:T(8,128)(2,1)}, u32[]{:S(2)}, u32[]{:S(2)}) collective-permute-start(bf16[128,256]{1,0:T(8,128)(2,1)} %get-tuple-element.102), channel_id=1, source_target_pairs={{0,2},{1,3},{2,0},{3,1},{4,6},{5,7},{6,4},{7,5},{8,10},{9,11},{10,... | collective-permute-start | bytes 196616 | tf_op jit(solution)/shard_map/ppermute | solution.py:46
  100.0 1.3 collective-permute-start.34
  102.0 11.4 %collective-permute-done.24.rest_3_ = bf16[128,768]{1,0:T(8,128)(2,1)} collective-permute-done((bf16[128,768]{1,0:T(8,128)(2,1)}, bf16[128,768]{1,0:T(8,128)(2,1)}, u32[]{:S(2)}, u32[]{:S(2)}) %collective-permute-start.24) | collective-permute-done | bytes 196640 | tf_op jit(solution)/shard_map/ppermute | solution.py:46
  113.3 3.5 %project_early.1 = (f32[128,256]{1,0:T(8,128)S(1)}, f32[128,128]{1,0:T(8,128)S(1)}, f32[128,128]{1,0:T(8,128)S(1)}, bf16[128,1024]{1,0:T(8,128)(2,1)S(1)}, f32[3...) custom-call(bf16[1,128,4096]{2,1,0:T(8,128)(2,1)} %h_ref.3, ...), custom_call_target="tpu_custom_call" | custom-call | flops 201326592 | bytes 4194304 | tf_op jit(solution)/shard_map/project_early/pallas_call | solution.py:365
  116.9 1.9 %project_late.1 = bf16[128,256]{1,0:T(8,128)(2,1)S(1)} custom-call(s32[1]{0:T(128)} %get-tuple-element.77.frames_ref, f32[128,256]{1,0:T(8,128)S(1)} %get-tuple-element.90.rest_0_, f32[128,128]{1,0:T(8,128)S(1)} %get-tuple-element.91.rest_1_, f32[128,128]{1,0:T(8,128)S(1)} %get-tuple-element.92.rest_2_, bf16[128,1024]{1,0:T(8,128)(2,1)S(1)} %get-tuple-element.93.rest_3_, ...), custom_call_target="tpu_custom_call" | custom-call | flops 67108864 | bytes 524288 | tf_op jit(solution)/shard_map/project_late/pallas_call | solution.py:432
  118.9 4.2 %conditional.1 = (bf16[128,256]{1,0:T(8,128)(2,1)}) conditional(s32[]{:T(128)} %clamp.3, bf16[128,256]{1,0:T(8,128)(2,1)S(1)} %project_late.1, bf16[128,256]{1,0:T(8,128)(2,1)S(1)} %project_late.1, bf16[128,256]{1,0:T(8,128)(2,1)S(1)} %project_late.1, bf16[128,256]{1,0:T(8,128)(2,1)S(1)} %project_late.1, ...), branch_computations={%region_3.4_spmd, %region_4.5_spmd, %region_5.6_spmd, %region_6.7_... | conditional | bytes 262192 | solution.py:557
  119.2 3.9 %collective-permute-done.14 = bf16[128,256]{1,0:T(8,128)(2,1)} collective-permute-done((bf16[128,256]{1,0:T(8,128)(2,1)S(1)}, bf16[128,256]{1,0:T(8,128)(2,1)}, u32[]{:S(2)}, u32[]{:S(2)}) %collective-permute-start.14) | collective-permute-done | bytes 65568 | tf_op jit(solution)/shard_map/cond/branch_14_fun/ppermute | solution.py:555
  123.1 3.3 %collective-permute-start.35 = (bf16[128,256]{1,0:T(8,128)(2,1)}, bf16[128,256]{1,0:T(8,128)(2,1)S(1)}, u32[]{:S(2)}, u32[]{:S(2)}) collective-permute-start(bf16[128,256]{1,0:T(8,128)(2,1)} %get-tuple-element.110.mid_ref), channel_id=1, source_target_pairs={{0,1},{1,0},{2,3},{3,2},{4,5},{5,4},{6,7},{7,6},{8,9},{9,8},{10,11... | collective-permute-start | bytes 196616 | tf_op jit(solution)/shard_map/ppermute | solution.py:624
  126.4 2.0 %collective-permute-start.36 = (bf16[128,256]{1,0:T(8,128)(2,1)}, bf16[128,256]{1,0:T(8,128)(2,1)S(1)}, u32[]{:S(2)}, u32[]{:S(2)}) collective-permute-start(bf16[128,256]{1,0:T(8,128)(2,1)} %get-tuple-element.110.mid_ref), channel_id=1, source_target_pairs={{1,2},{3,4},{5,6},{2,1},{4,3},{6,5},{9,10},{11,12},{13,14},{10,9},... | collective-permute-start | bytes 196616 | tf_op jit(solution)/shard_map/ppermute | solution.py:626
  128.4 3.8 %collective-permute-done.36.odd_ref = bf16[128,256]{1,0:T(8,128)(2,1)S(1)} collective-permute-done((bf16[128,256]{1,0:T(8,128)(2,1)}, bf16[128,256]{1,0:T(8,128)(2,1)S(1)}, u32[]{:S(2)}, u32[]{:S(2)}) %collective-permute-start.36) | collective-permute-done | bytes 65568 | tf_op jit(solution)/shard_map/ppermute | solution.py:626
  132.8 2.8 %refine.1 = bf16[1,128,256]{2,1,0:T(8,128)(2,1)} custom-call(s32[1]{0:T(128)} %get-tuple-element.75.frames_ref, bf16[128,256]{1,0:T(8,128)(2,1)} %get-tuple-element.110.mid_ref, bf16[128,256]{1,0:T(8,128)(2,1)} %copy-done, bf16[128,256]{1,0:T(8,128)(2,1)} %copy-done.1, bf16[3,2304,256]{2,1,0:T(8,128)(2,1)S(1)} %get-tuple-element.105.weight), custom_call_target="tpu_custom_call" | custom-call | flops 452984832 | bytes 3735552 | tf_op jit(solution)/shard_map/refine/pallas_call | solution.py:510
  (36 shorter events, 4.2 us)
Async XLA Ops:
  2.5 46.3 %collective-permute-start.15 = (bf16[3,128,768]{2,1,0:T(8,128)(2,1)}, bf16[3,128,768]{2,1,0:T(8,128)(2,1)}, u32[]{:S(2)}, u32[]{:S(2)}) collective-permute-start(bf16[3,128,768]{2,1,0:T(8,128)(2,1)} %get-tuple-element.80), channel_id=1, source_target_pairs={{0,2},{1,3},{2,0},{3,1},{4,6},{5,7},{6,4},{7,5},{8,10},{9,11},{10,... | collective-permute-start | bytes 1769480 | tf_op jit(solution)/shard_map/ppermute | solution.py:46
  2.7 47.9 %collective-permute-start.16 = (bf16[3,128,768]{2,1,0:T(8,128)(2,1)}, bf16[3,128,768]{2,1,0:T(8,128)(2,1)}, u32[]{:S(2)}, u32[]{:S(2)}) collective-permute-start(bf16[3,128,768]{2,1,0:T(8,128)(2,1)} %get-tuple-element.81), channel_id=1, source_target_pairs={{0,4},{1,5},{2,6},{3,7},{4,0},{5,1},{6,2},{7,3},{8,12},{9,13},{10,... | collective-permute-start | bytes 1769480 | tf_op jit(solution)/shard_map/ppermute | solution.py:46
  7.0 53.2 %collective-permute-start.17 = (bf16[3,128,768]{2,1,0:T(8,128)(2,1)}, bf16[3,128,768]{2,1,0:T(8,128)(2,1)}, u32[]{:S(2)}, u32[]{:S(2)}) collective-permute-start(bf16[3,128,768]{2,1,0:T(8,128)(2,1)} %pack.4), channel_id=1, source_target_pairs={{0,6},{1,7},{2,4},{3,5},{4,2},{5,3},{6,0},{7,1},{8,14},{9,15},{10,... | collective-permute-start | bytes 1769480 | tf_op jit(solution)/shard_map/ppermute | solution.py:46
  9.2 37.4 %collective-permute-start.25 = (bf16[3,128,256]{2,1,0:T(8,128)(2,1)}, bf16[3,128,256]{2,1,0:T(8,128)(2,1)S(1)}, u32[]{:S(2)}, u32[]{:S(2)}) collective-permute-start(bf16[3,128,256]{2,1,0:T(8,128)(2,1)} %get-tuple-element.98), channel_id=1, source_target_pairs={{0,2},{1,3},{2,0},{3,1},{4,6},{5,7},{6,4},{7,5},{8,10},{9,11},{10,... | collective-permute-start | bytes 589832 | tf_op jit(solution)/shard_map/ppermute | solution.py:46
  10.5 66.8 %collective-permute-start.18 = (bf16[3,128,768]{2,1,0:T(8,128)(2,1)}, bf16[3,128,768]{2,1,0:T(8,128)(2,1)}, u32[]{:S(2)}, u32[]{:S(2)}) collective-permute-start(bf16[3,128,768]{2,1,0:T(8,128)(2,1)} %get-tuple-element.79.rest_0_), channel_id=1, source_target_pairs={{0,1},{1,0},{2,3},{3,2},{4,5},{5,4},{6,7},{7,6},{8,9},{9,8},{10,11... | collective-permute-start | bytes 1769480 | tf_op jit(solution)/shard_map/ppermute | solution.py:50
  46.7 13.6 %copy-start.2 = (bf16[3,128,256]{2,1,0:T(8,128)(2,1)}, bf16[3,128,256]{2,1,0:T(8,128)(2,1)S(1)}, u32[]{:S(2)}) copy-start(bf16[3,128,256]{2,1,0:T(8,128)(2,1)S(1)} %collective-permute-done.25.rest_1_) | copy-start | bytes 589828
  46.7 17.8 %collective-permute-start.26 = (bf16[3,128,256]{2,1,0:T(8,128)(2,1)}, bf16[3,128,256]{2,1,0:T(8,128)(2,1)}, u32[]{:S(2)}, u32[]{:S(2)}) collective-permute-start(bf16[3,128,256]{2,1,0:T(8,128)(2,1)} %get-tuple-element.99), channel_id=1, source_target_pairs={{0,4},{1,5},{2,6},{3,7},{4,0},{5,1},{6,2},{7,3},{8,12},{9,13},{10,... | collective-permute-start | bytes 589832 | tf_op jit(solution)/shard_map/ppermute | solution.py:46
  48.8 28.7 %collective-permute-start.19 = (bf16[3,128,768]{2,1,0:T(8,128)(2,1)}, bf16[3,128,768]{2,1,0:T(8,128)(2,1)}, u32[]{:S(2)}, u32[]{:S(2)}) collective-permute-start(bf16[3,128,768]{2,1,0:T(8,128)(2,1)} %collective-permute-done.15.rest_1_), channel_id=1, source_target_pairs={{0,1},{1,0},{2,3},{3,2},{4,5},{5,4},{6,7},{7,6},{8,9},{9,8},{10,11... | collective-permute-start | bytes 1769480 | tf_op jit(solution)/shard_map/ppermute | solution.py:50
  50.6 27.2 %collective-permute-start.20 = (bf16[3,128,768]{2,1,0:T(8,128)(2,1)}, bf16[3,128,768]{2,1,0:T(8,128)(2,1)}, u32[]{:S(2)}, u32[]{:S(2)}) collective-permute-start(bf16[3,128,768]{2,1,0:T(8,128)(2,1)} %collective-permute-done.16.rest_2_), channel_id=1, source_target_pairs={{0,1},{1,0},{2,3},{3,2},{4,5},{5,4},{6,7},{7,6},{8,9},{9,8},{10,11... | collective-permute-start | bytes 1769480 | tf_op jit(solution)/shard_map/ppermute | solution.py:50
  60.2 17.7 %collective-permute-start.21 = (bf16[3,128,768]{2,1,0:T(8,128)(2,1)}, bf16[3,128,768]{2,1,0:T(8,128)(2,1)}, u32[]{:S(2)}, u32[]{:S(2)}) collective-permute-start(bf16[3,128,768]{2,1,0:T(8,128)(2,1)} %collective-permute-done.17.rest_3_), channel_id=1, source_target_pairs={{0,1},{1,0},{2,3},{3,2},{4,5},{5,4},{6,7},{7,6},{8,9},{9,8},{10,11... | collective-permute-start | bytes 1769480 | tf_op jit(solution)/shard_map/ppermute | solution.py:50
  64.4 12.5 %collective-permute-start.27 = (bf16[3,128,256]{2,1,0:T(8,128)(2,1)}, bf16[3,128,256]{2,1,0:T(8,128)(2,1)}, u32[]{:S(2)}, u32[]{:S(2)}) collective-permute-start(bf16[3,128,256]{2,1,0:T(8,128)(2,1)} %get-tuple-element.100), channel_id=1, source_target_pairs={{0,6},{1,7},{2,4},{3,5},{4,2},{5,3},{6,0},{7,1},{8,14},{9,15},{10,... | collective-permute-start | bytes 589832 | tf_op jit(solution)/shard_map/ppermute | solution.py:46
  76.9 14.7 %collective-permute-start.28 = (bf16[3,128,256]{2,1,0:T(8,128)(2,1)}, bf16[3,128,256]{2,1,0:T(8,128)(2,1)}, u32[]{:S(2)}, u32[]{:S(2)}) collective-permute-start(bf16[3,128,256]{2,1,0:T(8,128)(2,1)} %get-tuple-element.97.rest_0_), channel_id=1, source_target_pairs={{0,1},{1,0},{2,3},{3,2},{4,5},{5,4},{6,7},{7,6},{8,9},{9,8},{10,11... | collective-permute-start | bytes 589832 | tf_op jit(solution)/shard_map/ppermute | solution.py:50
  77.2 14.4 %collective-permute-start.29 = (bf16[3,128,256]{2,1,0:T(8,128)(2,1)}, bf16[3,128,256]{2,1,0:T(8,128)(2,1)}, u32[]{:S(2)}, u32[]{:S(2)}) collective-permute-start(bf16[3,128,256]{2,1,0:T(8,128)(2,1)} %copy-done.2), channel_id=1, source_target_pairs={{0,1},{1,0},{2,3},{3,2},{4,5},{5,4},{6,7},{7,6},{8,9},{9,8},{10,11... | collective-permute-start | bytes 589832 | tf_op jit(solution)/shard_map/ppermute | solution.py:50
  77.5 15.5 %collective-permute-start.30 = (bf16[3,128,256]{2,1,0:T(8,128)(2,1)}, bf16[3,128,256]{2,1,0:T(8,128)(2,1)}, u32[]{:S(2)}, u32[]{:S(2)}) collective-permute-start(bf16[3,128,256]{2,1,0:T(8,128)(2,1)} %collective-permute-done.26.rest_2_), channel_id=1, source_target_pairs={{0,1},{1,0},{2,3},{3,2},{4,5},{5,4},{6,7},{7,6},{8,9},{9,8},{10,11... | collective-permute-start | bytes 589832 | tf_op jit(solution)/shard_map/ppermute | solution.py:50
  77.8 15.2 %collective-permute-start.31 = (bf16[3,128,256]{2,1,0:T(8,128)(2,1)}, bf16[3,128,256]{2,1,0:T(8,128)(2,1)}, u32[]{:S(2)}, u32[]{:S(2)}) collective-permute-start(bf16[3,128,256]{2,1,0:T(8,128)(2,1)} %collective-permute-done.27.rest_3_), channel_id=1, source_target_pairs={{0,1},{1,0},{2,3},{3,2},{4,5},{5,4},{6,7},{7,6},{8,9},{9,8},{10,11... | collective-permute-start | bytes 589832 | tf_op jit(solution)/shard_map/ppermute | solution.py:50
  87.9 12.1 %collective-permute-start.22 = (bf16[128,768]{1,0:T(8,128)(2,1)}, bf16[128,768]{1,0:T(8,128)(2,1)}, u32[]{:S(2)}, u32[]{:S(2)}) collective-permute-start(bf16[128,768]{1,0:T(8,128)(2,1)} %get-tuple-element.83), channel_id=1, source_target_pairs={{0,2},{1,3},{2,0},{3,1},{4,6},{5,7},{6,4},{7,5},{8,10},{9,11},{10,... | collective-permute-start | bytes 589832 | tf_op jit(solution)/shard_map/ppermute | solution.py:46
  91.6 10.3 %collective-permute-start.23 = (bf16[128,768]{1,0:T(8,128)(2,1)}, bf16[128,768]{1,0:T(8,128)(2,1)}, u32[]{:S(2)}, u32[]{:S(2)}) collective-permute-start(bf16[128,768]{1,0:T(8,128)(2,1)} %get-tuple-element.84), channel_id=1, source_target_pairs={{0,4},{1,5},{2,6},{3,7},{4,0},{5,1},{6,2},{7,3},{8,12},{9,13},{10,... | collective-permute-start | bytes 589832 | tf_op jit(solution)/shard_map/ppermute | solution.py:46
  91.7 21.7 %collective-permute-start.24 = (bf16[128,768]{1,0:T(8,128)(2,1)}, bf16[128,768]{1,0:T(8,128)(2,1)}, u32[]{:S(2)}, u32[]{:S(2)}) collective-permute-start(bf16[128,768]{1,0:T(8,128)(2,1)} %get-tuple-element.85), channel_id=1, source_target_pairs={{0,6},{1,7},{2,4},{3,5},{4,2},{5,3},{6,0},{7,1},{8,14},{9,15},{10,... | collective-permute-start | bytes 589832 | tf_op jit(solution)/shard_map/ppermute | solution.py:46
  97.6 19.2 %collective-permute-start.32 = (bf16[128,256]{1,0:T(8,128)(2,1)}, bf16[128,256]{1,0:T(8,128)(2,1)}, u32[]{:S(2)}, u32[]{:S(2)}) collective-permute-start(bf16[128,256]{1,0:T(8,128)(2,1)} %get-tuple-element.102), channel_id=1, source_target_pairs={{0,2},{1,3},{2,0},{3,1},{4,6},{5,7},{6,4},{7,5},{8,10},{9,11},{10,... | collective-permute-start | bytes 196616 | tf_op jit(solution)/shard_map/ppermute | solution.py:46
  100.0 16.9 %collective-permute-start.33 = (bf16[128,256]{1,0:T(8,128)(2,1)}, bf16[128,256]{1,0:T(8,128)(2,1)}, u32[]{:S(2)}, u32[]{:S(2)}) collective-permute-start(bf16[128,256]{1,0:T(8,128)(2,1)} %get-tuple-element.103), channel_id=1, source_target_pairs={{0,4},{1,5},{2,6},{3,7},{4,0},{5,1},{6,2},{7,3},{8,12},{9,13},{10,... | collective-permute-start | bytes 196616 | tf_op jit(solution)/shard_map/ppermute | solution.py:46
  100.0 16.9 %collective-permute-start.34 = (bf16[128,256]{1,0:T(8,128)(2,1)}, bf16[128,256]{1,0:T(8,128)(2,1)}, u32[]{:S(2)}, u32[]{:S(2)}) collective-permute-start(bf16[128,256]{1,0:T(8,128)(2,1)} %get-tuple-element.104), channel_id=1, source_target_pairs={{0,6},{1,7},{2,4},{3,5},{4,2},{5,3},{6,0},{7,1},{8,14},{9,15},{10,... | collective-permute-start | bytes 196616 | tf_op jit(solution)/shard_map/ppermute | solution.py:46
  118.9 4.2 %collective-permute-start.14 = (bf16[128,256]{1,0:T(8,128)(2,1)S(1)}, bf16[128,256]{1,0:T(8,128)(2,1)}, u32[]{:S(2)}, u32[]{:S(2)}) collective-permute-start(bf16[128,256]{1,0:T(8,128)(2,1)S(1)} %param.14), channel_id=1, source_target_pairs={{0,24},{8,16},{16,0},{24,8},{1,25},{9,17},{17,1},{25,9},{2,26},{10... | collective-permute-start | bytes 196616 | tf_op jit(solution)/shard_map/cond/branch_14_fun/ppermute | solution.py:555
  123.1 5.3 %collective-permute-start.35 = (bf16[128,256]{1,0:T(8,128)(2,1)}, bf16[128,256]{1,0:T(8,128)(2,1)S(1)}, u32[]{:S(2)}, u32[]{:S(2)}) collective-permute-start(bf16[128,256]{1,0:T(8,128)(2,1)} %get-tuple-element.110.mid_ref), channel_id=1, source_target_pairs={{0,1},{1,0},{2,3},{3,2},{4,5},{5,4},{6,7},{7,6},{8,9},{9,8},{10,11... | collective-permute-start | bytes 196616 | tf_op jit(solution)/shard_map/ppermute | solution.py:624
  126.4 5.8 %collective-permute-start.36 = (bf16[128,256]{1,0:T(8,128)(2,1)}, bf16[128,256]{1,0:T(8,128)(2,1)S(1)}, u32[]{:S(2)}, u32[]{:S(2)}) collective-permute-start(bf16[128,256]{1,0:T(8,128)(2,1)} %get-tuple-element.110.mid_ref), channel_id=1, source_target_pairs={{1,2},{3,4},{5,6},{2,1},{4,3},{6,5},{9,10},{11,12},{13,14},{10,9},... | collective-permute-start | bytes 196616 | tf_op jit(solution)/shard_map/ppermute | solution.py:626
  128.4 3.8 %copy-start = (bf16[128,256]{1,0:T(8,128)(2,1)}, bf16[128,256]{1,0:T(8,128)(2,1)S(1)}, u32[]{:S(2)}) copy-start(bf16[128,256]{1,0:T(8,128)(2,1)S(1)} %collective-permute-done.35.even_ref) | copy-start | bytes 196612
  132.2 0.6 copy-start.1

commit v3 on v2

--- a/solution.py
+++ b/solution.py
@@ -36,7 +36,7 @@
 
 def far_first(chips):
     far = list(range(chips - 1, max(chips // 2, 1) - 1, -1))
-    return far + list(range(chips // 2 - 1, 0, -1)), far[-1]
+    return far + list(range(chips // 2 - 1, 0, -1))
 
 
 def send(value, step, chips):
@@ -591,7 +591,7 @@
     own, beside = [], []
     for chunk, width in enumerate(widths):
         packed = [None] * chips
-        order = far_first(chips)[0]
+        order = far_first(chips)
         for batch in (order[:1], order[1:] + [0]) if chunk == 0 else (order + [0],):
             pieces = pack(tensors, batch, chips, head_cols, sum(widths[:chunk]), width)
             for step, piece in zip(batch, pieces):
@@ -624,7 +624,7 @@
     even = lax.ppermute(mid, "ctx", [(i, i ^ 1) for i in range(count)])
     joints = [(i, i + 1) for i in range(1, count - 1, 2)]
     odd = lax.ppermute(mid, "ctx", joints + [(two, one) for one, two in joints])
-    return refine(clip_length, mid, even, odd, kept[7], limit)
+    return refine(clip_length, mid, even, odd, kept[7], limit - 4 * SPARE_BYTES)
 
 
 def solution(mesh):

time: 136 us -> 136 us (level)
  no operation moved by 1% of the time
where the time goes in v3:
time: 136 us
  waiting for transfers between devices  60 us (44%)
  Pallas kernels  32.9 us (24%)
  starting transfers between devices  29.4 us (22%)
  local copies, waits for them, and re-layouts  4.94 us (4%)
  between operations  4.89 us (4%)
  other arithmetic  3.46 us (3%)
    ppermute x12, waiting for transfers between devices, send(): return lax.ppermute(value, 'ctx', pairs)  52.3 us
    ppermute x12, starting transfers between devices, send(): return lax.ppermute(value, 'ctx', pairs)  16.1 us
    pallas_call x2, Pallas kernels, attend(): pl.pallas_call(functools.partial(attend_kernel, chips, heads, block_rows)...  14.6 us
    ppermute x8, starting transfers between devices, across(): return lax.ppermute(value, 'ctx', [(i, i ^ 1) for i in range(2 * chips)])  7.73 us
    pallas_call x3, Pallas kernels, pack(): pl.pallas_call(functools.partial(pack_kernel, steps, chips, kinds, head_c...  6.42 us
    ppermute x1, waiting for transfers between devices, take(): return lambda value: lax.ppermute(value, 'sec', list(enumerate(order)))  3.9 us
    ppermute x1, waiting for transfers between devices, body(): odd = lax.ppermute(mid, 'ctx', joints + [(two, one) for one, two in joints])  3.77 us
    pallas_call x1, Pallas kernels, prepare(): pl.pallas_call(functools.partial(prepare_kernel, chips, head_cols, width)...  3.57 us
  transfers between devices with their start and end apart: 23, of which 5 were waited for; matrix products, arithmetic and copies ran while one was open for 6% of the time, Pallas kernels for 19%

profile of v3, /device:TPU:15, one launch (start us, length us, event | category | flops | bytes accessed | tf_op | source)
XLA Modules:
  0.0 135.6 jit_solution(3335973207272287454)
XLA Ops:
  0.0 2.5 %pack.3 = (bf16[3,128,768]{2,1,0:T(8,128)(2,1)}, bf16[3,128,768]{2,1,0:T(8,128)(2,1)}, bf16[3,128,768]{2,1,0:T(8,128)(2,1)}) custom-call(bf16[1,128,4096]{2,1,0:T(8,128)(2,1)} %rest_0_.5, bf16[1,128,4096]{2,1,0:T(8,128)(2,1)} %rest_1_.5, bf16[1,128,4096]{2,1,0:T(8,128)(2,1)} %rest_2_.5), custom_call_target="tpu_custom_call" | custom-call | bytes 3538944 | tf_op jit(solution)/shard_map/pack/pallas_call | solution.py:86
  2.7 2.3 %collective-permute-start.16 = (bf16[3,128,768]{2,1,0:T(8,128)(2,1)}, bf16[3,128,768]{2,1,0:T(8,128)(2,1)}, u32[]{:S(2)}, u32[]{:S(2)}) collective-permute-start(bf16[3,128,768]{2,1,0:T(8,128)(2,1)} %get-tuple-element.81), channel_id=1, source_target_pairs={{0,4},{1,5},{2,6},{3,7},{4,0},{5,1},{6,2},{7,3},{8,12},{9,13},{10,... | collective-permute-start | bytes 1769480 | tf_op jit(solution)/shard_map/ppermute | solution.py:46
  5.0 2.0 %pack.4 = bf16[3,128,768]{2,1,0:T(8,128)(2,1)} custom-call(bf16[1,128,4096]{2,1,0:T(8,128)(2,1)} %rest_0_.5, bf16[1,128,4096]{2,1,0:T(8,128)(2,1)} %rest_1_.5, bf16[1,128,4096]{2,1,0:T(8,128)(2,1)} %rest_2_.5), custom_call_target="tpu_custom_call" | custom-call | bytes 1179648 | tf_op jit(solution)/shard_map/pack/pallas_call | solution.py:86
  7.2 2.0 %pack.5 = (bf16[3,128,256]{2,1,0:T(8,128)(2,1)}, bf16[3,128,256]{2,1,0:T(8,128)(2,1)}, bf16[3,128,256]{2,1,0:T(8,128)(2,1)}, bf16[3,128,256]{2,1,0:T(8,128)(2,1)}) custom-call(bf16[1,128,4096]{2,1,0:T(8,128)(2,1)} %rest_0_.5, bf16[1,128,4096]{2,1,0:T(8,128)(2,1)} %rest_1_.5, bf16[1,128,4096]{2,1,0:T(8,128)(2,1)} %rest_2_.5), custom_call_target="tpu_custom_call" | custom-call | bytes 1572864 | tf_op jit(solution)/shard_map/pack/pallas_call | solution.py:86
  9.2 1.2 collective-permute-start.25
  10.5 1.7 %collective-permute-start.18 = (bf16[3,128,768]{2,1,0:T(8,128)(2,1)}, bf16[3,128,768]{2,1,0:T(8,128)(2,1)}, u32[]{:S(2)}, u32[]{:S(2)}) collective-permute-start(bf16[3,128,768]{2,1,0:T(8,128)(2,1)} %get-tuple-element.79.rest_0_), channel_id=1, source_target_pairs={{0,1},{1,0},{2,3},{3,2},{4,5},{5,4},{6,7},{7,6},{8,9},{9,8},{10,11... | collective-permute-start | bytes 1769480 | tf_op jit(solution)/shard_map/ppermute | solution.py:50
  12.2 1.2 dynamic_slice.15
  15.3 31.3 %collective-permute-done.25.rest_1_ = bf16[3,128,256]{2,1,0:T(8,128)(2,1)S(1)} collective-permute-done((bf16[3,128,256]{2,1,0:T(8,128)(2,1)}, bf16[3,128,256]{2,1,0:T(8,128)(2,1)S(1)}, u32[]{:S(2)}, u32[]{:S(2)}) %collective-permute-start.25) | collective-permute-done | bytes 196640 | tf_op jit(solution)/shard_map/ppermute | solution.py:46
  46.7 2.1 %collective-permute-start.26 = (bf16[3,128,256]{2,1,0:T(8,128)(2,1)}, bf16[3,128,256]{2,1,0:T(8,128)(2,1)}, u32[]{:S(2)}, u32[]{:S(2)}) collective-permute-start(bf16[3,128,256]{2,1,0:T(8,128)(2,1)} %get-tuple-element.99), channel_id=1, source_target_pairs={{0,4},{1,5},{2,6},{3,7},{4,0},{5,1},{6,2},{7,3},{8,12},{9,13},{10,... | collective-permute-start | bytes 589832 | tf_op jit(solution)/shard_map/ppermute | solution.py:46
  48.8 1.8 %collective-permute-start.19 = (bf16[3,128,768]{2,1,0:T(8,128)(2,1)}, bf16[3,128,768]{2,1,0:T(8,128)(2,1)}, u32[]{:S(2)}, u32[]{:S(2)}) collective-permute-start(bf16[3,128,768]{2,1,0:T(8,128)(2,1)} %collective-permute-done.15.rest_1_), channel_id=1, source_target_pairs={{0,1},{1,0},{2,3},{3,2},{4,5},{5,4},{6,7},{7,6},{8,9},{9,8},{10,11... | collective-permute-start | bytes 1769480 | tf_op jit(solution)/shard_map/ppermute | solution.py:50
  50.7 9.6 %collective-permute-done.17.rest_3_ = bf16[3,128,768]{2,1,0:T(8,128)(2,1)} collective-permute-done((bf16[3,128,768]{2,1,0:T(8,128)(2,1)}, bf16[3,128,768]{2,1,0:T(8,128)(2,1)}, u32[]{:S(2)}, u32[]{:S(2)}) %collective-permute-start.17) | collective-permute-done | bytes 589856 | tf_op jit(solution)/shard_map/ppermute | solution.py:46
  60.2 3.1 %collective-permute-start.21 = (bf16[3,128,768]{2,1,0:T(8,128)(2,1)}, bf16[3,128,768]{2,1,0:T(8,128)(2,1)}, u32[]{:S(2)}, u32[]{:S(2)}) collective-permute-start(bf16[3,128,768]{2,1,0:T(8,128)(2,1)} %collective-permute-done.17.rest_3_), channel_id=1, source_target_pairs={{0,1},{1,0},{2,3},{3,2},{4,5},{5,4},{6,7},{7,6},{8,9},{9,8},{10,11... | collective-permute-start | bytes 1769480 | tf_op jit(solution)/shard_map/ppermute | solution.py:50
  64.4 1.4 %collective-permute-start.27 = (bf16[3,128,256]{2,1,0:T(8,128)(2,1)}, bf16[3,128,256]{2,1,0:T(8,128)(2,1)}, u32[]{:S(2)}, u32[]{:S(2)}) collective-permute-start(bf16[3,128,256]{2,1,0:T(8,128)(2,1)} %get-tuple-element.100), channel_id=1, source_target_pairs={{0,6},{1,7},{2,4},{3,5},{4,2},{5,3},{6,0},{7,1},{8,14},{9,15},{10,... | collective-permute-start | bytes 589832 | tf_op jit(solution)/shard_map/ppermute | solution.py:46
  65.8 1.4 %multiply_reduce_fusion = (s32[]{:T(128)}, s32[]{:T(128)}) fusion(s32[4]{0:T(128)} %param.35, s32[4]{0:T(128)} %constant.21.clone, s32[]{:T(128)S(6)} %axis_index.15), kind=kLoop, calls=%fused_computation.5 | loop fusion | flops 18 | bytes 44 | tf_op jit(solution)/shard_map/reduce_sum | solution.py:548
  69.9 1.4 %fusion.2 = (s32[1]{0:T(128)}, s32[1]{0:T(128)}) fusion(s32[4]{0:T(128)} %param.34, s32[]{:T(128)S(6)} %select_n.21, s32[]{:T(128)S(6)} %select_n.19), kind=kLoop, calls=%fused_computation.7 | loop fusion | bytes 24 | tf_op jit(solution)/shard_map/dynamic_slice | solution.py:606
  71.3 3.6 %prepare.1 = (bf16[128,1024]{1,0:T(8,128)(2,1)}, f32[3,1024]{1,0:T(4,128)}, bf16[1024,256]{1,0:T(8,128)(2,1)}, f32[2,8,256]{2,1,0:T(8,128)}) custom-call(bf16[1,128,4096]{2,1,0:T(8,128)(2,1)} %h_ref.3, f32[3,4096]{1,0:T(4,128)} %bitcast.6, bf16[4096,256]{1,0:T(8,128)(2,1)} %weight_ref.3), custom_call_target="tpu_custom_call" | custom-call | flops 67108864 | bytes 4194304 | tf_op jit(solution)/shard_map/prepare/pallas_call | solution.py:278
  74.9 2.1 %fusion.1 = s32[]{:T(128)} fusion(s32[15]{0:T(128)} %constant.20.clone, s32[]{:T(128)} %get-tuple-element.106), kind=kLoop, calls=%fused_computation.4 | loop fusion | flops 44 | bytes 68 | tf_op jit(solution)/shard_map/reduce_sum | solution.py:549
  78.0 9.9 %attend.2 = (bf16[128,768]{1,0:T(8,128)(2,1)}, bf16[128,768]{1,0:T(8,128)(2,1)}, bf16[128,768]{1,0:T(8,128)(2,1)}, bf16[128,768]{1,0:T(8,128)(2,1)}) custom-call(s32[1]{0:T(128)} %get-tuple-element.77.frames_ref, bf16[3,128,768]{2,1,0:T(8,128)(2,1)} %get-tuple-element.79.rest_0_, bf16[3,128,768]{2,1,0:T(8,128)(2,1)} %collective-permute-done.15.rest_1_, ...), custom_call_target="tpu_custom_call" | custom-call | flops 2415919104 | bytes 6291456 | tf_op jit(solution)/shard_map/attend/pallas_call | solution.py:192
  87.9 3.7 %collective-permute-start.22 = (bf16[128,768]{1,0:T(8,128)(2,1)}, bf16[128,768]{1,0:T(8,128)(2,1)}, u32[]{:S(2)}, u32[]{:S(2)}) collective-permute-start(bf16[128,768]{1,0:T(8,128)(2,1)} %get-tuple-element.83), channel_id=1, source_target_pairs={{0,2},{1,3},{2,0},{3,1},{4,6},{5,7},{6,4},{7,5},{8,10},{9,11},{10,... | collective-permute-start | bytes 589832 | tf_op jit(solution)/shard_map/ppermute | solution.py:46
  91.7 1.3 collective-permute-start.24
  92.9 4.7 %attend.3 = (bf16[128,256]{1,0:T(8,128)(2,1)}, bf16[128,256]{1,0:T(8,128)(2,1)}, bf16[128,256]{1,0:T(8,128)(2,1)}, bf16[128,256]{1,0:T(8,128)(2,1)}) custom-call(s32[1]{0:T(128)} %get-tuple-element.77.frames_ref, bf16[3,128,256]{2,1,0:T(8,128)(2,1)} %get-tuple-element.97.rest_0_, bf16[3,128,256]{2,1,0:T(8,128)(2,1)} %copy-done.2, ...), custom_call_target="tpu_custom_call" | custom-call | flops 805306368 | bytes 2097152 | tf_op jit(solution)/shard_map/attend/pallas_call | solution.py:192
  97.6 2.3 %collective-permute-start.32 = (bf16[128,256]{1,0:T(8,128)(2,1)}, bf16[128,256]{1,0:T(8,128)(2,1)}, u32[]{:S(2)}, u32[]{:S(2)}) collective-permute-start(bf16[128,256]{1,0:T(8,128)(2,1)} %get-tuple-element.102), channel_id=1, source_target_pairs={{0,2},{1,3},{2,0},{3,1},{4,6},{5,7},{6,4},{7,5},{8,10},{9,11},{10,... | collective-permute-start | bytes 196616 | tf_op jit(solution)/shard_map/ppermute | solution.py:46
  100.0 1.3 collective-permute-start.34
  102.0 11.4 %collective-permute-done.24.rest_3_ = bf16[128,768]{1,0:T(8,128)(2,1)} collective-permute-done((bf16[128,768]{1,0:T(8,128)(2,1)}, bf16[128,768]{1,0:T(8,128)(2,1)}, u32[]{:S(2)}, u32[]{:S(2)}) %collective-permute-start.24) | collective-permute-done | bytes 196640 | tf_op jit(solution)/shard_map/ppermute | solution.py:46
  113.3 3.5 %project_early.1 = (f32[128,256]{1,0:T(8,128)S(1)}, f32[128,128]{1,0:T(8,128)S(1)}, f32[128,128]{1,0:T(8,128)S(1)}, bf16[128,1024]{1,0:T(8,128)(2,1)S(1)}, f32[3...) custom-call(bf16[1,128,4096]{2,1,0:T(8,128)(2,1)} %h_ref.3, ...), custom_call_target="tpu_custom_call" | custom-call | flops 201326592 | bytes 4194304 | tf_op jit(solution)/shard_map/project_early/pallas_call | solution.py:365
  116.9 1.9 %project_late.1 = bf16[128,256]{1,0:T(8,128)(2,1)S(1)} custom-call(s32[1]{0:T(128)} %get-tuple-element.77.frames_ref, f32[128,256]{1,0:T(8,128)S(1)} %get-tuple-element.90.rest_0_, f32[128,128]{1,0:T(8,128)S(1)} %get-tuple-element.91.rest_1_, f32[128,128]{1,0:T(8,128)S(1)} %get-tuple-element.92.rest_2_, bf16[128,1024]{1,0:T(8,128)(2,1)S(1)} %get-tuple-element.93.rest_3_, ...), custom_call_target="tpu_custom_call" | custom-call | flops 67108864 | bytes 524288 | tf_op jit(solution)/shard_map/project_late/pallas_call | solution.py:432
  118.9 4.2 %conditional.1 = (bf16[128,256]{1,0:T(8,128)(2,1)}) conditional(s32[]{:T(128)} %clamp.3, bf16[128,256]{1,0:T(8,128)(2,1)S(1)} %project_late.1, bf16[128,256]{1,0:T(8,128)(2,1)S(1)} %project_late.1, bf16[128,256]{1,0:T(8,128)(2,1)S(1)} %project_late.1, bf16[128,256]{1,0:T(8,128)(2,1)S(1)} %project_late.1, ...), branch_computations={%region_3.4_spmd, %region_4.5_spmd, %region_5.6_spmd, %region_6.7_... | conditional | bytes 262192 | solution.py:557
  119.2 3.9 %collective-permute-done.14 = bf16[128,256]{1,0:T(8,128)(2,1)} collective-permute-done((bf16[128,256]{1,0:T(8,128)(2,1)S(1)}, bf16[128,256]{1,0:T(8,128)(2,1)}, u32[]{:S(2)}, u32[]{:S(2)}) %collective-permute-start.14) | collective-permute-done | bytes 65568 | tf_op jit(solution)/shard_map/cond/branch_14_fun/ppermute | solution.py:555
  123.1 3.3 %collective-permute-start.35 = (bf16[128,256]{1,0:T(8,128)(2,1)}, bf16[128,256]{1,0:T(8,128)(2,1)S(1)}, u32[]{:S(2)}, u32[]{:S(2)}) collective-permute-start(bf16[128,256]{1,0:T(8,128)(2,1)} %get-tuple-element.110.mid_ref), channel_id=1, source_target_pairs={{0,1},{1,0},{2,3},{3,2},{4,5},{5,4},{6,7},{7,6},{8,9},{9,8},{10,11... | collective-permute-start | bytes 196616 | tf_op jit(solution)/shard_map/ppermute | solution.py:624
  126.4 2.0 %collective-permute-start.36 = (bf16[128,256]{1,0:T(8,128)(2,1)}, bf16[128,256]{1,0:T(8,128)(2,1)S(1)}, u32[]{:S(2)}, u32[]{:S(2)}) collective-permute-start(bf16[128,256]{1,0:T(8,128)(2,1)} %get-tuple-element.110.mid_ref), channel_id=1, source_target_pairs={{1,2},{3,4},{5,6},{2,1},{4,3},{6,5},{9,10},{11,12},{13,14},{10,9},... | collective-permute-start | bytes 196616 | tf_op jit(solution)/shard_map/ppermute | solution.py:626
  128.4 3.8 %collective-permute-done.36.odd_ref = bf16[128,256]{1,0:T(8,128)(2,1)S(1)} collective-permute-done((bf16[128,256]{1,0:T(8,128)(2,1)}, bf16[128,256]{1,0:T(8,128)(2,1)S(1)}, u32[]{:S(2)}, u32[]{:S(2)}) %collective-permute-start.36) | collective-permute-done | bytes 65568 | tf_op jit(solution)/shard_map/ppermute | solution.py:626
  132.8 2.8 %refine.1 = bf16[1,128,256]{2,1,0:T(8,128)(2,1)} custom-call(s32[1]{0:T(128)} %get-tuple-element.75.frames_ref, bf16[128,256]{1,0:T(8,128)(2,1)} %get-tuple-element.110.mid_ref, bf16[128,256]{1,0:T(8,128)(2,1)} %copy-done, bf16[128,256]{1,0:T(8,128)(2,1)} %copy-done.1, bf16[3,2304,256]{2,1,0:T(8,128)(2,1)S(1)} %get-tuple-element.105.weight), custom_call_target="tpu_custom_call" | custom-call | flops 452984832 | bytes 3735552 | tf_op jit(solution)/shard_map/refine/pallas_call | solution.py:510
  (36 shorter events, 4.2 us)
Async XLA Ops:
  2.5 46.3 %collective-permute-start.15 = (bf16[3,128,768]{2,1,0:T(8,128)(2,1)}, bf16[3,128,768]{2,1,0:T(8,128)(2,1)}, u32[]{:S(2)}, u32[]{:S(2)}) collective-permute-start(bf16[3,128,768]{2,1,0:T(8,128)(2,1)} %get-tuple-element.80), channel_id=1, source_target_pairs={{0,2},{1,3},{2,0},{3,1},{4,6},{5,7},{6,4},{7,5},{8,10},{9,11},{10,... | collective-permute-start | bytes 1769480 | tf_op jit(solution)/shard_map/ppermute | solution.py:46
  2.7 47.9 %collective-permute-start.16 = (bf16[3,128,768]{2,1,0:T(8,128)(2,1)}, bf16[3,128,768]{2,1,0:T(8,128)(2,1)}, u32[]{:S(2)}, u32[]{:S(2)}) collective-permute-start(bf16[3,128,768]{2,1,0:T(8,128)(2,1)} %get-tuple-element.81), channel_id=1, source_target_pairs={{0,4},{1,5},{2,6},{3,7},{4,0},{5,1},{6,2},{7,3},{8,12},{9,13},{10,... | collective-permute-start | bytes 1769480 | tf_op jit(solution)/shard_map/ppermute | solution.py:46
  7.0 53.2 %collective-permute-start.17 = (bf16[3,128,768]{2,1,0:T(8,128)(2,1)}, bf16[3,128,768]{2,1,0:T(8,128)(2,1)}, u32[]{:S(2)}, u32[]{:S(2)}) collective-permute-start(bf16[3,128,768]{2,1,0:T(8,128)(2,1)} %pack.4), channel_id=1, source_target_pairs={{0,6},{1,7},{2,4},{3,5},{4,2},{5,3},{6,0},{7,1},{8,14},{9,15},{10,... | collective-permute-start | bytes 1769480 | tf_op jit(solution)/shard_map/ppermute | solution.py:46
  9.2 37.4 %collective-permute-start.25 = (bf16[3,128,256]{2,1,0:T(8,128)(2,1)}, bf16[3,128,256]{2,1,0:T(8,128)(2,1)S(1)}, u32[]{:S(2)}, u32[]{:S(2)}) collective-permute-start(bf16[3,128,256]{2,1,0:T(8,128)(2,1)} %get-tuple-element.98), channel_id=1, source_target_pairs={{0,2},{1,3},{2,0},{3,1},{4,6},{5,7},{6,4},{7,5},{8,10},{9,11},{10,... | collective-permute-start | bytes 589832 | tf_op jit(solution)/shard_map/ppermute | solution.py:46
  10.5 66.8 %collective-permute-start.18 = (bf16[3,128,768]{2,1,0:T(8,128)(2,1)}, bf16[3,128,768]{2,1,0:T(8,128)(2,1)}, u32[]{:S(2)}, u32[]{:S(2)}) collective-permute-start(bf16[3,128,768]{2,1,0:T(8,128)(2,1)} %get-tuple-element.79.rest_0_), channel_id=1, source_target_pairs={{0,1},{1,0},{2,3},{3,2},{4,5},{5,4},{6,7},{7,6},{8,9},{9,8},{10,11... | collective-permute-start | bytes 1769480 | tf_op jit(solution)/shard_map/ppermute | solution.py:50
  46.7 13.6 %copy-start.2 = (bf16[3,128,256]{2,1,0:T(8,128)(2,1)}, bf16[3,128,256]{2,1,0:T(8,128)(2,1)S(1)}, u32[]{:S(2)}) copy-start(bf16[3,128,256]{2,1,0:T(8,128)(2,1)S(1)} %collective-permute-done.25.rest_1_) | copy-start | bytes 589828
  46.7 17.8 %collective-permute-start.26 = (bf16[3,128,256]{2,1,0:T(8,128)(2,1)}, bf16[3,128,256]{2,1,0:T(8,128)(2,1)}, u32[]{:S(2)}, u32[]{:S(2)}) collective-permute-start(bf16[3,128,256]{2,1,0:T(8,128)(2,1)} %get-tuple-element.99), channel_id=1, source_target_pairs={{0,4},{1,5},{2,6},{3,7},{4,0},{5,1},{6,2},{7,3},{8,12},{9,13},{10,... | collective-permute-start | bytes 589832 | tf_op jit(solution)/shard_map/ppermute | solution.py:46
  48.8 28.7 %collective-permute-start.19 = (bf16[3,128,768]{2,1,0:T(8,128)(2,1)}, bf16[3,128,768]{2,1,0:T(8,128)(2,1)}, u32[]{:S(2)}, u32[]{:S(2)}) collective-permute-start(bf16[3,128,768]{2,1,0:T(8,128)(2,1)} %collective-permute-done.15.rest_1_), channel_id=1, source_target_pairs={{0,1},{1,0},{2,3},{3,2},{4,5},{5,4},{6,7},{7,6},{8,9},{9,8},{10,11... | collective-permute-start | bytes 1769480 | tf_op jit(solution)/shard_map/ppermute | solution.py:50
  50.6 27.2 %collective-permute-start.20 = (bf16[3,128,768]{2,1,0:T(8,128)(2,1)}, bf16[3,128,768]{2,1,0:T(8,128)(2,1)}, u32[]{:S(2)}, u32[]{:S(2)}) collective-permute-start(bf16[3,128,768]{2,1,0:T(8,128)(2,1)} %collective-permute-done.16.rest_2_), channel_id=1, source_target_pairs={{0,1},{1,0},{2,3},{3,2},{4,5},{5,4},{6,7},{7,6},{8,9},{9,8},{10,11... | collective-permute-start | bytes 1769480 | tf_op jit(solution)/shard_map/ppermute | solution.py:50
  60.2 17.7 %collective-permute-start.21 = (bf16[3,128,768]{2,1,0:T(8,128)(2,1)}, bf16[3,128,768]{2,1,0:T(8,128)(2,1)}, u32[]{:S(2)}, u32[]{:S(2)}) collective-permute-start(bf16[3,128,768]{2,1,0:T(8,128)(2,1)} %collective-permute-done.17.rest_3_), channel_id=1, source_target_pairs={{0,1},{1,0},{2,3},{3,2},{4,5},{5,4},{6,7},{7,6},{8,9},{9,8},{10,11... | collective-permute-start | bytes 1769480 | tf_op jit(solution)/shard_map/ppermute | solution.py:50
  64.4 12.5 %collective-permute-start.27 = (bf16[3,128,256]{2,1,0:T(8,128)(2,1)}, bf16[3,128,256]{2,1,0:T(8,128)(2,1)}, u32[]{:S(2)}, u32[]{:S(2)}) collective-permute-start(bf16[3,128,256]{2,1,0:T(8,128)(2,1)} %get-tuple-element.100), channel_id=1, source_target_pairs={{0,6},{1,7},{2,4},{3,5},{4,2},{5,3},{6,0},{7,1},{8,14},{9,15},{10,... | collective-permute-start | bytes 589832 | tf_op jit(solution)/shard_map/ppermute | solution.py:46
  76.9 14.7 %collective-permute-start.28 = (bf16[3,128,256]{2,1,0:T(8,128)(2,1)}, bf16[3,128,256]{2,1,0:T(8,128)(2,1)}, u32[]{:S(2)}, u32[]{:S(2)}) collective-permute-start(bf16[3,128,256]{2,1,0:T(8,128)(2,1)} %get-tuple-element.97.rest_0_), channel_id=1, source_target_pairs={{0,1},{1,0},{2,3},{3,2},{4,5},{5,4},{6,7},{7,6},{8,9},{9,8},{10,11... | collective-permute-start | bytes 589832 | tf_op jit(solution)/shard_map/ppermute | solution.py:50
  77.2 14.4 %collective-permute-start.29 = (bf16[3,128,256]{2,1,0:T(8,128)(2,1)}, bf16[3,128,256]{2,1,0:T(8,128)(2,1)}, u32[]{:S(2)}, u32[]{:S(2)}) collective-permute-start(bf16[3,128,256]{2,1,0:T(8,128)(2,1)} %copy-done.2), channel_id=1, source_target_pairs={{0,1},{1,0},{2,3},{3,2},{4,5},{5,4},{6,7},{7,6},{8,9},{9,8},{10,11... | collective-permute-start | bytes 589832 | tf_op jit(solution)/shard_map/ppermute | solution.py:50
  77.5 15.5 %collective-permute-start.30 = (bf16[3,128,256]{2,1,0:T(8,128)(2,1)}, bf16[3,128,256]{2,1,0:T(8,128)(2,1)}, u32[]{:S(2)}, u32[]{:S(2)}) collective-permute-start(bf16[3,128,256]{2,1,0:T(8,128)(2,1)} %collective-permute-done.26.rest_2_), channel_id=1, source_target_pairs={{0,1},{1,0},{2,3},{3,2},{4,5},{5,4},{6,7},{7,6},{8,9},{9,8},{10,11... | collective-permute-start | bytes 589832 | tf_op jit(solution)/shard_map/ppermute | solution.py:50
  77.8 15.2 %collective-permute-start.31 = (bf16[3,128,256]{2,1,0:T(8,128)(2,1)}, bf16[3,128,256]{2,1,0:T(8,128)(2,1)}, u32[]{:S(2)}, u32[]{:S(2)}) collective-permute-start(bf16[3,128,256]{2,1,0:T(8,128)(2,1)} %collective-permute-done.27.rest_3_), channel_id=1, source_target_pairs={{0,1},{1,0},{2,3},{3,2},{4,5},{5,4},{6,7},{7,6},{8,9},{9,8},{10,11... | collective-permute-start | bytes 589832 | tf_op jit(solution)/shard_map/ppermute | solution.py:50
  87.9 12.1 %collective-permute-start.22 = (bf16[128,768]{1,0:T(8,128)(2,1)}, bf16[128,768]{1,0:T(8,128)(2,1)}, u32[]{:S(2)}, u32[]{:S(2)}) collective-permute-start(bf16[128,768]{1,0:T(8,128)(2,1)} %get-tuple-element.83), channel_id=1, source_target_pairs={{0,2},{1,3},{2,0},{3,1},{4,6},{5,7},{6,4},{7,5},{8,10},{9,11},{10,... | collective-permute-start | bytes 589832 | tf_op jit(solution)/shard_map/ppermute | solution.py:46
  91.6 10.3 %collective-permute-start.23 = (bf16[128,768]{1,0:T(8,128)(2,1)}, bf16[128,768]{1,0:T(8,128)(2,1)}, u32[]{:S(2)}, u32[]{:S(2)}) collective-permute-start(bf16[128,768]{1,0:T(8,128)(2,1)} %get-tuple-element.84), channel_id=1, source_target_pairs={{0,4},{1,5},{2,6},{3,7},{4,0},{5,1},{6,2},{7,3},{8,12},{9,13},{10,... | collective-permute-start | bytes 589832 | tf_op jit(solution)/shard_map/ppermute | solution.py:46
  91.7 21.7 %collective-permute-start.24 = (bf16[128,768]{1,0:T(8,128)(2,1)}, bf16[128,768]{1,0:T(8,128)(2,1)}, u32[]{:S(2)}, u32[]{:S(2)}) collective-permute-start(bf16[128,768]{1,0:T(8,128)(2,1)} %get-tuple-element.85), channel_id=1, source_target_pairs={{0,6},{1,7},{2,4},{3,5},{4,2},{5,3},{6,0},{7,1},{8,14},{9,15},{10,... | collective-permute-start | bytes 589832 | tf_op jit(solution)/shard_map/ppermute | solution.py:46
  97.6 19.2 %collective-permute-start.32 = (bf16[128,256]{1,0:T(8,128)(2,1)}, bf16[128,256]{1,0:T(8,128)(2,1)}, u32[]{:S(2)}, u32[]{:S(2)}) collective-permute-start(bf16[128,256]{1,0:T(8,128)(2,1)} %get-tuple-element.102), channel_id=1, source_target_pairs={{0,2},{1,3},{2,0},{3,1},{4,6},{5,7},{6,4},{7,5},{8,10},{9,11},{10,... | collective-permute-start | bytes 196616 | tf_op jit(solution)/shard_map/ppermute | solution.py:46
  100.0 16.9 %collective-permute-start.33 = (bf16[128,256]{1,0:T(8,128)(2,1)}, bf16[128,256]{1,0:T(8,128)(2,1)}, u32[]{:S(2)}, u32[]{:S(2)}) collective-permute-start(bf16[128,256]{1,0:T(8,128)(2,1)} %get-tuple-element.103), channel_id=1, source_target_pairs={{0,4},{1,5},{2,6},{3,7},{4,0},{5,1},{6,2},{7,3},{8,12},{9,13},{10,... | collective-permute-start | bytes 196616 | tf_op jit(solution)/shard_map/ppermute | solution.py:46
  100.0 16.9 %collective-permute-start.34 = (bf16[128,256]{1,0:T(8,128)(2,1)}, bf16[128,256]{1,0:T(8,128)(2,1)}, u32[]{:S(2)}, u32[]{:S(2)}) collective-permute-start(bf16[128,256]{1,0:T(8,128)(2,1)} %get-tuple-element.104), channel_id=1, source_target_pairs={{0,6},{1,7},{2,4},{3,5},{4,2},{5,3},{6,0},{7,1},{8,14},{9,15},{10,... | collective-permute-start | bytes 196616 | tf_op jit(solution)/shard_map/ppermute | solution.py:46
  118.9 4.2 %collective-permute-start.14 = (bf16[128,256]{1,0:T(8,128)(2,1)S(1)}, bf16[128,256]{1,0:T(8,128)(2,1)}, u32[]{:S(2)}, u32[]{:S(2)}) collective-permute-start(bf16[128,256]{1,0:T(8,128)(2,1)S(1)} %param.14), channel_id=1, source_target_pairs={{0,24},{8,16},{16,0},{24,8},{1,25},{9,17},{17,1},{25,9},{2,26},{10... | collective-permute-start | bytes 196616 | tf_op jit(solution)/shard_map/cond/branch_14_fun/ppermute | solution.py:555
  123.1 5.3 %collective-permute-start.35 = (bf16[128,256]{1,0:T(8,128)(2,1)}, bf16[128,256]{1,0:T(8,128)(2,1)S(1)}, u32[]{:S(2)}, u32[]{:S(2)}) collective-permute-start(bf16[128,256]{1,0:T(8,128)(2,1)} %get-tuple-element.110.mid_ref), channel_id=1, source_target_pairs={{0,1},{1,0},{2,3},{3,2},{4,5},{5,4},{6,7},{7,6},{8,9},{9,8},{10,11... | collective-permute-start | bytes 196616 | tf_op jit(solution)/shard_map/ppermute | solution.py:624
  126.4 5.8 %collective-permute-start.36 = (bf16[128,256]{1,0:T(8,128)(2,1)}, bf16[128,256]{1,0:T(8,128)(2,1)S(1)}, u32[]{:S(2)}, u32[]{:S(2)}) collective-permute-start(bf16[128,256]{1,0:T(8,128)(2,1)} %get-tuple-element.110.mid_ref), channel_id=1, source_target_pairs={{1,2},{3,4},{5,6},{2,1},{4,3},{6,5},{9,10},{11,12},{13,14},{10,9},... | collective-permute-start | bytes 196616 | tf_op jit(solution)/shard_map/ppermute | solution.py:626
  128.4 3.8 %copy-start = (bf16[128,256]{1,0:T(8,128)(2,1)}, bf16[128,256]{1,0:T(8,128)(2,1)S(1)}, u32[]{:S(2)}) copy-start(bf16[128,256]{1,0:T(8,128)(2,1)S(1)} %collective-permute-done.35.even_ref) | copy-start | bytes 196612
  132.2 0.6 copy-start.1

commit v4 on v3

--- a/solution.py
+++ b/solution.py
@@ -473,30 +473,16 @@
     cells = HH * WW
     rows, _ = mid_ref.shape
     me = lax.axis_index("ctx")
-    odd = lax.rem(me, 2)
-    before, after = rows - cells, rows + cells
-
-    def at(start):
-        return pl.ds(pl.multiple_of(start, cells), cells)
-
-    copies = (
-        pltpu.make_async_copy(mid_ref, held.at[pl.ds(cells, rows), :], sem.at[0]),
-        pltpu.make_async_copy(
-            even_ref.at[at(odd * before), :], held.at[at((1 - odd) * after), :], sem.at[1]
-        ),
-        pltpu.make_async_copy(
-            odd_ref.at[at((1 - odd) * before), :], held.at[at(odd * after), :], sem.at[2]
-        ),
-    )
-
-    for copy in copies:
-        copy.start()
-    for copy in copies:
-        copy.wait()
-    gather_taps(
-        [held[pl.ds(start, cells), :] for start in range(0, rows + 2 * cells, cells)], taps
-    )
-    total = held[pl.ds(cells, rows), :].astype(jnp.float32)
+    odd = lax.rem(me, 2) == 1
+    copy = pltpu.make_async_copy(mid_ref, held, sem)
+    copy.start()
+    last, first = pl.ds(rows - cells, cells), pl.ds(0, cells)
+    low = jnp.where(odd, even_ref[last, :], odd_ref[last, :])
+    high = jnp.where(odd, odd_ref[first, :], even_ref[first, :])
+    copy.wait()
+    frames = [held[pl.ds(start, cells), :] for start in range(0, rows, cells)]
+    gather_taps([low, *frames, high], taps)
+    total = held[...].astype(jnp.float32)
     for ahead in range(3):
         total = total + jnp.dot(
             taps[pl.ds(ahead * cells, rows), :], weight[ahead], preferred_element_type=jnp.float32
@@ -507,17 +493,17 @@
 
 def refine(frames, mid, even, odd, taps, limit):
     rows, channels = mid.shape
+    on_chip = [pltpu.with_memory_space_constraint(one, pltpu.VMEM) for one in (even, odd, taps)]
     return pl.pallas_call(
         refine_kernel,
         out_shape=jax.ShapeDtypeStruct((1, rows, channels), jnp.bfloat16),
-        in_specs=[pl.BlockSpec(memory_space=pltpu.SMEM)]
-        + [pl.BlockSpec(memory_space=pl.ANY)] * 3
-        + [pl.BlockSpec(memory_space=pltpu.VMEM)],
+        in_specs=[pl.BlockSpec(memory_space=pltpu.SMEM), pl.BlockSpec(memory_space=pl.ANY)]
+        + [pl.BlockSpec(memory_space=pltpu.VMEM)] * 3,
         out_specs=pl.BlockSpec(memory_space=pltpu.VMEM),
         scratch_shapes=[
-            pltpu.VMEM((rows + 2 * HH * WW, channels), jnp.bfloat16),
+            pltpu.VMEM((rows, channels), jnp.bfloat16),
             pltpu.VMEM((rows + 2 * HH * WW, 9 * channels), jnp.bfloat16),
-            pltpu.SemaphoreType.DMA((3,)),
+            pltpu.SemaphoreType.DMA,
         ],
         cost_estimate=pl.CostEstimate(
             flops=54 * rows * channels * channels,
@@ -526,7 +512,7 @@
         ),
         compiler_params=pltpu.CompilerParams(vmem_limit_bytes=limit),
         name="refine",
-    )(frames, mid, even, odd, pltpu.with_memory_space_constraint(taps, pltpu.VMEM))
+    )(frames, mid, *on_chip)
 
 
 def clip_orders(sec_count):
@@ -621,10 +607,10 @@
     limit = share(hidden_state.shape[1], channels, later)
     projected = project_late(own_frames, kept[:7], returned[1], model_width, limit)
     mid = handoff(projected, which, source, sec_count)
-    even = lax.ppermute(mid, "ctx", [(i, i ^ 1) for i in range(count)])
     joints = [(i, i + 1) for i in range(1, count - 1, 2)]
     odd = lax.ppermute(mid, "ctx", joints + [(two, one) for one, two in joints])
-    return refine(clip_length, mid, even, odd, kept[7], limit - 4 * SPARE_BYTES)
+    even = across(mid, chips)
+    return refine(clip_length, mid, even, odd, kept[7], limit // 2)
 
 
 def solution(mesh):

time: 136 us -> 136 us (level)
  the two profiles are of different devices: /device:TPU:15 before, /device:TPU:13 now
where the time goes in v4:
time: 136 us; the launch traced here: 135 us
  waiting for transfers between devices  59.9 us (44%)
  Pallas kernels  33.2 us (24%)
  starting transfers between devices  29.4 us (22%)
  between operations  4.79 us (4%)
  local copies, waits for them, and re-layouts  4.33 us (3%)
  other arithmetic  3.43 us (3%)
    ppermute x12, waiting for transfers between devices, send(): return lax.ppermute(value, 'ctx', pairs)  52.2 us
    ppermute x12, starting transfers between devices, send(): return lax.ppermute(value, 'ctx', pairs)  16.1 us
    pallas_call x2, Pallas kernels, attend(): pl.pallas_call(functools.partial(attend_kernel, chips, heads, block_rows)...  14.9 us
    ppermute x9, starting transfers between devices, across(): return lax.ppermute(value, 'ctx', [(i, i ^ 1) for i in range(2 * chips)])  11.1 us
    pallas_call x3, Pallas kernels, pack(): pl.pallas_call(functools.partial(pack_kernel, steps, chips, kinds, head_c...  6.42 us
    ppermute x1, waiting for transfers between devices, take(): return lambda value: lax.ppermute(value, 'sec', list(enumerate(order)))  3.89 us
    ppermute x1, waiting for transfers between devices, body(): odd = lax.ppermute(mid, 'ctx', joints + [(two, one) for one, two in joints])  3.78 us
    pallas_call x1, Pallas kernels, prepare(): pl.pallas_call(functools.partial(prepare_kernel, chips, head_cols, width)...  3.57 us
  transfers between devices with their start and end apart: 23, of which 5 were waited for; matrix products, arithmetic and copies ran while one was open for 6% of the time, Pallas kernels for 19%

profile of v4, /device:TPU:13, one launch (start us, length us, event | category | flops | bytes accessed | tf_op | source)
XLA Modules:
  0.0 135.2 jit_solution(9580231966111782654)
XLA Ops:
  0.0 2.4 %pack.3 = (bf16[3,128,768]{2,1,0:T(8,128)(2,1)}, bf16[3,128,768]{2,1,0:T(8,128)(2,1)}, bf16[3,128,768]{2,1,0:T(8,128)(2,1)}) custom-call(bf16[1,128,4096]{2,1,0:T(8,128)(2,1)} %rest_0_.5, bf16[1,128,4096]{2,1,0:T(8,128)(2,1)} %rest_1_.5, bf16[1,128,4096]{2,1,0:T(8,128)(2,1)} %rest_2_.5), custom_call_target="tpu_custom_call" | custom-call | bytes 3538944 | tf_op jit(solution)/shard_map/pack/pallas_call | solution.py:86
  2.7 2.3 %collective-permute-start.16 = (bf16[3,128,768]{2,1,0:T(8,128)(2,1)}, bf16[3,128,768]{2,1,0:T(8,128)(2,1)}, u32[]{:S(2)}, u32[]{:S(2)}) collective-permute-start(bf16[3,128,768]{2,1,0:T(8,128)(2,1)} %get-tuple-element.81), channel_id=1, source_target_pairs={{0,4},{1,5},{2,6},{3,7},{4,0},{5,1},{6,2},{7,3},{8,12},{9,13},{10,... | collective-permute-start | bytes 1769480 | tf_op jit(solution)/shard_map/ppermute | solution.py:46
  5.0 2.0 %pack.4 = bf16[3,128,768]{2,1,0:T(8,128)(2,1)} custom-call(bf16[1,128,4096]{2,1,0:T(8,128)(2,1)} %rest_0_.5, bf16[1,128,4096]{2,1,0:T(8,128)(2,1)} %rest_1_.5, bf16[1,128,4096]{2,1,0:T(8,128)(2,1)} %rest_2_.5), custom_call_target="tpu_custom_call" | custom-call | bytes 1179648 | tf_op jit(solution)/shard_map/pack/pallas_call | solution.py:86
  7.2 2.0 %pack.5 = (bf16[3,128,256]{2,1,0:T(8,128)(2,1)}, bf16[3,128,256]{2,1,0:T(8,128)(2,1)}, bf16[3,128,256]{2,1,0:T(8,128)(2,1)}, bf16[3,128,256]{2,1,0:T(8,128)(2,1)}) custom-call(bf16[1,128,4096]{2,1,0:T(8,128)(2,1)} %rest_0_.5, bf16[1,128,4096]{2,1,0:T(8,128)(2,1)} %rest_1_.5, bf16[1,128,4096]{2,1,0:T(8,128)(2,1)} %rest_2_.5), custom_call_target="tpu_custom_call" | custom-call | bytes 1572864 | tf_op jit(solution)/shard_map/pack/pallas_call | solution.py:86
  9.2 1.2 collective-permute-start.25
  10.5 1.7 %collective-permute-start.18 = (bf16[3,128,768]{2,1,0:T(8,128)(2,1)}, bf16[3,128,768]{2,1,0:T(8,128)(2,1)}, u32[]{:S(2)}, u32[]{:S(2)}) collective-permute-start(bf16[3,128,768]{2,1,0:T(8,128)(2,1)} %get-tuple-element.79.rest_0_), channel_id=1, source_target_pairs={{0,1},{1,0},{2,3},{3,2},{4,5},{5,4},{6,7},{7,6},{8,9},{9,8},{10,11... | collective-permute-start | bytes 1769480 | tf_op jit(solution)/shard_map/ppermute | solution.py:50
  12.2 1.2 dynamic_slice.15
  15.3 31.3 %collective-permute-done.25.rest_1_ = bf16[3,128,256]{2,1,0:T(8,128)(2,1)S(1)} collective-permute-done((bf16[3,128,256]{2,1,0:T(8,128)(2,1)}, bf16[3,128,256]{2,1,0:T(8,128)(2,1)S(1)}, u32[]{:S(2)}, u32[]{:S(2)}) %collective-permute-start.25) | collective-permute-done | bytes 196640 | tf_op jit(solution)/shard_map/ppermute | solution.py:46
  46.6 2.1 %collective-permute-start.26 = (bf16[3,128,256]{2,1,0:T(8,128)(2,1)}, bf16[3,128,256]{2,1,0:T(8,128)(2,1)}, u32[]{:S(2)}, u32[]{:S(2)}) collective-permute-start(bf16[3,128,256]{2,1,0:T(8,128)(2,1)} %get-tuple-element.99), channel_id=1, source_target_pairs={{0,4},{1,5},{2,6},{3,7},{4,0},{5,1},{6,2},{7,3},{8,12},{9,13},{10,... | collective-permute-start | bytes 589832 | tf_op jit(solution)/shard_map/ppermute | solution.py:46
  48.8 1.8 %collective-permute-start.19 = (bf16[3,128,768]{2,1,0:T(8,128)(2,1)}, bf16[3,128,768]{2,1,0:T(8,128)(2,1)}, u32[]{:S(2)}, u32[]{:S(2)}) collective-permute-start(bf16[3,128,768]{2,1,0:T(8,128)(2,1)} %collective-permute-done.15.rest_1_), channel_id=1, source_target_pairs={{0,1},{1,0},{2,3},{3,2},{4,5},{5,4},{6,7},{7,6},{8,9},{9,8},{10,11... | collective-permute-start | bytes 1769480 | tf_op jit(solution)/shard_map/ppermute | solution.py:50
  50.6 9.6 %collective-permute-done.17.rest_3_ = bf16[3,128,768]{2,1,0:T(8,128)(2,1)} collective-permute-done((bf16[3,128,768]{2,1,0:T(8,128)(2,1)}, bf16[3,128,768]{2,1,0:T(8,128)(2,1)}, u32[]{:S(2)}, u32[]{:S(2)}) %collective-permute-start.17) | collective-permute-done | bytes 589856 | tf_op jit(solution)/shard_map/ppermute | solution.py:46
  60.2 3.1 %collective-permute-start.21 = (bf16[3,128,768]{2,1,0:T(8,128)(2,1)}, bf16[3,128,768]{2,1,0:T(8,128)(2,1)}, u32[]{:S(2)}, u32[]{:S(2)}) collective-permute-start(bf16[3,128,768]{2,1,0:T(8,128)(2,1)} %collective-permute-done.17.rest_3_), channel_id=1, source_target_pairs={{0,1},{1,0},{2,3},{3,2},{4,5},{5,4},{6,7},{7,6},{8,9},{9,8},{10,11... | collective-permute-start | bytes 1769480 | tf_op jit(solution)/shard_map/ppermute | solution.py:50
  64.4 1.4 %collective-permute-start.27 = (bf16[3,128,256]{2,1,0:T(8,128)(2,1)}, bf16[3,128,256]{2,1,0:T(8,128)(2,1)}, u32[]{:S(2)}, u32[]{:S(2)}) collective-permute-start(bf16[3,128,256]{2,1,0:T(8,128)(2,1)} %get-tuple-element.100), channel_id=1, source_target_pairs={{0,6},{1,7},{2,4},{3,5},{4,2},{5,3},{6,0},{7,1},{8,14},{9,15},{10,... | collective-permute-start | bytes 589832 | tf_op jit(solution)/shard_map/ppermute | solution.py:46
  65.8 1.4 %multiply_reduce_fusion = (s32[]{:T(128)}, s32[]{:T(128)}) fusion(s32[4]{0:T(128)} %param.35, s32[4]{0:T(128)} %constant.21.clone, s32[]{:T(128)S(6)} %axis_index.15), kind=kLoop, calls=%fused_computation.5 | loop fusion | flops 18 | bytes 44 | tf_op jit(solution)/shard_map/reduce_sum | solution.py:534
  69.9 1.4 %fusion.2 = (s32[1]{0:T(128)}, s32[1]{0:T(128)}) fusion(s32[4]{0:T(128)} %param.34, s32[]{:T(128)S(6)} %select_n.21, s32[]{:T(128)S(6)} %select_n.19), kind=kLoop, calls=%fused_computation.7 | loop fusion | bytes 24 | tf_op jit(solution)/shard_map/dynamic_slice | solution.py:592
  71.3 3.6 %prepare.1 = (bf16[128,1024]{1,0:T(8,128)(2,1)}, f32[3,1024]{1,0:T(4,128)}, bf16[1024,256]{1,0:T(8,128)(2,1)}, f32[2,8,256]{2,1,0:T(8,128)}) custom-call(bf16[1,128,4096]{2,1,0:T(8,128)(2,1)} %h_ref.3, f32[3,4096]{1,0:T(4,128)} %bitcast.6, bf16[4096,256]{1,0:T(8,128)(2,1)} %weight_ref.3), custom_call_target="tpu_custom_call" | custom-call | flops 67108864 | bytes 4194304 | tf_op jit(solution)/shard_map/prepare/pallas_call | solution.py:278
  74.9 2.0 %fusion.1 = s32[]{:T(128)} fusion(s32[15]{0:T(128)} %constant.20.clone, s32[]{:T(128)} %get-tuple-element.106), kind=kLoop, calls=%fused_computation.4 | loop fusion | flops 44 | bytes 68 | tf_op jit(solution)/shard_map/reduce_sum | solution.py:535
  77.9 10.1 %attend.2 = (bf16[128,768]{1,0:T(8,128)(2,1)}, bf16[128,768]{1,0:T(8,128)(2,1)}, bf16[128,768]{1,0:T(8,128)(2,1)}, bf16[128,768]{1,0:T(8,128)(2,1)}) custom-call(s32[1]{0:T(128)} %get-tuple-element.77.frames_ref, bf16[3,128,768]{2,1,0:T(8,128)(2,1)} %get-tuple-element.79.rest_0_, bf16[3,128,768]{2,1,0:T(8,128)(2,1)} %collective-permute-done.15.rest_1_, ...), custom_call_target="tpu_custom_call" | custom-call | flops 2415919104 | bytes 6291456 | tf_op jit(solution)/shard_map/attend/pallas_call | solution.py:192
  88.0 3.7 %collective-permute-start.22 = (bf16[128,768]{1,0:T(8,128)(2,1)}, bf16[128,768]{1,0:T(8,128)(2,1)}, u32[]{:S(2)}, u32[]{:S(2)}) collective-permute-start(bf16[128,768]{1,0:T(8,128)(2,1)} %get-tuple-element.83), channel_id=1, source_target_pairs={{0,2},{1,3},{2,0},{3,1},{4,6},{5,7},{6,4},{7,5},{8,10},{9,11},{10,... | collective-permute-start | bytes 589832 | tf_op jit(solution)/shard_map/ppermute | solution.py:46
  91.7 1.3 collective-permute-start.24
  93.0 4.8 %attend.3 = (bf16[128,256]{1,0:T(8,128)(2,1)}, bf16[128,256]{1,0:T(8,128)(2,1)}, bf16[128,256]{1,0:T(8,128)(2,1)}, bf16[128,256]{1,0:T(8,128)(2,1)}) custom-call(s32[1]{0:T(128)} %get-tuple-element.77.frames_ref, bf16[3,128,256]{2,1,0:T(8,128)(2,1)} %get-tuple-element.97.rest_0_, bf16[3,128,256]{2,1,0:T(8,128)(2,1)} %copy-done, ...), custom_call_target="tpu_custom_call" | custom-call | flops 805306368 | bytes 2097152 | tf_op jit(solution)/shard_map/attend/pallas_call | solution.py:192
  97.8 2.3 %collective-permute-start.32 = (bf16[128,256]{1,0:T(8,128)(2,1)}, bf16[128,256]{1,0:T(8,128)(2,1)}, u32[]{:S(2)}, u32[]{:S(2)}) collective-permute-start(bf16[128,256]{1,0:T(8,128)(2,1)} %get-tuple-element.102), channel_id=1, source_target_pairs={{0,2},{1,3},{2,0},{3,1},{4,6},{5,7},{6,4},{7,5},{8,10},{9,11},{10,... | collective-permute-start | bytes 196616 | tf_op jit(solution)/shard_map/ppermute | solution.py:46
  100.2 1.3 collective-permute-start.34
  102.1 11.3 %collective-permute-done.24.rest_3_ = bf16[128,768]{1,0:T(8,128)(2,1)} collective-permute-done((bf16[128,768]{1,0:T(8,128)(2,1)}, bf16[128,768]{1,0:T(8,128)(2,1)}, u32[]{:S(2)}, u32[]{:S(2)}) %collective-permute-start.24) | collective-permute-done | bytes 196640 | tf_op jit(solution)/shard_map/ppermute | solution.py:46
  113.4 3.5 %project_early.1 = (f32[128,256]{1,0:T(8,128)S(1)}, f32[128,128]{1,0:T(8,128)S(1)}, f32[128,128]{1,0:T(8,128)S(1)}, bf16[128,1024]{1,0:T(8,128)(2,1)S(1)}, f32[3...) custom-call(bf16[1,128,4096]{2,1,0:T(8,128)(2,1)} %h_ref.3, ...), custom_call_target="tpu_custom_call" | custom-call | flops 201326592 | bytes 4194304 | tf_op jit(solution)/shard_map/project_early/pallas_call | solution.py:365
  117.0 2.1 %project_late.1 = bf16[128,256]{1,0:T(8,128)(2,1)S(1)} custom-call(s32[1]{0:T(128)} %get-tuple-element.77.frames_ref, f32[128,256]{1,0:T(8,128)S(1)} %get-tuple-element.90.rest_0_, f32[128,128]{1,0:T(8,128)S(1)} %get-tuple-element.91.rest_1_, f32[128,128]{1,0:T(8,128)S(1)} %get-tuple-element.92.rest_2_, bf16[128,1024]{1,0:T(8,128)(2,1)S(1)} %get-tuple-element.93.rest_3_, ...), custom_call_target="tpu_custom_call" | custom-call | flops 67108864 | bytes 524288 | tf_op jit(solution)/shard_map/project_late/pallas_call | solution.py:432
  119.1 4.2 %conditional.1 = (bf16[128,256]{1,0:T(8,128)(2,1)}) conditional(s32[]{:T(128)} %clamp.3, bf16[128,256]{1,0:T(8,128)(2,1)S(1)} %project_late.1, bf16[128,256]{1,0:T(8,128)(2,1)S(1)} %project_late.1, bf16[128,256]{1,0:T(8,128)(2,1)S(1)} %project_late.1, bf16[128,256]{1,0:T(8,128)(2,1)S(1)} %project_late.1, ...), branch_computations={%region_3.4_spmd, %region_4.5_spmd, %region_5.6_spmd, %region_6.7_... | conditional | bytes 262192 | solution.py:543
  119.4 3.9 %collective-permute-done.14 = bf16[128,256]{1,0:T(8,128)(2,1)} collective-permute-done((bf16[128,256]{1,0:T(8,128)(2,1)S(1)}, bf16[128,256]{1,0:T(8,128)(2,1)}, u32[]{:S(2)}, u32[]{:S(2)}) %collective-permute-start.14) | collective-permute-done | bytes 65568 | tf_op jit(solution)/shard_map/cond/branch_14_fun/ppermute | solution.py:541
  123.3 3.4 %collective-permute-start.35 = (bf16[128,256]{1,0:T(8,128)(2,1)}, bf16[128,256]{1,0:T(8,128)(2,1)S(1)}, u32[]{:S(2)}, u32[]{:S(2)}) collective-permute-start(bf16[128,256]{1,0:T(8,128)(2,1)} %get-tuple-element.110.mid_ref), channel_id=1, source_target_pairs={{0,1},{1,0},{2,3},{3,2},{4,5},{5,4},{6,7},{7,6},{8,9},{9,8},{10,11... | collective-permute-start | bytes 196616 | tf_op jit(solution)/shard_map/ppermute | solution.py:50
  126.6 2.0 %collective-permute-start.36 = (bf16[128,256]{1,0:T(8,128)(2,1)}, bf16[128,256]{1,0:T(8,128)(2,1)S(1)}, u32[]{:S(2)}, u32[]{:S(2)}) collective-permute-start(bf16[128,256]{1,0:T(8,128)(2,1)} %get-tuple-element.110.mid_ref), channel_id=1, source_target_pairs={{1,2},{3,4},{5,6},{2,1},{4,3},{6,5},{9,10},{11,12},{13,14},{10,9},... | collective-permute-start | bytes 196616 | tf_op jit(solution)/shard_map/ppermute | solution.py:611
  128.6 3.8 %collective-permute-done.36.odd_ref = bf16[128,256]{1,0:T(8,128)(2,1)S(1)} collective-permute-done((bf16[128,256]{1,0:T(8,128)(2,1)}, bf16[128,256]{1,0:T(8,128)(2,1)S(1)}, u32[]{:S(2)}, u32[]{:S(2)}) %collective-permute-start.36) | collective-permute-done | bytes 65568 | tf_op jit(solution)/shard_map/ppermute | solution.py:611
  132.4 2.8 %refine.1 = bf16[1,128,256]{2,1,0:T(8,128)(2,1)} custom-call(s32[1]{0:T(128)} %get-tuple-element.75.frames_ref, bf16[128,256]{1,0:T(8,128)(2,1)} %get-tuple-element.110.mid_ref, bf16[128,256]{1,0:T(8,128)(2,1)S(1)} %collective-permute-done.35.even_ref, bf16[128,256]{1,0:T(8,128)(2,1)S(1)} %collective-permute-done.36.odd_ref, ...), custom_call_target="tpu_custom_call" | custom-call | flops 452984832 | bytes 3735552 | tf_op jit(solution)/shard_map/refine/pallas_call | solution.py:497
  (32 shorter events, 3.6 us)
Async XLA Ops:
  2.5 46.3 %collective-permute-start.15 = (bf16[3,128,768]{2,1,0:T(8,128)(2,1)}, bf16[3,128,768]{2,1,0:T(8,128)(2,1)}, u32[]{:S(2)}, u32[]{:S(2)}) collective-permute-start(bf16[3,128,768]{2,1,0:T(8,128)(2,1)} %get-tuple-element.80), channel_id=1, source_target_pairs={{0,2},{1,3},{2,0},{3,1},{4,6},{5,7},{6,4},{7,5},{8,10},{9,11},{10,... | collective-permute-start | bytes 1769480 | tf_op jit(solution)/shard_map/ppermute | solution.py:46
  2.7 47.9 %collective-permute-start.16 = (bf16[3,128,768]{2,1,0:T(8,128)(2,1)}, bf16[3,128,768]{2,1,0:T(8,128)(2,1)}, u32[]{:S(2)}, u32[]{:S(2)}) collective-permute-start(bf16[3,128,768]{2,1,0:T(8,128)(2,1)} %get-tuple-element.81), channel_id=1, source_target_pairs={{0,4},{1,5},{2,6},{3,7},{4,0},{5,1},{6,2},{7,3},{8,12},{9,13},{10,... | collective-permute-start | bytes 1769480 | tf_op jit(solution)/shard_map/ppermute | solution.py:46
  7.0 53.2 %collective-permute-start.17 = (bf16[3,128,768]{2,1,0:T(8,128)(2,1)}, bf16[3,128,768]{2,1,0:T(8,128)(2,1)}, u32[]{:S(2)}, u32[]{:S(2)}) collective-permute-start(bf16[3,128,768]{2,1,0:T(8,128)(2,1)} %pack.4), channel_id=1, source_target_pairs={{0,6},{1,7},{2,4},{3,5},{4,2},{5,3},{6,0},{7,1},{8,14},{9,15},{10,... | collective-permute-start | bytes 1769480 | tf_op jit(solution)/shard_map/ppermute | solution.py:46
  9.2 37.4 %collective-permute-start.25 = (bf16[3,128,256]{2,1,0:T(8,128)(2,1)}, bf16[3,128,256]{2,1,0:T(8,128)(2,1)S(1)}, u32[]{:S(2)}, u32[]{:S(2)}) collective-permute-start(bf16[3,128,256]{2,1,0:T(8,128)(2,1)} %get-tuple-element.98), channel_id=1, source_target_pairs={{0,2},{1,3},{2,0},{3,1},{4,6},{5,7},{6,4},{7,5},{8,10},{9,11},{10,... | collective-permute-start | bytes 589832 | tf_op jit(solution)/shard_map/ppermute | solution.py:46
  10.5 66.7 %collective-permute-start.18 = (bf16[3,128,768]{2,1,0:T(8,128)(2,1)}, bf16[3,128,768]{2,1,0:T(8,128)(2,1)}, u32[]{:S(2)}, u32[]{:S(2)}) collective-permute-start(bf16[3,128,768]{2,1,0:T(8,128)(2,1)} %get-tuple-element.79.rest_0_), channel_id=1, source_target_pairs={{0,1},{1,0},{2,3},{3,2},{4,5},{5,4},{6,7},{7,6},{8,9},{9,8},{10,11... | collective-permute-start | bytes 1769480 | tf_op jit(solution)/shard_map/ppermute | solution.py:50
  46.6 13.6 %copy-start = (bf16[3,128,256]{2,1,0:T(8,128)(2,1)}, bf16[3,128,256]{2,1,0:T(8,128)(2,1)S(1)}, u32[]{:S(2)}) copy-start(bf16[3,128,256]{2,1,0:T(8,128)(2,1)S(1)} %collective-permute-done.25.rest_1_) | copy-start | bytes 589828
  46.6 17.8 %collective-permute-start.26 = (bf16[3,128,256]{2,1,0:T(8,128)(2,1)}, bf16[3,128,256]{2,1,0:T(8,128)(2,1)}, u32[]{:S(2)}, u32[]{:S(2)}) collective-permute-start(bf16[3,128,256]{2,1,0:T(8,128)(2,1)} %get-tuple-element.99), channel_id=1, source_target_pairs={{0,4},{1,5},{2,6},{3,7},{4,0},{5,1},{6,2},{7,3},{8,12},{9,13},{10,... | collective-permute-start | bytes 589832 | tf_op jit(solution)/shard_map/ppermute | solution.py:46
  48.8 28.6 %collective-permute-start.19 = (bf16[3,128,768]{2,1,0:T(8,128)(2,1)}, bf16[3,128,768]{2,1,0:T(8,128)(2,1)}, u32[]{:S(2)}, u32[]{:S(2)}) collective-permute-start(bf16[3,128,768]{2,1,0:T(8,128)(2,1)} %collective-permute-done.15.rest_1_), channel_id=1, source_target_pairs={{0,1},{1,0},{2,3},{3,2},{4,5},{5,4},{6,7},{7,6},{8,9},{9,8},{10,11... | collective-permute-start | bytes 1769480 | tf_op jit(solution)/shard_map/ppermute | solution.py:50
  50.6 27.1 %collective-permute-start.20 = (bf16[3,128,768]{2,1,0:T(8,128)(2,1)}, bf16[3,128,768]{2,1,0:T(8,128)(2,1)}, u32[]{:S(2)}, u32[]{:S(2)}) collective-permute-start(bf16[3,128,768]{2,1,0:T(8,128)(2,1)} %collective-permute-done.16.rest_2_), channel_id=1, source_target_pairs={{0,1},{1,0},{2,3},{3,2},{4,5},{5,4},{6,7},{7,6},{8,9},{9,8},{10,11... | collective-permute-start | bytes 1769480 | tf_op jit(solution)/shard_map/ppermute | solution.py:50
  60.2 17.7 %collective-permute-start.21 = (bf16[3,128,768]{2,1,0:T(8,128)(2,1)}, bf16[3,128,768]{2,1,0:T(8,128)(2,1)}, u32[]{:S(2)}, u32[]{:S(2)}) collective-permute-start(bf16[3,128,768]{2,1,0:T(8,128)(2,1)} %collective-permute-done.17.rest_3_), channel_id=1, source_target_pairs={{0,1},{1,0},{2,3},{3,2},{4,5},{5,4},{6,7},{7,6},{8,9},{9,8},{10,11... | collective-permute-start | bytes 1769480 | tf_op jit(solution)/shard_map/ppermute | solution.py:50
  64.4 12.5 %collective-permute-start.27 = (bf16[3,128,256]{2,1,0:T(8,128)(2,1)}, bf16[3,128,256]{2,1,0:T(8,128)(2,1)}, u32[]{:S(2)}, u32[]{:S(2)}) collective-permute-start(bf16[3,128,256]{2,1,0:T(8,128)(2,1)} %get-tuple-element.100), channel_id=1, source_target_pairs={{0,6},{1,7},{2,4},{3,5},{4,2},{5,3},{6,0},{7,1},{8,14},{9,15},{10,... | collective-permute-start | bytes 589832 | tf_op jit(solution)/shard_map/ppermute | solution.py:46
  76.9 14.8 %collective-permute-start.28 = (bf16[3,128,256]{2,1,0:T(8,128)(2,1)}, bf16[3,128,256]{2,1,0:T(8,128)(2,1)}, u32[]{:S(2)}, u32[]{:S(2)}) collective-permute-start(bf16[3,128,256]{2,1,0:T(8,128)(2,1)} %get-tuple-element.97.rest_0_), channel_id=1, source_target_pairs={{0,1},{1,0},{2,3},{3,2},{4,5},{5,4},{6,7},{7,6},{8,9},{9,8},{10,11... | collective-permute-start | bytes 589832 | tf_op jit(solution)/shard_map/ppermute | solution.py:50
  77.2 14.6 %collective-permute-start.29 = (bf16[3,128,256]{2,1,0:T(8,128)(2,1)}, bf16[3,128,256]{2,1,0:T(8,128)(2,1)}, u32[]{:S(2)}, u32[]{:S(2)}) collective-permute-start(bf16[3,128,256]{2,1,0:T(8,128)(2,1)} %copy-done), channel_id=1, source_target_pairs={{0,1},{1,0},{2,3},{3,2},{4,5},{5,4},{6,7},{7,6},{8,9},{9,8},{10,11... | collective-permute-start | bytes 589832 | tf_op jit(solution)/shard_map/ppermute | solution.py:50
  77.4 15.6 %collective-permute-start.30 = (bf16[3,128,256]{2,1,0:T(8,128)(2,1)}, bf16[3,128,256]{2,1,0:T(8,128)(2,1)}, u32[]{:S(2)}, u32[]{:S(2)}) collective-permute-start(bf16[3,128,256]{2,1,0:T(8,128)(2,1)} %collective-permute-done.26.rest_2_), channel_id=1, source_target_pairs={{0,1},{1,0},{2,3},{3,2},{4,5},{5,4},{6,7},{7,6},{8,9},{9,8},{10,11... | collective-permute-start | bytes 589832 | tf_op jit(solution)/shard_map/ppermute | solution.py:50
  77.7 15.3 %collective-permute-start.31 = (bf16[3,128,256]{2,1,0:T(8,128)(2,1)}, bf16[3,128,256]{2,1,0:T(8,128)(2,1)}, u32[]{:S(2)}, u32[]{:S(2)}) collective-permute-start(bf16[3,128,256]{2,1,0:T(8,128)(2,1)} %collective-permute-done.27.rest_3_), channel_id=1, source_target_pairs={{0,1},{1,0},{2,3},{3,2},{4,5},{5,4},{6,7},{7,6},{8,9},{9,8},{10,11... | collective-permute-start | bytes 589832 | tf_op jit(solution)/shard_map/ppermute | solution.py:50
  88.0 12.2 %collective-permute-start.22 = (bf16[128,768]{1,0:T(8,128)(2,1)}, bf16[128,768]{1,0:T(8,128)(2,1)}, u32[]{:S(2)}, u32[]{:S(2)}) collective-permute-start(bf16[128,768]{1,0:T(8,128)(2,1)} %get-tuple-element.83), channel_id=1, source_target_pairs={{0,2},{1,3},{2,0},{3,1},{4,6},{5,7},{6,4},{7,5},{8,10},{9,11},{10,... | collective-permute-start | bytes 589832 | tf_op jit(solution)/shard_map/ppermute | solution.py:46
  91.7 10.3 %collective-permute-start.23 = (bf16[128,768]{1,0:T(8,128)(2,1)}, bf16[128,768]{1,0:T(8,128)(2,1)}, u32[]{:S(2)}, u32[]{:S(2)}) collective-permute-start(bf16[128,768]{1,0:T(8,128)(2,1)} %get-tuple-element.84), channel_id=1, source_target_pairs={{0,4},{1,5},{2,6},{3,7},{4,0},{5,1},{6,2},{7,3},{8,12},{9,13},{10,... | collective-permute-start | bytes 589832 | tf_op jit(solution)/shard_map/ppermute | solution.py:46
  91.7 21.7 %collective-permute-start.24 = (bf16[128,768]{1,0:T(8,128)(2,1)}, bf16[128,768]{1,0:T(8,128)(2,1)}, u32[]{:S(2)}, u32[]{:S(2)}) collective-permute-start(bf16[128,768]{1,0:T(8,128)(2,1)} %get-tuple-element.85), channel_id=1, source_target_pairs={{0,6},{1,7},{2,4},{3,5},{4,2},{5,3},{6,0},{7,1},{8,14},{9,15},{10,... | collective-permute-start | bytes 589832 | tf_op jit(solution)/shard_map/ppermute | solution.py:46
  97.8 19.1 %collective-permute-start.32 = (bf16[128,256]{1,0:T(8,128)(2,1)}, bf16[128,256]{1,0:T(8,128)(2,1)}, u32[]{:S(2)}, u32[]{:S(2)}) collective-permute-start(bf16[128,256]{1,0:T(8,128)(2,1)} %get-tuple-element.102), channel_id=1, source_target_pairs={{0,2},{1,3},{2,0},{3,1},{4,6},{5,7},{6,4},{7,5},{8,10},{9,11},{10,... | collective-permute-start | bytes 196616 | tf_op jit(solution)/shard_map/ppermute | solution.py:46
  100.2 16.8 %collective-permute-start.33 = (bf16[128,256]{1,0:T(8,128)(2,1)}, bf16[128,256]{1,0:T(8,128)(2,1)}, u32[]{:S(2)}, u32[]{:S(2)}) collective-permute-start(bf16[128,256]{1,0:T(8,128)(2,1)} %get-tuple-element.103), channel_id=1, source_target_pairs={{0,4},{1,5},{2,6},{3,7},{4,0},{5,1},{6,2},{7,3},{8,12},{9,13},{10,... | collective-permute-start | bytes 196616 | tf_op jit(solution)/shard_map/ppermute | solution.py:46
  100.2 16.8 %collective-permute-start.34 = (bf16[128,256]{1,0:T(8,128)(2,1)}, bf16[128,256]{1,0:T(8,128)(2,1)}, u32[]{:S(2)}, u32[]{:S(2)}) collective-permute-start(bf16[128,256]{1,0:T(8,128)(2,1)} %get-tuple-element.104), channel_id=1, source_target_pairs={{0,6},{1,7},{2,4},{3,5},{4,2},{5,3},{6,0},{7,1},{8,14},{9,15},{10,... | collective-permute-start | bytes 196616 | tf_op jit(solution)/shard_map/ppermute | solution.py:46
  119.1 4.2 %collective-permute-start.14 = (bf16[128,256]{1,0:T(8,128)(2,1)S(1)}, bf16[128,256]{1,0:T(8,128)(2,1)}, u32[]{:S(2)}, u32[]{:S(2)}) collective-permute-start(bf16[128,256]{1,0:T(8,128)(2,1)S(1)} %param.14), channel_id=1, source_target_pairs={{0,24},{8,16},{16,0},{24,8},{1,25},{9,17},{17,1},{25,9},{2,26},{10... | collective-permute-start | bytes 196616 | tf_op jit(solution)/shard_map/cond/branch_14_fun/ppermute | solution.py:541
  123.3 5.3 %collective-permute-start.35 = (bf16[128,256]{1,0:T(8,128)(2,1)}, bf16[128,256]{1,0:T(8,128)(2,1)S(1)}, u32[]{:S(2)}, u32[]{:S(2)}) collective-permute-start(bf16[128,256]{1,0:T(8,128)(2,1)} %get-tuple-element.110.mid_ref), channel_id=1, source_target_pairs={{0,1},{1,0},{2,3},{3,2},{4,5},{5,4},{6,7},{7,6},{8,9},{9,8},{10,11... | collective-permute-start | bytes 196616 | tf_op jit(solution)/shard_map/ppermute | solution.py:50
  126.6 5.8 %collective-permute-start.36 = (bf16[128,256]{1,0:T(8,128)(2,1)}, bf16[128,256]{1,0:T(8,128)(2,1)S(1)}, u32[]{:S(2)}, u32[]{:S(2)}) collective-permute-start(bf16[128,256]{1,0:T(8,128)(2,1)} %get-tuple-element.110.mid_ref), channel_id=1, source_target_pairs={{1,2},{3,4},{5,6},{2,1},{4,3},{6,5},{9,10},{11,12},{13,14},{10,9},... | collective-permute-start | bytes 196616 | tf_op jit(solution)/shard_map/ppermute | solution.py:611
